TPU v7x, 32 devices: a whole 2x2x4 slice. The times are simulated.
32 devices in a mesh: groups: 2 (over x), row: 16 (over z, y, core).
Axes of the slice: x: 2, y: 2, z: 4, core: 2. Of those that a mesh axis runs over, the one named last changes fastest.
Arguments:
- bound_coeff: bfloat16 [4, 64, 8192], P('groups', 'row'), parts along dimension 0, may hold values from -0.044 to 0.044
- status: int32 [4, 8192], P('groups'), parts along dimension 0, may hold values from 0 to 2
- slope_bit: int32 [4, 8192], P('groups'), parts along dimension 0, may hold values from 0 to 1
- pre_lower: float32 [4, 8192], P('groups'), parts along dimension 0, may hold values from -2 to -0.1
- pre_upper: float32 [4, 8192], P('groups'), parts along dimension 0, may hold values from 0.1 to 2
- weight: bfloat16 [16384, 8192], P('groups', 'row'), parts along dimension 0, may hold values from -0.0625 to 0.0625
- layer_bias: float32 [16384], P('groups'), parts along dimension 0, may hold values from -6 to 6
- center_input: float32 [4, 8192], P('groups', 'row'), parts along dimension 0, may hold values from -6 to 6
- radius: float32 [4, 8192], P('groups', 'row'), parts along dimension 0, may hold values from 0.05 to 1
Outputs:
- lower_bound: float32 [4, 64], P('groups', 'row'), parts along dimension 0
- upper_bound: float32 [4, 64], P('groups', 'row'), parts along dimension 0
There are 2 independent parts, one for each index of `groups`. A program takes and returns all parts, laid end to end along the dimension named above; each array names one. Nothing has to cross between parts.
All inputs are finite; a program needn't handle non-finite values.
Results may differ from a plain program's by a relative error of at most 0.0003.
Values may be sent and summed in bfloat16 or wider, within the bound.
No kernel may reach another device: no remote copies, remote signals or barrier semaphores. Data moves between devices by JAX's collectives and lax.ppermute only.
A program may use at most 64 MiB of HBM per device.

v0:
```python
import jax
import jax.numpy as jnp
from jax import lax
from jax.sharding import PartitionSpec as P


def relax_coeff(bound_coeff, status, slope_bit, pre_lower, pre_upper):
    values = bound_coeff.astype(jnp.float32)
    upper_slope = (pre_upper / (pre_upper - pre_lower))[:, None, :]
    chosen = slope_bit.astype(jnp.float32)[:, None, :]
    unstable = (status == 2)[:, None, :]
    active = (status == 1)[:, None, :]
    positive = values >= 0.0
    slope_low = jnp.where(
        active, 1.0, jnp.where(unstable, jnp.where(positive, chosen, upper_slope), 0.0)
    )
    slope_up = jnp.where(
        active, 1.0, jnp.where(unstable, jnp.where(positive, upper_slope, chosen), 0.0)
    )
    return ((values * slope_low).astype(jnp.bfloat16), (values * slope_up).astype(jnp.bfloat16))


def intercepts(bound_coeff, status, pre_lower, pre_upper):
    values = bound_coeff.astype(jnp.float32)
    upper_slope = pre_upper / (pre_upper - pre_lower)
    offset = (-upper_slope * pre_lower)[:, None, :]
    unstable = (status == 2)[:, None, :]
    positive = values >= 0.0
    below_term = jnp.sum(
        jnp.where(unstable & jnp.logical_not(positive), values * offset, 0.0), axis=-1
    )
    above_term = jnp.sum(jnp.where(unstable & positive, values * offset, 0.0), axis=-1)
    return (below_term, above_term)


def on_device(
    bound_coeff, status, slope_bit, pre_lower, pre_upper, weight, layer_bias, center_input, radius
):
    examples = bound_coeff.shape[0]
    num_neurons = bound_coeff.shape[2]
    local_cols = weight.shape[1]
    sign_pair = jnp.array([-1.0, 1.0], dtype=jnp.float32)
    part_center = jnp.einsum(
        "jd,ed->ej", weight.astype(jnp.float32), center_input, precision=lax.Precision.HIGHEST
    )
    center = lax.psum(part_center, "row") + layer_bias[None, :]
    relaxed_low, relaxed_up = relax_coeff(bound_coeff, status, slope_bit, pre_lower, pre_upper)
    below_term, above_term = intercepts(bound_coeff, status, pre_lower, pre_upper)
    stacked = lax.all_gather(jnp.stack([relaxed_low, relaxed_up]), "row", axis=2, tiled=True)
    num_rows = stacked.shape[2]
    flat_rows = stacked.reshape(2 * examples * num_rows, num_neurons)
    mapped = jnp.dot(flat_rows, weight, preferred_element_type=jnp.float32).reshape(
        2, examples, num_rows, local_cols
    )
    result = sign_pair[:, None, None] * jnp.einsum(
        "lerd,ed->ler", jnp.abs(mapped), radius, precision=lax.Precision.HIGHEST
    )
    summed = lax.psum_scatter(result, "row", scatter_dimension=2, tiled=True)
    near_low = jnp.einsum(
        "erj,ej->er", relaxed_low.astype(jnp.float32), center, precision=lax.Precision.HIGHEST
    )
    near_up = jnp.einsum(
        "erj,ej->er", relaxed_up.astype(jnp.float32), center, precision=lax.Precision.HIGHEST
    )
    lower_bound = near_low + below_term + summed[0]
    upper_bound = near_up + above_term + summed[1]
    return (lower_bound, upper_bound)


def solution(mesh):
    in_specs = (
        P("groups", "row", None),
        P("groups", None),
        P("groups", None),
        P("groups", None),
        P("groups", None),
        P("groups", "row"),
        P("groups"),
        P("groups", "row"),
        P("groups", "row"),
    )
    out_specs = (P("groups", "row"), P("groups", "row"))
    return jax.shard_map(
        on_device, mesh=mesh, in_specs=in_specs, out_specs=out_specs, check_vma=False
    )
```

profile of v0, /device:TPU:0, one launch (start us, length us, event | category | flops | bytes accessed | tf_op | source)
XLA Modules:
  0.0 207.5 jit_solution(9305162727291835596)
XLA Ops:
  7.2 0.0 copy-start
  7.2 0.0 copy-start.9
  7.2 0.0 copy-start.2
  7.2 0.0 copy-start.3
  7.2 0.0 copy-start.5
  7.2 0.0 copy-start.4
  7.2 0.0 copy-start.1
  7.2 0.0 copy-start.6
  7.3 0.0 all-reduce.3.cloned.1.call-start
  7.3 0.6 copy-done
  7.9 9.5 %fusion.24 = f32[2,8192]{1,0:T(2,128)} fusion(f32[2,512]{1,0:T(2,128)S(1)} %copy-done, bf16[8192,512]{1,0:T(8,128)(2,1)} %param.15), kind=kOutput, calls=%fused_computation.37 | convolution fusion | flops 100663296 | bytes 8458240 | tf_op jit(solution)/shard_map/jd,ed->ej/dot_general | solution.py:43
  17.4 0.0 all-reduce.3.cloned.1.call-update
  17.4 0.0 all-gather.2.cloned.1.call-start
  17.5 0.0 copy-done.2
  17.5 0.0 copy-done.3
  17.5 0.1 broadcast_compare_fusion.1
  17.6 0.0 copy-done.5
  17.6 0.0 copy-done.4
  17.6 0.1 negate_multiply_fusion
  17.7 0.0 copy-done.1
  17.7 1.1 fusion.12
  18.8 1.0 pad_maximum_fusion
  19.8 0.0 all-gather.2.cloned.1.call-update
  19.8 0.0 copy-done.9
  19.8 0.6 dynamic-slice
  21.1 83.7 %all-reduce.3.cloned.1.call-done = f32[2,8192]{1,0:T(2,128)} async-done(((f32[2,8192]{1,0:T(2,128)}), f32[2,8192]{1,0:T(2,128)}) %all-reduce.3.cloned.1.call-update) | async-done | bytes 65552 | tf_op jit(solution)/shard_map/psum | solution.py:46
  104.7 0.0 copy-done.6
  104.7 0.9 add_bitcast_fusion
  105.6 0.7 fusion.16
  106.3 0.1 copy.23
  106.4 0.7 fusion.14
  107.2 0.1 copy.29
  107.3 0.0 copy-start.7
  107.3 0.0 copy-start.8
  107.3 52.0 %all-gather.2.cloned.1.call-done = bf16[2,2,64,8192]{3,1,0,2:T(2,128)(2,1)} async-done(((bf16[2,2,4,8192]{3,1,0,2:T(2,128)(2,1)}), bf16[2,2,64,8192]{3,1,0,2:T(2,128)(2,1)}) %all-gather.2.cloned.1.call-update) | async-done | bytes 4194320 | tf_op jit(solution)/shard_map/all_gather | solution.py:49
  159.3 7.8 %fusion.3 = f32[2,2,64,512]{3,2,1,0:T(8,128)S(1)} fusion(bf16[8192,512]{1,0:T(8,128)(2,1)} %param.15, bf16[2,2,64,8192]{3,1,0,2:T(2,128)(2,1)} %all-gather.2.cloned.1.call-done), kind=kOutput, calls=%fused_computation.3 | convolution fusion | flops 2147614720 | bytes 13107200 | tf_op jit(solution)/shard_map/dot_general | solution.py:52
  167.1 0.0 copy-done.7
  167.1 0.7 fusion.8
  167.8 0.0 copy-done.8
  167.8 0.1 fusion.22
  167.9 31.1 %all-reduce = f32[2,2,64]{2,1,0:T(2,128)S(1)} all-reduce(f32[2,2,64]{2,1,0:T(2,128)S(1)} %fusion.22), channel_id=2, replica_groups=mesh['groups'=2,'row'=16] {'row'}, use_global_device_ids=true, to_apply=%region_2.3.clone | all-reduce | flops 256 | bytes 2048
  199.1 0.1 dynamic-slice_bitcast_fusion
  199.1 0.1 copy.18
  199.2 0.1 copy.17
  199.3 0.7 copy.20
  200.0 0.6 copy.19
  (2 shorter events, 0.0 us)
Async XLA Ops:
  7.2 0.7 copy-start
  7.2 12.7 %copy-start.9 = (u32[32]{0:T(128)S(1)}, u32[32]{0:T(128)}, u32[]{:S(2)}) copy-start(u32[32]{0:T(128)} %constant.15) | copy-start | bytes 388
  7.2 10.3 %copy-start.2 = (s32[2,8192]{1,0:T(2,128)S(1)}, s32[2,8192]{1,0:T(2,128)}, u32[]{:S(2)}) copy-start(s32[2,8192]{1,0:T(2,128)} %param.12) | copy-start | bytes 196612
  7.2 10.3 %copy-start.3 = (s32[2,8192]{1,0:T(2,128)S(1)}, s32[2,8192]{1,0:T(2,128)}, u32[]{:S(2)}) copy-start(s32[2,8192]{1,0:T(2,128)} %param.11) | copy-start | bytes 196612
  7.2 10.4 %copy-start.5 = (f32[2,8192]{1,0:T(2,128)S(1)}, f32[2,8192]{1,0:T(2,128)}, u32[]{:S(2)}) copy-start(f32[2,8192]{1,0:T(2,128)} %param.14) | copy-start | bytes 196612
  7.2 10.4 %copy-start.4 = (f32[2,8192]{1,0:T(2,128)S(1)}, f32[2,8192]{1,0:T(2,128)}, u32[]{:S(2)}) copy-start(f32[2,8192]{1,0:T(2,128)} %param.13) | copy-start | bytes 196612
  7.2 10.5 %copy-start.1 = (bf16[2,4,8192]{2,1,0:T(4,128)(2,1)S(1)}, bf16[2,4,8192]{2,1,0:T(4,128)(2,1)}, u32[]{:S(2)}) copy-start(bf16[2,4,8192]{2,1,0:T(4,128)(2,1)} %param.10) | copy-start | bytes 393220
  7.2 97.5 %copy-start.6 = (f32[8192]{0:T(1024)S(1)}, f32[8192]{0:T(1024)}, u32[]{:S(2)}) copy-start(f32[8192]{0:T(1024)} %param.16) | copy-start | bytes 98308
  7.3 97.5 %all-reduce.3.cloned.1.call-start = ((), (), s32[]{:S(2)}) async-start(), calls=%async_computation | async-start | bytes 131072 | tf_op jit(solution)/shard_map/psum | solution.py:46
  17.4 141.9 %all-gather.2.cloned.1.call-start = ((), (), s32[]{:S(2)}) async-start(), calls=%async_computation.1 | async-start | bytes 4456448 | tf_op jit(solution)/shard_map/all_gather | solution.py:49
  107.3 59.8 %copy-start.7 = (f32[2,512]{1,0:T(2,128)S(1)}, f32[2,512]{1,0:T(2,128)}, u32[]{:S(2)}) copy-start(f32[2,512]{1,0:T(2,128)} %param.18) | copy-start | bytes 12292
  107.3 60.5 %copy-start.8 = (f32[2]{0:T(128)S(1)}, f32[2]{0:T(128)}, u32[]{:S(2)}) copy-start(f32[2]{0:T(128)} %constant.4.clone) | copy-start | bytes 28
Sparse Core Ops, SparseCore 0:
  17.5 87.1 all-reduce.2
  107.1 52.1 all-gather.1
where the time goes:
time: 208 us; the launch traced here: 207 us
  waiting for transfers between devices  136 us (65%)
  blocking collectives  31.1 us (15%)
  matrix products  19.5 us (9%)
  between operations  14.9 us (7%)
  other arithmetic  3.24 us (2%)
  local copies, waits for them, and re-layouts  2.94 us (1%)
    psum x1, waiting for transfers between devices, on_device(): center = lax.psum(part_center, 'row') + layer_bias[None, :]  83.7 us
    all_gather x1, waiting for transfers between devices, on_device(): lax.all_gather(jnp.stack([relaxed_low, relaxed_up]), 'row', axis=2, tiled...  52 us
    unnamed x1, blocking collectives  31.1 us
    dot_general x1, matrix products, on_device(): jnp.einsum('jd,ed->ej', weight.astype(jnp.float32), center_input, precisi...  9.53 us
    dot_general x1, matrix products, on_device(): jnp.dot(flat_rows, weight, preferred_element_type=jnp.float32)  7.77 us
  transfers between devices with their start and end apart: 2, of which 2 were waited for; matrix products, arithmetic and copies ran while one was open for 3% of the time, Pallas kernels for 0%

commit v1 on v0

v1 whole, which is shorter than its diff:
```python
import jax
import jax.numpy as jnp
from jax import lax
from jax.sharding import PartitionSpec as P


def slopes(status, slope_bit, pre_lower, pre_upper):
    upper_slope = pre_upper / (pre_upper - pre_lower)
    chosen = slope_bit.astype(jnp.float32)
    unstable = status == 2
    active = status == 1
    inner = jnp.where(active, 1.0, jnp.where(unstable, chosen, 0.0))
    outer = jnp.where(active, 1.0, jnp.where(unstable, upper_slope, 0.0))
    offset = jnp.where(unstable, -upper_slope * pre_lower, 0.0)
    return inner, outer, offset


def relax(values, inner, outer):
    positive = values >= 0.0
    low = values * jnp.where(positive, inner, outer)
    up = values * jnp.where(positive, outer, inner)
    return low.astype(jnp.bfloat16), up.astype(jnp.bfloat16)


def on_device(
    bound_coeff, status, slope_bit, pre_lower, pre_upper, weight, layer_bias, center_input, radius
):
    examples = bound_coeff.shape[0]
    num_neurons = bound_coeff.shape[2]
    local_cols = weight.shape[1]
    inner, outer, offset = slopes(status, slope_bit, pre_lower, pre_upper)
    inner, outer, offset = inner[:, None, :], outer[:, None, :], offset[:, None, :]

    values = bound_coeff.astype(jnp.float32)
    own_low, own_up = relax(values, inner, outer)
    term = values * offset
    bias = layer_bias[None, None, :]
    own_lower = jnp.sum(jnp.where(values < 0.0, term, 0.0) + own_low.astype(jnp.float32) * bias, axis=-1)
    own_upper = jnp.sum(jnp.where(values >= 0.0, term, 0.0) + own_up.astype(jnp.float32) * bias, axis=-1)

    gathered = lax.all_gather(bound_coeff, "row", axis=0, tiled=False)
    num_devices = gathered.shape[0]
    low, up = relax(gathered.astype(jnp.float32), inner, outer)
    stacked = jnp.stack([low, up], axis=1)
    mapped = jnp.dot(
        stacked.reshape(-1, num_neurons), weight, preferred_element_type=jnp.float32
    ).reshape(num_devices, 2, examples, -1, local_cols)
    sign = jnp.array([-1.0, 1.0], dtype=jnp.float32)[None, :, None, None, None]
    cell = mapped * center_input[None, None, :, None, :] + sign * jnp.abs(mapped) * radius[None, None, :, None, :]
    part = jnp.sum(cell, axis=-1)
    mine = jnp.sum(lax.all_to_all(part, "row", 0, 0, tiled=True), axis=0)
    return (own_lower + mine[0], own_upper + mine[1])


def solution(mesh):
    in_specs = (
        P("groups", "row", None),
        P("groups", None),
        P("groups", None),
        P("groups", None),
        P("groups", None),
        P("groups", "row"),
        P("groups"),
        P("groups", "row"),
        P("groups", "row"),
    )
    out_specs = (P("groups", "row"), P("groups", "row"))
    return jax.shard_map(
        on_device, mesh=mesh, in_specs=in_specs, out_specs=out_specs, check_vma=False
    )
```

time: 208 us -> 83.5 us (0.40)
  waiting for transfers between devices: 136 us -> 51.3 us
  blocking collectives: 31.1 us -> 0 us
  matrix products: 19.5 us -> 5.85 us
  other arithmetic: 3.24 us -> 7.63 us
  starting transfers between devices: 0.08 us -> 3.52 us
  local copies, waits for them, and re-layouts: 2.94 us -> 0.74 us
    psum x1 -> x0, waiting for transfers between devices: 83.7 us -> none  [on_device(): center = lax.psum(part_center, 'row') + layer_bias[None, :]]
    unnamed x1 -> x0, blocking collectives: 31.1 us -> none
    dot_general x5 -> x1, matrix products: 19.5 us -> 5.85 us  [on_device(): jnp.dot(stacked.reshape(-1, num_neurons), weight, preferred_element_type=...]
    all_gather x1, waiting for transfers between devices: 52 us -> 44.4 us  [on_device(): gathered = lax.all_gather(bound_coeff, 'row', axis=0, tiled=False)]
    all_to_all x0 -> x1, waiting for transfers between devices: none -> 6.18 us  [on_device(): mine = jnp.sum(lax.all_to_all(part, 'row', 0, 0, tiled=True), axis=0)]
    all_to_all x0 -> x1, starting transfers between devices: none -> 3.48 us  [on_device(): mine = jnp.sum(lax.all_to_all(part, 'row', 0, 0, tiled=True), axis=0)]
    unnamed x23 -> x10, local copies, waits for them, and re-layouts: 2.49 us -> 0.03 us
where the time goes in v1:
time: 83.5 us; the launch traced here: 83.2 us
  waiting for transfers between devices  51.3 us (61%)
  between operations  14.1 us (17%)
  other arithmetic  7.63 us (9%)
  matrix products  5.85 us (7%)
  starting transfers between devices  3.52 us (4%)
    all_gather x1, waiting for transfers between devices, on_device(): gathered = lax.all_gather(bound_coeff, 'row', axis=0, tiled=False)  44.4 us
    all_to_all x1, waiting for transfers between devices, on_device(): mine = jnp.sum(lax.all_to_all(part, 'row', 0, 0, tiled=True), axis=0)  6.18 us
    dot_general x1, matrix products, on_device(): jnp.dot(stacked.reshape(-1, num_neurons), weight, preferred_element_type=...  5.85 us
    all_to_all x1, starting transfers between devices, on_device(): mine = jnp.sum(lax.all_to_all(part, 'row', 0, 0, tiled=True), axis=0)  3.48 us
    another operation x1, other arithmetic, on_device(): stacked = jnp.stack([low, up], axis=1)  2.59 us
    convert_element_type x1, other arithmetic, on_device(): low, up = relax(gathered.astype(jnp.float32), inner, outer)  2.06 us
  transfers between devices with their start and end apart: 2, of which 2 were waited for; matrix products, arithmetic and copies ran while one was open for 3% of the time, Pallas kernels for 0%

profile of v1, /device:TPU:0, one launch (start us, length us, event | category | flops | bytes accessed | tf_op | source)
XLA Modules:
  0.0 83.2 jit_solution(11027747687834911454)
XLA Ops:
  7.2 0.0 all-gather.3.cloned.1.call-start
  7.2 0.7 all-gather.3.cloned.1.call-update
  7.9 1.0 %multiply_select_fusion = (f32[2,8192]{1,0:T(2,128)S(1)}, f32[2,8192]{1,0:T(2,128)S(1)}) fusion(f32[2,8192]{1,0:T(2,128)} %param.13, s32[2,8192]{1,0:T(2,128)} %param.11, f32[2,8192]{1,0:T(2,128)} %param.14), kind=kLoop, calls=%fused_computation.27 | loop fusion | flops 98304 | bytes 327680 | tf_op jit(solution)/shard_map/jit(_where)/select_n | solution.py:14
  8.9 1.0 %select_select_fusion.1 = (f32[2,8192]{1,0:T(2,128)S(1)}, f32[2,8192]{1,0:T(2,128)S(1)}) fusion(s32[2,8192]{1,0:T(2,128)} %param.12, s32[2,8192]{1,0:T(2,128)} %param.11, f32[2,8192]{1,0:T(2,128)S(1)} %get-tuple-element.5), kind=kLoop, calls=%fused_computation.26 | loop fusion | flops 114688 | bytes 327680 | tf_op jit(solution)/shard_map/jit(_where)/select_n | solution.py:12
  9.9 44.4 %all-gather.3.cloned.1.call-done = bf16[32,4,8192]{2,1,0:T(4,128)(2,1)} async-done(((bf16[2,4,8192]{2,1,0:T(4,128)(2,1)}), bf16[32,4,8192]{2,1,0:T(4,128)(2,1)}) %all-gather.3.cloned.1.call-update) | async-done | bytes 2097168 | tf_op jit(solution)/shard_map/all_gather | solution.py:41
  54.3 2.1 %convert = f32[16,2,4,8192]{3,2,1,0:T(4,128)S(1)} convert(bf16[16,2,4,8192]{3,2,1,0:T(4,128)(2,1)} %bitcast.21) | non-fusion elementwise | flops 1048576 | bytes 6291456 | tf_op jit(solution)/shard_map/convert_element_type | solution.py:43
  56.4 0.0 copy-start.2
  56.4 0.0 copy-start.3
  56.4 0.0 copy-start.4
  56.4 2.6 %fusion.5 = (bf16[16,1,2,4,8192]{4,0,3,2,1:T(8,128)(2,1)S(1)}, bf16[16,1,2,4,8192]{4,0,3,2,1:T(8,128)(2,1)S(1)}) fusion(f32[16,2,4,8192]{3,2,1,0:T(4,128)S(1)} %convert, f32[2,8192]{1,0:T(2,128)S(1)} %get-tuple-element.9, f32[2,8192]{1,0:T(2,128)S(1)} %get-tuple-element.8), kind=kLoop, calls=%fused_computation.8 | loop fusion | flops 7340032 | bytes 8519680 | tf_op jit(solution)/shard_map/stack | solution.py:44
  59.0 0.0 copy-done.2
  59.0 0.0 copy-done.3
  59.0 0.0 copy-done.4
  59.0 0.0 copy-start
  59.0 0.0 copy-start.1
  59.0 5.9 %add_reduce_fusion = f32[16,2,2,4]{0,3,2,1:T(4,128)S(1)} fusion(bf16[8192,512]{1,0:T(8,128)(2,1)} %param.15, bf16[16,1,2,4,8192]{4,0,3,2,1:T(8,128)(2,1)S(1)} %get-tuple-element.7, bf16[16,1,2,4,8192]{4,0,3,2,1:T(8,128)(2,1)S(1)} %get-tuple-element.6, f32[2,512]{1,0:T(2,128)S(1)} %copy-done.2, f32[2]{0:T(128)S(1)} %copy-done.4, f32[2,512]{1,0:T(2,128)S(1)} %copy-done.3), kind=kOutput, calls=%fused_computation.10 | convolution fusion | flops 2150366976 | bytes 12592136 | tf_op jit(solution)/shard_map/dot_general | solution.py:45
  64.9 0.7 copy.21
  65.6 3.5 %all-to-all-start = ((f32[16,2,2,4]{3,2,1,0:T(2,128)}), f32[16,2,2,4]{3,2,1,0:T(2,128)S(1)}, u32[]{:S(2)}, u32[]{:S(2)}) async-start(f32[16,2,2,4]{3,2,1,0:T(2,128)} %copy.21), calls=%async_computation | async-start | bytes 65536 | tf_op jit(solution)/shard_map/all_to_all | solution.py:51
  69.1 0.0 copy-done
  69.1 0.0 copy-done.1
  69.1 0.4 fusion.16
  69.5 6.2 %all-to-all-done = f32[16,2,2,4]{3,2,1,0:T(2,128)S(1)} async-done(((f32[16,2,2,4]{3,2,1,0:T(2,128)}), f32[16,2,2,4]{3,2,1,0:T(2,128)S(1)}, u32[]{:S(2)}, u32[]{:S(2)}) %all-to-all-start) | async-done | bytes 1056 | tf_op jit(solution)/shard_map/all_to_all | solution.py:51
  75.8 0.6 fusion.19
  (1 shorter events, 0.0 us)
Async XLA Ops:
  7.2 47.1 %all-gather.3.cloned.1.call-start = ((), (), s32[]{:S(2)}) async-start(), calls=%async_computation.1 | async-start | bytes 2228224 | tf_op jit(solution)/shard_map/all_gather | solution.py:41
  56.4 2.6 %copy-start.2 = (f32[2,512]{1,0:T(2,128)S(1)}, f32[2,512]{1,0:T(2,128)}, u32[]{:S(2)}) copy-start(f32[2,512]{1,0:T(2,128)} %param.18) | copy-start | bytes 12292
  56.4 2.6 %copy-start.3 = (f32[2,512]{1,0:T(2,128)S(1)}, f32[2,512]{1,0:T(2,128)}, u32[]{:S(2)}) copy-start(f32[2,512]{1,0:T(2,128)} %param.17) | copy-start | bytes 12292
  56.4 2.6 %copy-start.4 = (f32[2]{0:T(128)S(1)}, f32[2]{0:T(128)}, u32[]{:S(2)}) copy-start(f32[2]{0:T(128)} %constant.3.clone) | copy-start | bytes 28
  59.0 10.1 %copy-start = (bf16[2,4,8192]{2,1,0:T(4,128)(2,1)S(1)}, bf16[2,4,8192]{2,1,0:T(4,128)(2,1)}, u32[]{:S(2)}) copy-start(bf16[2,4,8192]{2,1,0:T(4,128)(2,1)} %param.10) | copy-start | bytes 393220
  59.0 10.1 %copy-start.1 = (f32[8192]{0:T(1024)S(1)}, f32[8192]{0:T(1024)}, u32[]{:S(2)}) copy-start(f32[8192]{0:T(1024)} %param.16) | copy-start | bytes 98308
  65.6 10.1 %all-to-all-start = ((f32[16,2,2,4]{3,2,1,0:T(2,128)}), f32[16,2,2,4]{3,2,1,0:T(2,128)S(1)}, u32[]{:S(2)}, u32[]{:S(2)}) async-start(f32[16,2,2,4]{3,2,1,0:T(2,128)} %copy.21), calls=%async_computation | async-start | bytes 65536 | tf_op jit(solution)/shard_map/all_to_all | solution.py:51
Sparse Core Ops, SparseCore 0:
  10.2 44.0 all-gather.2

commit v2 on v1

v2 whole, which is shorter than its diff:
```python
import functools

import jax
import jax.numpy as jnp
from jax import lax
from jax.experimental import pallas as pl
from jax.experimental.pallas import tpu as pltpu
from jax.sharding import PartitionSpec as P

F32 = jnp.float32
BF16 = jnp.bfloat16
LANES = 128
VMEM = pl.BlockSpec(memory_space=pltpu.VMEM)


def lane_sums(cells):
    rows, columns = cells.shape
    width = min(columns, LANES)
    folded = cells[:, 0:width]
    for start in range(width, columns, width):
        folded = folded + cells[:, start : start + width]
    return jnp.sum(folded.T, axis=0, keepdims=True)


def prep_kernel(coeff, status, bit, lower, upper, bias, inner_out, outer_out, own_out):
    examples, specs, neurons = coeff.shape
    low, high = lower[...], upper[...]
    slope = high / (high - low)
    unstable = status[...] == 2
    active = status[...] == 1
    inner = jnp.where(active, 1.0, jnp.where(unstable, bit[...].astype(F32), 0.0))
    outer = jnp.where(active, 1.0, jnp.where(unstable, slope, 0.0))
    offset = jnp.where(unstable, -slope * low, 0.0)
    biases = bias[...]
    below, above = [], []
    for e in range(examples):
        inner_rows = jnp.broadcast_to(inner[e : e + 1], (specs, neurons))
        outer_rows = jnp.broadcast_to(outer[e : e + 1], (specs, neurons))
        inner_out[e * specs : (e + 1) * specs, :] = inner_rows
        outer_out[e * specs : (e + 1) * specs, :] = outer_rows
        values = coeff[e].astype(F32)
        positive = values >= 0.0
        relaxed_low = (values * jnp.where(positive, inner_rows, outer_rows)).astype(BF16).astype(F32)
        relaxed_up = (values * jnp.where(positive, outer_rows, inner_rows)).astype(BF16).astype(F32)
        term = values * offset[e : e + 1]
        below.append(jnp.where(positive, 0.0, term) + relaxed_low * biases)
        above.append(jnp.where(positive, term, 0.0) + relaxed_up * biases)
    cells = jnp.concatenate(below + above, axis=0)
    rows = cells.shape[0]
    folded = cells[:, 0:LANES]
    for start in range(LANES, neurons, LANES):
        folded = folded + cells[:, start : start + LANES]
    if rows < LANES:
        folded = jnp.concatenate([folded, jnp.zeros((LANES - rows, LANES), F32)], axis=0)
    own_out[...] = jnp.sum(folded.T, axis=0, keepdims=True)[:, 0:rows]


def prep(coeff, status, bit, lower, upper, bias):
    examples, specs, neurons = coeff.shape
    rows = examples * specs
    return pl.pallas_call(
        prep_kernel,
        in_specs=[VMEM] * 6,
        out_specs=(VMEM, VMEM, VMEM),
        out_shape=(
            jax.ShapeDtypeStruct((rows, neurons), F32),
            jax.ShapeDtypeStruct((rows, neurons), F32),
            jax.ShapeDtypeStruct((1, 2 * rows), F32),
        ),
        compiler_params=pltpu.CompilerParams(vmem_limit_bytes=16 << 20),
        name="prep",
    )(coeff, status, bit, lower, upper, bias)


def map_kernel(num_pieces, *refs):
    pieces = refs[:num_pieces]
    inner, outer, weight, center, radius, out, relaxed = refs[num_pieces:]
    examples, specs, neurons = pieces[0].shape
    rows = examples * specs
    columns = weight.shape[1]
    step = min(neurons, 2048)
    for start in range(0, neurons, step):
        span = slice(start, start + step)
        inner_rows, outer_rows = inner[:, span], outer[:, span]
        for index, piece in enumerate(pieces):
            values = jnp.concatenate([piece[e, :, span].astype(F32) for e in range(examples)], axis=0)
            positive = values >= 0.0
            low = (values * jnp.where(positive, inner_rows, outer_rows)).astype(BF16)
            up = (values * jnp.where(positive, outer_rows, inner_rows)).astype(BF16)
            at = index * 2 * rows
            relaxed[at : at + 2 * rows, span] = jnp.concatenate([low, up], axis=0)
    mapped = jnp.dot(relaxed[...], weight[...], preferred_element_type=F32)
    centers, radii = center[...], radius[...]

    def per_row(values_low, values_up):
        halves = []
        for values in (values_low, values_up):
            for e in range(examples):
                halves.append(jnp.broadcast_to(values[e : e + 1], (specs, columns)))
        block = jnp.concatenate(halves, axis=0)[None]
        return jnp.broadcast_to(block, (num_pieces, 2 * rows, columns)).reshape(num_pieces * 2 * rows, columns)

    cells = mapped * per_row(centers, centers) + jnp.abs(mapped) * per_row(-radii, radii)
    out[...] = lane_sums(cells)


def map_rows(pieces, inner, outer, weight, center, radius):
    examples, specs, neurons = pieces[0].shape
    rows = 2 * examples * specs * len(pieces)
    columns = weight.shape[1]
    return pl.pallas_call(
        functools.partial(map_kernel, len(pieces)),
        in_specs=[VMEM] * (len(pieces) + 5),
        out_specs=VMEM,
        out_shape=jax.ShapeDtypeStruct((1, rows), F32),
        scratch_shapes=[pltpu.VMEM((rows, neurons), BF16)],
        compiler_params=pltpu.CompilerParams(vmem_limit_bytes=32 << 20),
        cost_estimate=pl.CostEstimate(
            flops=2 * rows * neurons * columns, bytes_accessed=2 * rows * neurons, transcendentals=0
        ),
        name="map_rows",
    )(*pieces, inner, outer, weight, center, radius)


def fold_kernel(kept, came, keep_out, send_out):
    total = kept[...] + came[...]
    half = total.shape[1] // 2
    keep_out[...] = total[:, 0:half]
    send_out[...] = total[:, half:]


def fold(kept, came):
    half = kept.shape[1] // 2
    return pl.pallas_call(
        fold_kernel,
        in_specs=[VMEM] * 2,
        out_specs=(VMEM, VMEM),
        out_shape=(jax.ShapeDtypeStruct((1, half), F32),) * 2,
        name="fold",
    )(kept, came)


def finish_kernel(kept, came, own, lower_out, upper_out):
    total = kept[...] + came[...] + own[...]
    examples, specs = lower_out.shape
    for e in range(examples):
        lower_out[e : e + 1, :] = total[:, e * specs : (e + 1) * specs]
        at = (examples + e) * specs
        upper_out[e : e + 1, :] = total[:, at : at + specs]


def finish(kept, came, own, examples, specs):
    return pl.pallas_call(
        finish_kernel,
        in_specs=[VMEM] * 3,
        out_specs=(VMEM, VMEM),
        out_shape=(jax.ShapeDtypeStruct((examples, specs), F32),) * 2,
        name="finish",
    )(kept, came, own)


def on_device(
    num_devices, bound_coeff, status, slope_bit, pre_lower, pre_upper, weight, layer_bias, center_input, radius
):
    examples, specs, neurons = bound_coeff.shape

    def swap(array, mask):
        return lax.ppermute(array, "row", [(i, i ^ mask) for i in range(num_devices)])

    inner, outer, own = prep(bound_coeff, status, slope_bit, pre_lower, pre_upper, layer_bias.reshape(1, neurons))

    pieces = {0: bound_coeff}
    for mask in range(4, num_devices, 4):
        pieces[mask] = swap(bound_coeff, mask)
    for mask in range(0, num_devices, 4):
        pieces[mask + 2] = swap(pieces[mask], 2)
    for mask in range(0, num_devices, 2):
        pieces[mask + 1] = swap(pieces[mask], 1)

    args = (inner, outer, weight, center_input, radius)
    bits = num_devices.bit_length() - 1
    order = [int(format(i, "b").zfill(bits)[::-1], 2) for i in range(num_devices)]
    half = num_devices // 2
    keep = map_rows([pieces[m] for m in order[:half]], *args)
    send = map_rows([pieces[m] for m in order[half:]], *args)
    for bit in range(bits):
        came = swap(send, 1 << bit)
        if bit < bits - 1:
            keep, send = fold(keep, came)
    return finish(keep, came, own, examples, specs)


def solution(mesh):
    in_specs = (
        P("groups", "row", None),
        P("groups", None),
        P("groups", None),
        P("groups", None),
        P("groups", None),
        P("groups", "row"),
        P("groups"),
        P("groups", "row"),
        P("groups", "row"),
    )
    out_specs = (P("groups", "row"), P("groups", "row"))
    return jax.shard_map(
        functools.partial(on_device, mesh.shape["row"]),
        mesh=mesh,
        in_specs=in_specs,
        out_specs=out_specs,
        check_vma=False,
    )
```

time: 83.5 us -> 59.3 us (0.71)
  waiting for transfers between devices: 51.3 us -> 15.7 us
  starting transfers between devices: 3.52 us -> 19.3 us
  local copies, waits for them, and re-layouts: 0.74 us -> 14.3 us
  between operations: 14.1 us -> 0.74 us
  Pallas kernels: 0 us -> 8.58 us
  other arithmetic: 7.63 us -> 0 us
  matrix products: 5.85 us -> 0 us
    all_gather x1 -> x0, waiting for transfers between devices: 44.4 us -> none  [on_device(): gathered = lax.all_gather(bound_coeff, 'row', axis=0, tiled=False)]
    ppermute x0 -> x19, starting transfers between devices: none -> 19.3 us  [swap(): lax.ppermute(array, 'row', [(i, i ^ mask) for i in range(num_devices)])]
    ppermute x0 -> x19, waiting for transfers between devices: none -> 15.7 us  [swap(): lax.ppermute(array, 'row', [(i, i ^ mask) for i in range(num_devices)])]
    unnamed x10 -> x34, local copies, waits for them, and re-layouts: 0.03 us -> 14.3 us
    pallas_call x0 -> x7, Pallas kernels: none -> 8.58 us  [the longest x3 3.83 us: fold(): pl.pallas_call(fold_kernel, in_specs=[VMEM] * 2, out_specs=(VMEM, VMEM),...]
    all_to_all x1 -> x0, waiting for transfers between devices: 6.18 us -> none  [on_device(): mine = jnp.sum(lax.all_to_all(part, 'row', 0, 0, tiled=True), axis=0)]
    dot_general x1 -> x0, matrix products: 5.85 us -> none  [on_device(): jnp.dot(stacked.reshape(-1, num_neurons), weight, preferred_element_type=...]
    all_to_all x1 -> x0, starting transfers between devices: 3.48 us -> none  [on_device(): mine = jnp.sum(lax.all_to_all(part, 'row', 0, 0, tiled=True), axis=0)]
  transfers between devices with their start and end apart: 2 -> 19, of which waited for: 2 -> 8; matrix products, arithmetic and copies ran while one was open for 3% -> 0% of each run, Pallas kernels for 0% -> 4%
where the time goes in v2:
time: 59.3 us; the launch traced here: 58.7 us
  starting transfers between devices  19.3 us (33%)
  waiting for transfers between devices  15.7 us (26%)
  local copies, waits for them, and re-layouts  14.3 us (24%)
  Pallas kernels  8.58 us (14%)
  between operations  0.74 us (1%)
    ppermute x19, starting transfers between devices, swap(): lax.ppermute(array, 'row', [(i, i ^ mask) for i in range(num_devices)])  19.3 us
    ppermute x19, waiting for transfers between devices, swap(): lax.ppermute(array, 'row', [(i, i ^ mask) for i in range(num_devices)])  15.7 us
    unnamed x34, local copies, waits for them, and re-layouts  14.3 us
    pallas_call x3, Pallas kernels, fold(): pl.pallas_call(fold_kernel, in_specs=[VMEM] * 2, out_specs=(VMEM, VMEM),...  3.83 us
    pallas_call x2, Pallas kernels, map_rows(): pl.pallas_call(functools.partial(map_kernel, len(pieces)), in_specs=[VMEM...  2.75 us
    pallas_call x1, Pallas kernels, finish(): pl.pallas_call(finish_kernel, in_specs=[VMEM] * 3, out_specs=(VMEM, VMEM)...  1.3 us
  transfers between devices with their start and end apart: 19, of which 8 were waited for; matrix products, arithmetic and copies ran while one was open for 0% of the time, Pallas kernels for 4%

profile of v2, /device:TPU:0, one launch (start us, length us, event | category | flops | bytes accessed | tf_op | source)
XLA Modules:
  0.0 58.7 jit_solution(9881214828031431833)
XLA Ops:
  0.6 4.1 %collective-permute-start = (bf16[2,4,8192]{2,1,0:T(4,128)(2,1)}, bf16[2,4,8192]{2,1,0:T(4,128)(2,1)S(1)}, u32[]{:S(2)}, u32[]{:S(2)}) collective-permute-start(bf16[2,4,8192]{2,1,0:T(4,128)(2,1)} %refs_0_.1), channel_id=1, source_target_pairs={{0,8},{1,9},{2,10},{3,11},{4,12},{5,13},{6,14},{7,15},{8,0},{9,1},... | collective-permute-start | bytes 393224 | tf_op jit(solution)/shard_map/ppermute | solution.py:168
  4.7 1.6 %collective-permute-start.1 = (bf16[2,4,8192]{2,1,0:T(4,128)(2,1)}, bf16[2,4,8192]{2,1,0:T(4,128)(2,1)S(1)}, u32[]{:S(2)}, u32[]{:S(2)}) collective-permute-start(bf16[2,4,8192]{2,1,0:T(4,128)(2,1)} %refs_0_.1), channel_id=1, source_target_pairs={{0,4},{1,5},{2,6},{3,7},{4,0},{5,1},{6,2},{7,3},{8,12},{9,13},{10,... | collective-permute-start | bytes 393224 | tf_op jit(solution)/shard_map/ppermute | solution.py:168
  6.3 1.7 %collective-permute-start.3 = (bf16[2,4,8192]{2,1,0:T(4,128)(2,1)}, bf16[2,4,8192]{2,1,0:T(4,128)(2,1)S(1)}, u32[]{:S(2)}, u32[]{:S(2)}) collective-permute-start(bf16[2,4,8192]{2,1,0:T(4,128)(2,1)} %refs_0_.1), channel_id=1, source_target_pairs={{0,2},{1,3},{2,0},{3,1},{4,6},{5,7},{6,4},{7,5},{8,10},{9,11},{10,... | collective-permute-start | bytes 393224 | tf_op jit(solution)/shard_map/ppermute | solution.py:168
  8.1 0.0 collective-permute-start.7
  8.1 4.8 %collective-permute-done.refs_1_ = bf16[2,4,8192]{2,1,0:T(4,128)(2,1)S(1)} collective-permute-done((bf16[2,4,8192]{2,1,0:T(4,128)(2,1)}, bf16[2,4,8192]{2,1,0:T(4,128)(2,1)S(1)}, u32[]{:S(2)}, u32[]{:S(2)}) %collective-permute-start) | collective-permute-done | bytes 131104 | tf_op jit(solution)/shard_map/ppermute | solution.py:168
  12.9 2.2 %collective-permute-start.4 = (bf16[2,4,8192]{2,1,0:T(4,128)(2,1)S(1)}, bf16[2,4,8192]{2,1,0:T(4,128)(2,1)S(1)}, u32[]{:S(2)}, u32[]{:S(2)}) collective-permute-start(bf16[2,4,8192]{2,1,0:T(4,128)(2,1)S(1)} %collective-permute-done.refs_1_), channel_id=1, source_target_pairs={{0,2},{1,3},{2,0},{3,1},{4,6},{5,7},{6,4},{7,5},{8,10},{9,11},{10,... | collective-permute-start | bytes 393224 | tf_op jit(solution)/shard_map/ppermute | solution.py:168
  15.1 0.0 collective-permute-start.5
  15.1 0.2 collective-permute-done.2.refs_3_
  15.3 1.8 %collective-permute-start.6 = (bf16[2,4,8192]{2,1,0:T(4,128)(2,1)S(1)}, bf16[2,4,8192]{2,1,0:T(4,128)(2,1)S(1)}, u32[]{:S(2)}, u32[]{:S(2)}) collective-permute-start(bf16[2,4,8192]{2,1,0:T(4,128)(2,1)S(1)} %collective-permute-done.2.refs_3_), channel_id=1, source_target_pairs={{0,2},{1,3},{2,0},{3,1},{4,6},{5,7},{6,4},{7,5},{8,10},{9,11},{10,... | collective-permute-start | bytes 393224 | tf_op jit(solution)/shard_map/ppermute | solution.py:168
  17.1 0.0 collective-permute-done.3.refs_4_
  17.1 0.0 collective-permute-start.8
  17.1 0.5 collective-permute-start.9
  17.6 1.6 %collective-permute-done.4.refs_5_ = bf16[2,4,8192]{2,1,0:T(4,128)(2,1)S(1)} collective-permute-done((bf16[2,4,8192]{2,1,0:T(4,128)(2,1)S(1)}, bf16[2,4,8192]{2,1,0:T(4,128)(2,1)S(1)}, u32[]{:S(2)}, u32[]{:S(2)}) %collective-permute-start.4) | collective-permute-done | bytes 131104 | tf_op jit(solution)/shard_map/ppermute | solution.py:168
  19.2 1.6 %collective-permute-done.5.refs_6_ = bf16[2,4,8192]{2,1,0:T(4,128)(2,1)S(1)} collective-permute-done((bf16[2,4,8192]{2,1,0:T(4,128)(2,1)S(1)}, bf16[2,4,8192]{2,1,0:T(4,128)(2,1)S(1)}, u32[]{:S(2)}, u32[]{:S(2)}) %collective-permute-start.5) | collective-permute-done | bytes 131104 | tf_op jit(solution)/shard_map/ppermute | solution.py:168
  20.8 1.4 %collective-permute-done.6.refs_7_ = bf16[2,4,8192]{2,1,0:T(4,128)(2,1)S(1)} collective-permute-done((bf16[2,4,8192]{2,1,0:T(4,128)(2,1)S(1)}, bf16[2,4,8192]{2,1,0:T(4,128)(2,1)S(1)}, u32[]{:S(2)}, u32[]{:S(2)}) %collective-permute-start.6) | collective-permute-done | bytes 131104 | tf_op jit(solution)/shard_map/ppermute | solution.py:168
  22.2 0.5 collective-permute-start.13
  22.7 0.1 collective-permute-start.14
  22.8 0.9 %copy-done.2 = bf16[2,4,8192]{2,1,0:T(4,128)(2,1)S(1)} copy-done((bf16[2,4,8192]{2,1,0:T(4,128)(2,1)S(1)}, bf16[2,4,8192]{2,1,0:T(4,128)(2,1)}, u32[]{:S(2)}) %copy-start.2) | copy-done | bytes 131096
  23.7 0.8 %copy-done.4 = s32[2,8192]{1,0:T(2,128)S(1)} copy-done((s32[2,8192]{1,0:T(2,128)S(1)}, s32[2,8192]{1,0:T(2,128)}, u32[]{:S(2)}) %copy-start.4) | copy-done | bytes 65560
  24.6 0.8 %copy-done.5 = s32[2,8192]{1,0:T(2,128)S(1)} copy-done((s32[2,8192]{1,0:T(2,128)S(1)}, s32[2,8192]{1,0:T(2,128)}, u32[]{:S(2)}) %copy-start.5) | copy-done | bytes 65560
  25.4 0.8 %copy-done.6 = f32[2,8192]{1,0:T(2,128)S(1)} copy-done((f32[2,8192]{1,0:T(2,128)S(1)}, f32[2,8192]{1,0:T(2,128)}, u32[]{:S(2)}) %copy-start.6) | copy-done | bytes 65560
  26.2 0.8 %copy-done.7 = f32[2,8192]{1,0:T(2,128)S(1)} copy-done((f32[2,8192]{1,0:T(2,128)S(1)}, f32[2,8192]{1,0:T(2,128)}, u32[]{:S(2)}) %copy-start.7) | copy-done | bytes 65560
  27.1 0.8 %copy-done.8 = f32[8192]{0:T(1024)S(1)} copy-done((f32[8192]{0:T(1024)S(1)}, f32[8192]{0:T(1024)}, u32[]{:S(2)}) %copy-start.8) | copy-done | bytes 32792
  27.8 0.7 %prep.1 = (f32[8,8192]{1,0:T(8,128)S(1)}, f32[8,8192]{1,0:T(8,128)S(1)}, f32[1,16]{1,0:T(1,128)S(1)}) custom-call(bf16[2,4,8192]{2,1,0:T(4,128)(2,1)S(1)} %copy-done.2, s32[2,8192]{1,0:T(2,128)S(1)} %copy-done.4, s32[2,8192]{1,0:T(2,128)S(1)} %copy-done.5, f32[2,8192]{1,0:T(2,128)S(1)} %copy-done.6, f32[2,8192]{1,0:T(2,128)S(1)} %copy-done.7, ...), custom_call_target="tpu_custom_call" | custom-call | tf_op jit(solution)/shard_map/prep/pallas_call | solution.py:61
  28.6 0.5 copy-done.12
  29.1 3.4 %copy-done = bf16[8192,512]{1,0:T(8,128)(2,1)S(1)} copy-done((bf16[8192,512]{1,0:T(8,128)(2,1)S(1)}, bf16[8192,512]{1,0:T(8,128)(2,1)}, u32[]{:S(2)}) %copy-start) | copy-done | bytes 8388632
  32.4 0.7 %copy-done.9 = f32[2,512]{1,0:T(2,128)S(1)} copy-done((f32[2,512]{1,0:T(2,128)S(1)}, f32[2,512]{1,0:T(2,128)}, u32[]{:S(2)}) %copy-start.9) | copy-done | bytes 4120
  33.1 0.7 %copy-done.10 = f32[2,512]{1,0:T(2,128)S(1)} copy-done((f32[2,512]{1,0:T(2,128)S(1)}, f32[2,512]{1,0:T(2,128)}, u32[]{:S(2)}) %copy-start.10) | copy-done | bytes 4120
  33.8 1.4 %map_rows.3 = f32[1,128]{1,0:T(1,128)S(1)} custom-call(bf16[2,4,8192]{2,1,0:T(4,128)(2,1)S(1)} %collective-permute-done.7.refs_0_, bf16[2,4,8192]{2,1,0:T(4,128)(2,1)S(1)} %collective-permute-done.8.refs_1_, bf16[2,4,8192]{2,1,0:T(4,128)(2,1)S(1)} %collective-permute-done.9.refs_2_, bf16[2,4,8192]{2,1,0:T(4,128)(2,1)S(1)} %collective-permute-done.10.refs_3_, ...), custom_call_target="tpu_custom_call" | custom-call | flops 1073741824 | bytes 2097152 | tf_op jit(solution)/shard_map/map_rows/pallas_call | solution.py:111
  35.2 0.5 collective-permute-start.15
  35.7 1.5 %copy-done.1 = bf16[8192,512]{1,0:T(8,128)(2,1)S(1)} copy-done((bf16[8192,512]{1,0:T(8,128)(2,1)S(1)}, bf16[8192,512]{1,0:T(8,128)(2,1)}, u32[]{:S(2)}) %copy-start.1) | copy-done | bytes 8388632
  37.2 1.4 %map_rows.2.kept = f32[1,128]{1,0:T(1,128)S(1)} custom-call(bf16[2,4,8192]{2,1,0:T(4,128)(2,1)S(1)} %copy-done.3, bf16[2,4,8192]{2,1,0:T(4,128)(2,1)S(1)} %collective-permute-done.refs_1_, bf16[2,4,8192]{2,1,0:T(4,128)(2,1)S(1)} %collective-permute-done.1.refs_2_, bf16[2,4,8192]{2,1,0:T(4,128)(2,1)S(1)} %collective-permute-done.2.refs_3_, ...), custom_call_target="tpu_custom_call" | custom-call | flops 1073741824 | bytes 2097152 | tf_op jit(solution)/shard_map/map_rows/pallas_call | solution.py:111
  38.6 0.0 copy-start.11
  38.6 0.5 copy-done.11
  39.1 0.5 copy-done.13
  39.6 1.3 %fold.3 = (f32[1,64]{1,0:T(1,128)}, f32[1,64]{1,0:T(1,128)}) custom-call(f32[1,128]{1,0:T(1,128)} %copy-done.11, f32[1,128]{1,0:T(1,128)} %copy-done.13), custom_call_target="tpu_custom_call" | custom-call | tf_op jit(solution)/shard_map/fold/pallas_call | solution.py:134
  40.9 1.7 %collective-permute-start.16 = (f32[1,64]{1,0:T(1,128)}, f32[1,64]{1,0:T(1,128)S(1)}, u32[]{:S(2)}, u32[]{:S(2)}) collective-permute-start(f32[1,64]{1,0:T(1,128)} %get-tuple-element.14), channel_id=1, source_target_pairs={{0,2},{1,3},{2,0},{3,1},{4,6},{5,7},{6,4},{7,5},{8,10},{9,11},{10,... | collective-permute-start | bytes 776 | tf_op jit(solution)/shard_map/ppermute | solution.py:168
  42.6 2.1 %collective-permute-done.16.came = f32[1,64]{1,0:T(1,128)S(1)} collective-permute-done((f32[1,64]{1,0:T(1,128)}, f32[1,64]{1,0:T(1,128)S(1)}, u32[]{:S(2)}, u32[]{:S(2)}) %collective-permute-start.16) | collective-permute-done | bytes 288 | tf_op jit(solution)/shard_map/ppermute | solution.py:168
  44.6 0.5 copy-done.15
  45.1 1.3 %fold.4 = (f32[1,32]{1,0:T(1,128)}, f32[1,32]{1,0:T(1,128)}) custom-call(f32[1,64]{1,0:T(1,128)} %get-tuple-element.13.kept, f32[1,64]{1,0:T(1,128)} %copy-done.15), custom_call_target="tpu_custom_call" | custom-call | tf_op jit(solution)/shard_map/fold/pallas_call | solution.py:134
  46.4 1.4 %collective-permute-start.17 = (f32[1,32]{1,0:T(1,128)}, f32[1,32]{1,0:T(1,128)S(1)}, u32[]{:S(2)}, u32[]{:S(2)}) collective-permute-start(f32[1,32]{1,0:T(1,128)} %get-tuple-element.16), channel_id=1, source_target_pairs={{0,4},{1,5},{2,6},{3,7},{4,0},{5,1},{6,2},{7,3},{8,12},{9,13},{10,... | collective-permute-start | bytes 392 | tf_op jit(solution)/shard_map/ppermute | solution.py:168
  47.9 2.3 %collective-permute-done.17.came = f32[1,32]{1,0:T(1,128)S(1)} collective-permute-done((f32[1,32]{1,0:T(1,128)}, f32[1,32]{1,0:T(1,128)S(1)}, u32[]{:S(2)}, u32[]{:S(2)}) %collective-permute-start.17) | collective-permute-done | bytes 160 | tf_op jit(solution)/shard_map/ppermute | solution.py:168
  50.2 0.5 copy-done.16
  50.7 1.3 %fold.5 = (f32[1,16]{1,0:T(1,128)}, f32[1,16]{1,0:T(1,128)}) custom-call(f32[1,32]{1,0:T(1,128)} %get-tuple-element.15.kept, f32[1,32]{1,0:T(1,128)} %copy-done.16), custom_call_target="tpu_custom_call" | custom-call | tf_op jit(solution)/shard_map/fold/pallas_call | solution.py:134
  52.0 3.2 %collective-permute-start.18 = (f32[1,16]{1,0:T(1,128)}, f32[1,16]{1,0:T(1,128)S(1)}, u32[]{:S(2)}, u32[]{:S(2)}) collective-permute-start(f32[1,16]{1,0:T(1,128)} %get-tuple-element.18), channel_id=1, source_target_pairs={{0,8},{1,9},{2,10},{3,11},{4,12},{5,13},{6,14},{7,15},{8,0},{9,1},... | collective-permute-start | bytes 200 | tf_op jit(solution)/shard_map/ppermute | solution.py:168
  55.1 1.7 %collective-permute-done.18.came = f32[1,16]{1,0:T(1,128)S(1)} collective-permute-done((f32[1,16]{1,0:T(1,128)}, f32[1,16]{1,0:T(1,128)S(1)}, u32[]{:S(2)}, u32[]{:S(2)}) %collective-permute-start.18) | collective-permute-done | bytes 96 | tf_op jit(solution)/shard_map/ppermute | solution.py:168
  56.9 0.5 copy-done.14
  57.4 1.3 %finish.1 = (f32[2,4]{1,0:T(2,128)}, f32[2,4]{1,0:T(2,128)}) custom-call(f32[1,16]{1,0:T(1,128)} %get-tuple-element.17.kept, f32[1,16]{1,0:T(1,128)} %copy-done.14, f32[1,16]{1,0:T(1,128)} %copy-done.12), custom_call_target="tpu_custom_call" | custom-call | tf_op jit(solution)/shard_map/finish/pallas_call | solution.py:153
  (31 shorter events, 0.1 us)
Async XLA Ops:
  0.6 12.3 %collective-permute-start = (bf16[2,4,8192]{2,1,0:T(4,128)(2,1)}, bf16[2,4,8192]{2,1,0:T(4,128)(2,1)S(1)}, u32[]{:S(2)}, u32[]{:S(2)}) collective-permute-start(bf16[2,4,8192]{2,1,0:T(4,128)(2,1)} %refs_0_.1), channel_id=1, source_target_pairs={{0,8},{1,9},{2,10},{3,11},{4,12},{5,13},{6,14},{7,15},{8,0},{9,1},... | collective-permute-start | bytes 393224 | tf_op jit(solution)/shard_map/ppermute | solution.py:168
  4.7 10.3 %collective-permute-start.1 = (bf16[2,4,8192]{2,1,0:T(4,128)(2,1)}, bf16[2,4,8192]{2,1,0:T(4,128)(2,1)S(1)}, u32[]{:S(2)}, u32[]{:S(2)}) collective-permute-start(bf16[2,4,8192]{2,1,0:T(4,128)(2,1)} %refs_0_.1), channel_id=1, source_target_pairs={{0,4},{1,5},{2,6},{3,7},{4,0},{5,1},{6,2},{7,3},{8,12},{9,13},{10,... | collective-permute-start | bytes 393224 | tf_op jit(solution)/shard_map/ppermute | solution.py:168
  6.3 9.0 %collective-permute-start.2 = (bf16[2,4,8192]{2,1,0:T(4,128)(2,1)}, bf16[2,4,8192]{2,1,0:T(4,128)(2,1)S(1)}, u32[]{:S(2)}, u32[]{:S(2)}) collective-permute-start(bf16[2,4,8192]{2,1,0:T(4,128)(2,1)} %refs_0_.1), channel_id=1, source_target_pairs={{0,12},{1,13},{2,14},{3,15},{4,8},{5,9},{6,10},{7,11},{8,4},{9,5},... | collective-permute-start | bytes 393224 | tf_op jit(solution)/shard_map/ppermute | solution.py:168
  6.3 10.8 %collective-permute-start.3 = (bf16[2,4,8192]{2,1,0:T(4,128)(2,1)}, bf16[2,4,8192]{2,1,0:T(4,128)(2,1)S(1)}, u32[]{:S(2)}, u32[]{:S(2)}) collective-permute-start(bf16[2,4,8192]{2,1,0:T(4,128)(2,1)} %refs_0_.1), channel_id=1, source_target_pairs={{0,2},{1,3},{2,0},{3,1},{4,6},{5,7},{6,4},{7,5},{8,10},{9,11},{10,... | collective-permute-start | bytes 393224 | tf_op jit(solution)/shard_map/ppermute | solution.py:168
  8.1 9.0 %collective-permute-start.7 = (bf16[2,4,8192]{2,1,0:T(4,128)(2,1)}, bf16[2,4,8192]{2,1,0:T(4,128)(2,1)S(1)}, u32[]{:S(2)}, u32[]{:S(2)}) collective-permute-start(bf16[2,4,8192]{2,1,0:T(4,128)(2,1)} %refs_0_.1), channel_id=1, source_target_pairs={{0,1},{1,0},{2,3},{3,2},{4,5},{5,4},{6,7},{7,6},{8,9},{9,8},{10,11... | collective-permute-start | bytes 393224 | tf_op jit(solution)/shard_map/ppermute | solution.py:168
  12.9 6.3 %collective-permute-start.4 = (bf16[2,4,8192]{2,1,0:T(4,128)(2,1)S(1)}, bf16[2,4,8192]{2,1,0:T(4,128)(2,1)S(1)}, u32[]{:S(2)}, u32[]{:S(2)}) collective-permute-start(bf16[2,4,8192]{2,1,0:T(4,128)(2,1)S(1)} %collective-permute-done.refs_1_), channel_id=1, source_target_pairs={{0,2},{1,3},{2,0},{3,1},{4,6},{5,7},{6,4},{7,5},{8,10},{9,11},{10,... | collective-permute-start | bytes 393224 | tf_op jit(solution)/shard_map/ppermute | solution.py:168
  15.1 5.8 %collective-permute-start.5 = (bf16[2,4,8192]{2,1,0:T(4,128)(2,1)S(1)}, bf16[2,4,8192]{2,1,0:T(4,128)(2,1)S(1)}, u32[]{:S(2)}, u32[]{:S(2)}) collective-permute-start(bf16[2,4,8192]{2,1,0:T(4,128)(2,1)S(1)} %collective-permute-done.1.refs_2_), channel_id=1, source_target_pairs={{0,2},{1,3},{2,0},{3,1},{4,6},{5,7},{6,4},{7,5},{8,10},{9,11},{10,... | collective-permute-start | bytes 393224 | tf_op jit(solution)/shard_map/ppermute | solution.py:168
  15.3 6.9 %collective-permute-start.6 = (bf16[2,4,8192]{2,1,0:T(4,128)(2,1)S(1)}, bf16[2,4,8192]{2,1,0:T(4,128)(2,1)S(1)}, u32[]{:S(2)}, u32[]{:S(2)}) collective-permute-start(bf16[2,4,8192]{2,1,0:T(4,128)(2,1)S(1)} %collective-permute-done.2.refs_3_), channel_id=1, source_target_pairs={{0,2},{1,3},{2,0},{3,1},{4,6},{5,7},{6,4},{7,5},{8,10},{9,11},{10,... | collective-permute-start | bytes 393224 | tf_op jit(solution)/shard_map/ppermute | solution.py:168
  17.1 5.1 %collective-permute-start.8 = (bf16[2,4,8192]{2,1,0:T(4,128)(2,1)S(1)}, bf16[2,4,8192]{2,1,0:T(4,128)(2,1)S(1)}, u32[]{:S(2)}, u32[]{:S(2)}) collective-permute-start(bf16[2,4,8192]{2,1,0:T(4,128)(2,1)S(1)} %collective-permute-done.refs_1_), channel_id=1, source_target_pairs={{0,1},{1,0},{2,3},{3,2},{4,5},{5,4},{6,7},{7,6},{8,9},{9,8},{10,11... | collective-permute-start | bytes 393224 | tf_op jit(solution)/shard_map/ppermute | solution.py:168
  17.1 5.6 %collective-permute-start.9 = (bf16[2,4,8192]{2,1,0:T(4,128)(2,1)S(1)}, bf16[2,4,8192]{2,1,0:T(4,128)(2,1)S(1)}, u32[]{:S(2)}, u32[]{:S(2)}) collective-permute-start(bf16[2,4,8192]{2,1,0:T(4,128)(2,1)S(1)} %collective-permute-done.1.refs_2_), channel_id=1, source_target_pairs={{0,1},{1,0},{2,3},{3,2},{4,5},{5,4},{6,7},{7,6},{8,9},{9,8},{10,11... | collective-permute-start | bytes 393224 | tf_op jit(solution)/shard_map/ppermute | solution.py:168
  19.2 9.3 %collective-permute-start.10 = (bf16[2,4,8192]{2,1,0:T(4,128)(2,1)S(1)}, bf16[2,4,8192]{2,1,0:T(4,128)(2,1)S(1)}, u32[]{:S(2)}, u32[]{:S(2)}) collective-permute-start(bf16[2,4,8192]{2,1,0:T(4,128)(2,1)S(1)} %collective-permute-done.2.refs_3_), channel_id=1, source_target_pairs={{0,1},{1,0},{2,3},{3,2},{4,5},{5,4},{6,7},{7,6},{8,9},{9,8},{10,11... | collective-permute-start | bytes 393224 | tf_op jit(solution)/shard_map/ppermute | solution.py:168
  20.8 7.7 %collective-permute-start.11 = (bf16[2,4,8192]{2,1,0:T(4,128)(2,1)S(1)}, bf16[2,4,8192]{2,1,0:T(4,128)(2,1)S(1)}, u32[]{:S(2)}, u32[]{:S(2)}) collective-permute-start(bf16[2,4,8192]{2,1,0:T(4,128)(2,1)S(1)} %collective-permute-done.3.refs_4_), channel_id=1, source_target_pairs={{0,1},{1,0},{2,3},{3,2},{4,5},{5,4},{6,7},{7,6},{8,9},{9,8},{10,11... | collective-permute-start | bytes 393224 | tf_op jit(solution)/shard_map/ppermute | solution.py:168
  22.2 6.3 %collective-permute-start.12 = (bf16[2,4,8192]{2,1,0:T(4,128)(2,1)S(1)}, bf16[2,4,8192]{2,1,0:T(4,128)(2,1)S(1)}, u32[]{:S(2)}, u32[]{:S(2)}) collective-permute-start(bf16[2,4,8192]{2,1,0:T(4,128)(2,1)S(1)} %collective-permute-done.4.refs_5_), channel_id=1, source_target_pairs={{0,1},{1,0},{2,3},{3,2},{4,5},{5,4},{6,7},{7,6},{8,9},{9,8},{10,11... | collective-permute-start | bytes 393224 | tf_op jit(solution)/shard_map/ppermute | solution.py:168
  22.2 6.3 %collective-permute-start.13 = (bf16[2,4,8192]{2,1,0:T(4,128)(2,1)S(1)}, bf16[2,4,8192]{2,1,0:T(4,128)(2,1)S(1)}, u32[]{:S(2)}, u32[]{:S(2)}) collective-permute-start(bf16[2,4,8192]{2,1,0:T(4,128)(2,1)S(1)} %collective-permute-done.5.refs_6_), channel_id=1, source_target_pairs={{0,1},{1,0},{2,3},{3,2},{4,5},{5,4},{6,7},{7,6},{8,9},{9,8},{10,11... | collective-permute-start | bytes 393224 | tf_op jit(solution)/shard_map/ppermute | solution.py:168
  22.7 5.8 %collective-permute-start.14 = (bf16[2,4,8192]{2,1,0:T(4,128)(2,1)S(1)}, bf16[2,4,8192]{2,1,0:T(4,128)(2,1)S(1)}, u32[]{:S(2)}, u32[]{:S(2)}) collective-permute-start(bf16[2,4,8192]{2,1,0:T(4,128)(2,1)S(1)} %collective-permute-done.6.refs_7_), channel_id=1, source_target_pairs={{0,1},{1,0},{2,3},{3,2},{4,5},{5,4},{6,7},{7,6},{8,9},{9,8},{10,11... | collective-permute-start | bytes 393224 | tf_op jit(solution)/shard_map/ppermute | solution.py:168
  22.8 0.9 %copy-start.2 = (bf16[2,4,8192]{2,1,0:T(4,128)(2,1)S(1)}, bf16[2,4,8192]{2,1,0:T(4,128)(2,1)}, u32[]{:S(2)}) copy-start(bf16[2,4,8192]{2,1,0:T(4,128)(2,1)} %refs_0_.1) | copy-start | bytes 393220
  23.7 0.8 %copy-start.4 = (s32[2,8192]{1,0:T(2,128)S(1)}, s32[2,8192]{1,0:T(2,128)}, u32[]{:S(2)}) copy-start(s32[2,8192]{1,0:T(2,128)} %status.1) | copy-start | bytes 196612
  24.5 0.8 %copy-start.5 = (s32[2,8192]{1,0:T(2,128)S(1)}, s32[2,8192]{1,0:T(2,128)}, u32[]{:S(2)}) copy-start(s32[2,8192]{1,0:T(2,128)} %bit.1) | copy-start | bytes 196612
  25.4 0.8 %copy-start.6 = (f32[2,8192]{1,0:T(2,128)S(1)}, f32[2,8192]{1,0:T(2,128)}, u32[]{:S(2)}) copy-start(f32[2,8192]{1,0:T(2,128)} %lower.1) | copy-start | bytes 196612
  26.2 0.8 %copy-start.7 = (f32[2,8192]{1,0:T(2,128)S(1)}, f32[2,8192]{1,0:T(2,128)}, u32[]{:S(2)}) copy-start(f32[2,8192]{1,0:T(2,128)} %upper.1) | copy-start | bytes 196612
  27.1 0.8 %copy-start.8 = (f32[8192]{0:T(1024)S(1)}, f32[8192]{0:T(1024)}, u32[]{:S(2)}) copy-start(f32[8192]{0:T(1024)} %param.15) | copy-start | bytes 98308
  27.8 7.9 %copy-start.3 = (bf16[2,4,8192]{2,1,0:T(4,128)(2,1)S(1)}, bf16[2,4,8192]{2,1,0:T(4,128)(2,1)}, u32[]{:S(2)}) copy-start(bf16[2,4,8192]{2,1,0:T(4,128)(2,1)} %refs_0_.1) | copy-start | bytes 393220
  28.5 0.5 copy-start.12
  29.1 3.4 %copy-start = (bf16[8192,512]{1,0:T(8,128)(2,1)S(1)}, bf16[8192,512]{1,0:T(8,128)(2,1)}, u32[]{:S(2)}) copy-start(bf16[8192,512]{1,0:T(8,128)(2,1)} %refs_10_.3) | copy-start | bytes 25165828
  32.4 0.7 %copy-start.9 = (f32[2,512]{1,0:T(2,128)S(1)}, f32[2,512]{1,0:T(2,128)}, u32[]{:S(2)}) copy-start(f32[2,512]{1,0:T(2,128)} %refs_11_.3) | copy-start | bytes 12292
  33.1 0.7 %copy-start.10 = (f32[2,512]{1,0:T(2,128)S(1)}, f32[2,512]{1,0:T(2,128)}, u32[]{:S(2)}) copy-start(f32[2,512]{1,0:T(2,128)} %refs_12_.3) | copy-start | bytes 12292
  33.8 3.4 %copy-start.1 = (bf16[8192,512]{1,0:T(8,128)(2,1)S(1)}, bf16[8192,512]{1,0:T(8,128)(2,1)}, u32[]{:S(2)}) copy-start(bf16[8192,512]{1,0:T(8,128)(2,1)} %refs_10_.3) | copy-start | bytes 25165828
  35.2 3.9 %collective-permute-start.15 = (f32[1,128]{1,0:T(1,128)S(1)}, f32[1,128]{1,0:T(1,128)S(1)}, u32[]{:S(2)}, u32[]{:S(2)}) collective-permute-start(f32[1,128]{1,0:T(1,128)S(1)} %map_rows.3), channel_id=1, source_target_pairs={{0,1},{1,0},{2,3},{3,2},{4,5},{5,4},{6,7},{7,6},{8,9},{9,8},{10,11... | collective-permute-start | bytes 1544 | tf_op jit(solution)/shard_map/ppermute | solution.py:168
  38.6 0.5 copy-start.11
  39.1 0.5 copy-start.13
  40.9 3.8 %collective-permute-start.16 = (f32[1,64]{1,0:T(1,128)}, f32[1,64]{1,0:T(1,128)S(1)}, u32[]{:S(2)}, u32[]{:S(2)}) collective-permute-start(f32[1,64]{1,0:T(1,128)} %get-tuple-element.14), channel_id=1, source_target_pairs={{0,2},{1,3},{2,0},{3,1},{4,6},{5,7},{6,4},{7,5},{8,10},{9,11},{10,... | collective-permute-start | bytes 776 | tf_op jit(solution)/shard_map/ppermute | solution.py:168
  44.6 0.5 copy-start.15
  46.4 3.8 %collective-permute-start.17 = (f32[1,32]{1,0:T(1,128)}, f32[1,32]{1,0:T(1,128)S(1)}, u32[]{:S(2)}, u32[]{:S(2)}) collective-permute-start(f32[1,32]{1,0:T(1,128)} %get-tuple-element.16), channel_id=1, source_target_pairs={{0,4},{1,5},{2,6},{3,7},{4,0},{5,1},{6,2},{7,3},{8,12},{9,13},{10,... | collective-permute-start | bytes 392 | tf_op jit(solution)/shard_map/ppermute | solution.py:168
  50.2 0.5 copy-start.16
  52.0 4.9 %collective-permute-start.18 = (f32[1,16]{1,0:T(1,128)}, f32[1,16]{1,0:T(1,128)S(1)}, u32[]{:S(2)}, u32[]{:S(2)}) collective-permute-start(f32[1,16]{1,0:T(1,128)} %get-tuple-element.18), channel_id=1, source_target_pairs={{0,8},{1,9},{2,10},{3,11},{4,12},{5,13},{6,14},{7,15},{8,0},{9,1},... | collective-permute-start | bytes 200 | tf_op jit(solution)/shard_map/ppermute | solution.py:168
  56.9 0.5 copy-start.14

commit v3 on v2

--- a/solution.py
+++ b/solution.py
@@ -22,7 +22,15 @@
     return jnp.sum(folded.T, axis=0, keepdims=True)
 
 
-def prep_kernel(coeff, status, bit, lower, upper, bias, inner_out, outer_out, own_out):
+def prep_kernel(*refs):
+    sources, (inner_out, outer_out, own_out, weight_out), held, done = refs[:7], refs[7:11], refs[11:17], refs[17]
+    targets = (*held, weight_out)
+    copies = [pltpu.make_async_copy(s, t, done.at[i]) for i, (s, t) in enumerate(zip(sources, targets))]
+    for copy in copies:
+        copy.start()
+    for copy in copies[:-1]:
+        copy.wait()
+    coeff, status, bit, lower, upper, bias = held
     examples, specs, neurons = coeff.shape
     low, high = lower[...], upper[...]
     slope = high / (high - low)
@@ -53,23 +61,30 @@
     if rows < LANES:
         folded = jnp.concatenate([folded, jnp.zeros((LANES - rows, LANES), F32)], axis=0)
     own_out[...] = jnp.sum(folded.T, axis=0, keepdims=True)[:, 0:rows]
-
-
-def prep(coeff, status, bit, lower, upper, bias):
+    copies[-1].wait()
+
+
+def prep(coeff, status, bit, lower, upper, bias, weight):
     examples, specs, neurons = coeff.shape
     rows = examples * specs
+    small = (coeff, status, bit, lower, upper, bias)
     return pl.pallas_call(
         prep_kernel,
-        in_specs=[VMEM] * 6,
-        out_specs=(VMEM, VMEM, VMEM),
+        in_specs=[pl.BlockSpec(memory_space=pltpu.HBM)] * 7,
+        out_specs=(VMEM, VMEM, VMEM, VMEM),
         out_shape=(
             jax.ShapeDtypeStruct((rows, neurons), F32),
             jax.ShapeDtypeStruct((rows, neurons), F32),
             jax.ShapeDtypeStruct((1, 2 * rows), F32),
+            jax.ShapeDtypeStruct(weight.shape, weight.dtype),
         ),
-        compiler_params=pltpu.CompilerParams(vmem_limit_bytes=16 << 20),
+        scratch_shapes=[pltpu.VMEM(a.shape, a.dtype) for a in small] + [pltpu.SemaphoreType.DMA((7,))],
+        compiler_params=pltpu.CompilerParams(vmem_limit_bytes=8 << 20),
+        cost_estimate=pl.CostEstimate(
+            flops=20 * rows * neurons, bytes_accessed=2 * weight.size + 12 * rows * neurons, transcendentals=0
+        ),
         name="prep",
-    )(coeff, status, bit, lower, upper, bias)
+    )(*[pltpu.with_memory_space_constraint(a, pltpu.HBM) for a in (*small, weight)])
 
 
 def map_kernel(num_pieces, *refs):
@@ -104,22 +119,43 @@
     out[...] = lane_sums(cells)
 
 
-def map_rows(pieces, inner, outer, weight, center, radius):
+def join_kernel(order, num_pieces, *refs):
+    *ins, early, keep_out, send_out, relaxed, late = refs
+    map_kernel(num_pieces, *ins, late, relaxed)
+    width = early.shape[1] // (len(order) - num_pieces)
+    parts = []
+    for source, index in order:
+        parts.append((early, late)[source][:, index * width : (index + 1) * width])
+    half = len(parts) // 2
+    keep_out[...] = jnp.concatenate(parts[:half], axis=1)
+    send_out[...] = jnp.concatenate(parts[half:], axis=1)
+
+
+def map_rows(pieces, args, early=None, order=None):
     examples, specs, neurons = pieces[0].shape
     rows = 2 * examples * specs * len(pieces)
-    columns = weight.shape[1]
-    return pl.pallas_call(
-        functools.partial(map_kernel, len(pieces)),
-        in_specs=[VMEM] * (len(pieces) + 5),
-        out_specs=VMEM,
-        out_shape=jax.ShapeDtypeStruct((1, rows), F32),
-        scratch_shapes=[pltpu.VMEM((rows, neurons), BF16)],
-        compiler_params=pltpu.CompilerParams(vmem_limit_bytes=32 << 20),
+    columns = args[2].shape[1]
+    scratch = [pltpu.VMEM((rows, neurons), BF16)]
+    if early is None:
+        kernel, more = functools.partial(map_kernel, len(pieces)), ()
+        out_specs, out_shape = VMEM, jax.ShapeDtypeStruct((1, rows), F32)
+    else:
+        kernel, more = functools.partial(join_kernel, order, len(pieces)), (early,)
+        half = (rows + early.shape[1]) // 2
+        out_specs, out_shape = (VMEM, VMEM), (jax.ShapeDtypeStruct((1, half), F32),) * 2
+        scratch.append(pltpu.VMEM((1, rows), F32))
+    return pl.pallas_call(
+        kernel,
+        in_specs=[VMEM] * (len(pieces) + len(args) + len(more)),
+        out_specs=out_specs,
+        out_shape=out_shape,
+        scratch_shapes=scratch,
+        compiler_params=pltpu.CompilerParams(vmem_limit_bytes=24 << 20),
         cost_estimate=pl.CostEstimate(
             flops=2 * rows * neurons * columns, bytes_accessed=2 * rows * neurons, transcendentals=0
         ),
         name="map_rows",
-    )(*pieces, inner, outer, weight, center, radius)
+    )(*pieces, *args, *more)
 
 
 def fold_kernel(kept, came, keep_out, send_out):
@@ -136,6 +172,7 @@
         in_specs=[VMEM] * 2,
         out_specs=(VMEM, VMEM),
         out_shape=(jax.ShapeDtypeStruct((1, half), F32),) * 2,
+        compiler_params=pltpu.CompilerParams(vmem_limit_bytes=1 << 20),
         name="fold",
     )(kept, came)
 
@@ -155,6 +192,7 @@
         in_specs=[VMEM] * 3,
         out_specs=(VMEM, VMEM),
         out_shape=(jax.ShapeDtypeStruct((examples, specs), F32),) * 2,
+        compiler_params=pltpu.CompilerParams(vmem_limit_bytes=1 << 20),
         name="finish",
     )(kept, came, own)
 
@@ -167,22 +205,30 @@
     def swap(array, mask):
         return lax.ppermute(array, "row", [(i, i ^ mask) for i in range(num_devices)])
 
-    inner, outer, own = prep(bound_coeff, status, slope_bit, pre_lower, pre_upper, layer_bias.reshape(1, neurons))
+    inner, outer, own, held = prep(
+        bound_coeff, status, slope_bit, pre_lower, pre_upper, layer_bias.reshape(1, neurons), weight
+    )
 
     pieces = {0: bound_coeff}
     for mask in range(4, num_devices, 4):
         pieces[mask] = swap(bound_coeff, mask)
+    pieces[4], held = lax.optimization_barrier((pieces[4], held))
     for mask in range(0, num_devices, 4):
         pieces[mask + 2] = swap(pieces[mask], 2)
-    for mask in range(0, num_devices, 2):
+    args = (inner, outer, held, center_input, radius)
+    early = [0, 4, 2, 6, 1, 5, 3, 7]
+    late = sorted(set(range(num_devices)) - set(early), key=lambda m: (m & 1, m & 2, -m))
+    for mask in (0, 4, 2, 6):
         pieces[mask + 1] = swap(pieces[mask], 1)
-
-    args = (inner, outer, weight, center_input, radius)
+    first = map_rows([pieces[m] for m in early], args)
+    for mask in late:
+        if mask & 1 == 0:
+            pieces[mask + 1] = swap(pieces[mask], 1)
+
     bits = num_devices.bit_length() - 1
-    order = [int(format(i, "b").zfill(bits)[::-1], 2) for i in range(num_devices)]
-    half = num_devices // 2
-    keep = map_rows([pieces[m] for m in order[:half]], *args)
-    send = map_rows([pieces[m] for m in order[half:]], *args)
+    sent = [int(format(i, "b").zfill(bits)[::-1], 2) for i in range(num_devices)]
+    order = [(0, early.index(m)) if m in early else (1, late.index(m)) for m in sent]
+    keep, send = map_rows([pieces[m] for m in late], args, first, order)
     for bit in range(bits):
         came = swap(send, 1 << bit)
         if bit < bits - 1:

time: 59.3 us -> 42.9 us (0.72)
  local copies, waits for them, and re-layouts: 14.3 us -> 0.01 us
  starting transfers between devices: 19.3 us -> 13.6 us
  waiting for transfers between devices: 15.7 us -> 20.9 us
  Pallas kernels: 8.58 us -> 7.45 us
    unnamed x34 -> x6, local copies, waits for them, and re-layouts: 14.3 us -> 0.01 us
    ppermute x19, starting transfers between devices: 19.3 us -> 13.6 us  [swap(): lax.ppermute(array, 'row', [(i, i ^ mask) for i in range(num_devices)])]
    ppermute x19, waiting for transfers between devices: 15.7 us -> 20.9 us  [swap(): lax.ppermute(array, 'row', [(i, i ^ mask) for i in range(num_devices)])]
    pallas_call x3, Pallas kernels: 3.83 us -> 0.22 us  [fold(): pl.pallas_call(fold_kernel, in_specs=[VMEM] * 2, out_specs=(VMEM, VMEM),...]
    pallas_call x3, Pallas kernels: 3.45 us -> 6.59 us  [the longest x1 3.7 us: prep(): pl.pallas_call(prep_kernel, in_specs=[pl.BlockSpec(memory_space=pltpu.HBM...]
    pallas_call x1, Pallas kernels: 1.3 us -> 0.64 us  [finish(): pl.pallas_call(finish_kernel, in_specs=[VMEM] * 3, out_specs=(VMEM, VMEM)...]
  transfers between devices with their start and end apart: 19 -> 19, of which waited for: 8 -> 7; matrix products, arithmetic and copies ran while one was open for 0% -> 0% of each run, Pallas kernels for 4% -> 12%
where the time goes in v3:
time: 42.9 us; the launch traced here: 42.7 us
  waiting for transfers between devices  20.9 us (49%)
  starting transfers between devices  13.6 us (32%)
  Pallas kernels  7.45 us (17%)
  between operations  0.76 us (2%)
    ppermute x19, waiting for transfers between devices, swap(): lax.ppermute(array, 'row', [(i, i ^ mask) for i in range(num_devices)])  20.9 us
    ppermute x19, starting transfers between devices, swap(): lax.ppermute(array, 'row', [(i, i ^ mask) for i in range(num_devices)])  13.6 us
    pallas_call x1, Pallas kernels, prep(): pl.pallas_call(prep_kernel, in_specs=[pl.BlockSpec(memory_space=pltpu.HBM...  3.7 us
    pallas_call x2, Pallas kernels, map_rows(): pl.pallas_call(kernel, in_specs=[VMEM] * (len(pieces) + len(args) + len(m...  2.9 us
  transfers between devices with their start and end apart: 19, of which 7 were waited for; matrix products, arithmetic and copies ran while one was open for 0% of the time, Pallas kernels for 12%

profile of v3, /device:TPU:0, one launch (start us, length us, event | category | flops | bytes accessed | tf_op | source)
XLA Modules:
  0.0 42.7 jit_solution(4168991924552044928)
XLA Ops:
  0.6 0.0 copy-start
  0.6 0.0 copy-start.1
  0.7 3.1 %collective-permute-start.8 = (bf16[2,4,8192]{2,1,0:T(4,128)(2,1)}, bf16[2,4,8192]{2,1,0:T(4,128)(2,1)S(1)}, u32[]{:S(2)}, u32[]{:S(2)}) collective-permute-start(bf16[2,4,8192]{2,1,0:T(4,128)(2,1)} %refs_0_.3), channel_id=1, source_target_pairs={{0,4},{1,5},{2,6},{3,7},{4,0},{5,1},{6,2},{7,3},{8,12},{9,13},{10,... | collective-permute-start | bytes 393224 | tf_op jit(solution)/shard_map/ppermute | solution.py:206
  3.8 1.5 %collective-permute-start.9 = (bf16[2,4,8192]{2,1,0:T(4,128)(2,1)}, bf16[2,4,8192]{2,1,0:T(4,128)(2,1)S(1)}, u32[]{:S(2)}, u32[]{:S(2)}) collective-permute-start(bf16[2,4,8192]{2,1,0:T(4,128)(2,1)} %refs_0_.3), channel_id=1, source_target_pairs={{0,2},{1,3},{2,0},{3,1},{4,6},{5,7},{6,4},{7,5},{8,10},{9,11},{10,... | collective-permute-start | bytes 393224 | tf_op jit(solution)/shard_map/ppermute | solution.py:206
  5.3 0.0 collective-permute-start.11
  5.3 2.5 %collective-permute-start = (bf16[2,4,8192]{2,1,0:T(4,128)(2,1)}, bf16[2,4,8192]{2,1,0:T(4,128)(2,1)S(1)}, u32[]{:S(2)}, u32[]{:S(2)}) collective-permute-start(bf16[2,4,8192]{2,1,0:T(4,128)(2,1)} %refs_0_.3), channel_id=1, source_target_pairs={{0,12},{1,13},{2,14},{3,15},{4,8},{5,9},{6,10},{7,11},{8,4},{9,5},... | collective-permute-start | bytes 393224 | tf_op jit(solution)/shard_map/ppermute | solution.py:206
  7.8 0.1 collective-permute-start.1
  7.9 3.7 %prep.1 = (f32[8,8192]{1,0:T(8,128)S(1)}, f32[8,8192]{1,0:T(8,128)S(1)}, f32[1,16]{1,0:T(1,128)S(1)}, bf16[8192,512]{1,0:T(8,128)(2,1)S(1)}) custom-call(bf16[2,4,8192]{2,1,0:T(4,128)(2,1)} %refs_0_.3, s32[2,8192]{1,0:T(2,128)} %refs_1_.1, s32[2,8192]{1,0:T(2,128)} %refs_2_.1, f32[2,8192]{1,0:T(2,128)} %refs_3_.1, f32[2,8192]{1,0:T(2,128)} %refs_4_.1, ...), custom_call_target="tpu_custom_call" | custom-call | flops 1310720 | bytes 9175040 | tf_op jit(solution)/shard_map/prep/pallas_call | solution.py:71
  11.6 0.0 collective-permute-done.8.refs_1_
  11.6 0.6 %collective-permute-start.10 = (bf16[2,4,8192]{2,1,0:T(4,128)(2,1)S(1)}, bf16[2,4,8192]{2,1,0:T(4,128)(2,1)S(1)}, u32[]{:S(2)}, u32[]{:S(2)}) collective-permute-start(bf16[2,4,8192]{2,1,0:T(4,128)(2,1)S(1)} %collective-permute-done.8.refs_1_), channel_id=1, source_target_pairs={{0,2},{1,3},{2,0},{3,1},{4,6},{5,7},{6,4},{7,5},{8,10},{9,11},{10,... | collective-permute-start | bytes 393224 | tf_op jit(solution)/shard_map/ppermute | solution.py:206
  12.2 0.0 collective-permute-done.9.refs_2_
  12.2 0.0 collective-permute-start.12
  12.2 0.0 collective-permute-done.11.refs_4_
  12.2 0.5 %collective-permute-start.13 = (bf16[2,4,8192]{2,1,0:T(4,128)(2,1)S(1)}, bf16[2,4,8192]{2,1,0:T(4,128)(2,1)S(1)}, u32[]{:S(2)}, u32[]{:S(2)}) collective-permute-start(bf16[2,4,8192]{2,1,0:T(4,128)(2,1)S(1)} %collective-permute-done.9.refs_2_), channel_id=1, source_target_pairs={{0,1},{1,0},{2,3},{3,2},{4,5},{5,4},{6,7},{7,6},{8,9},{9,8},{10,11... | collective-permute-start | bytes 393224 | tf_op jit(solution)/shard_map/ppermute | solution.py:206
  12.7 1.0 %collective-permute-done.refs_0_ = bf16[2,4,8192]{2,1,0:T(4,128)(2,1)S(1)} collective-permute-done((bf16[2,4,8192]{2,1,0:T(4,128)(2,1)}, bf16[2,4,8192]{2,1,0:T(4,128)(2,1)S(1)}, u32[]{:S(2)}, u32[]{:S(2)}) %collective-permute-start) | collective-permute-done | bytes 131104 | tf_op jit(solution)/shard_map/ppermute | solution.py:206
  13.7 0.6 %collective-permute-start.2 = (bf16[2,4,8192]{2,1,0:T(4,128)(2,1)S(1)}, bf16[2,4,8192]{2,1,0:T(4,128)(2,1)S(1)}, u32[]{:S(2)}, u32[]{:S(2)}) collective-permute-start(bf16[2,4,8192]{2,1,0:T(4,128)(2,1)S(1)} %collective-permute-done.refs_0_), channel_id=1, source_target_pairs={{0,2},{1,3},{2,0},{3,1},{4,6},{5,7},{6,4},{7,5},{8,10},{9,11},{10,... | collective-permute-start | bytes 393224 | tf_op jit(solution)/shard_map/ppermute | solution.py:206
  14.3 6.4 %collective-permute-done.1.refs_1_ = bf16[2,4,8192]{2,1,0:T(4,128)(2,1)S(1)} collective-permute-done((bf16[2,4,8192]{2,1,0:T(4,128)(2,1)}, bf16[2,4,8192]{2,1,0:T(4,128)(2,1)S(1)}, u32[]{:S(2)}, u32[]{:S(2)}) %collective-permute-start.1) | collective-permute-done | bytes 131104 | tf_op jit(solution)/shard_map/ppermute | solution.py:206
  20.7 0.5 %collective-permute-start.3 = (bf16[2,4,8192]{2,1,0:T(4,128)(2,1)S(1)}, bf16[2,4,8192]{2,1,0:T(4,128)(2,1)S(1)}, u32[]{:S(2)}, u32[]{:S(2)}) collective-permute-start(bf16[2,4,8192]{2,1,0:T(4,128)(2,1)S(1)} %collective-permute-done.1.refs_1_), channel_id=1, source_target_pairs={{0,2},{1,3},{2,0},{3,1},{4,6},{5,7},{6,4},{7,5},{8,10},{9,11},{10,... | collective-permute-start | bytes 393224 | tf_op jit(solution)/shard_map/ppermute | solution.py:206
  21.2 0.0 collective-permute-done.10.refs_3_
  21.2 0.0 collective-permute-start.14
  21.2 0.0 collective-permute-done.12.refs_5_
  21.2 0.5 %collective-permute-start.4 = (bf16[2,4,8192]{2,1,0:T(4,128)(2,1)S(1)}, bf16[2,4,8192]{2,1,0:T(4,128)(2,1)S(1)}, u32[]{:S(2)}, u32[]{:S(2)}) collective-permute-start(bf16[2,4,8192]{2,1,0:T(4,128)(2,1)S(1)} %collective-permute-done.refs_0_), channel_id=1, source_target_pairs={{0,1},{1,0},{2,3},{3,2},{4,5},{5,4},{6,7},{7,6},{8,9},{9,8},{10,11... | collective-permute-start | bytes 393224 | tf_op jit(solution)/shard_map/ppermute | solution.py:206
  21.7 0.0 collective-permute-done.13.refs_6_
  21.7 0.1 collective-permute-start.5
  21.8 0.0 collective-permute-done.2.refs_2_
  21.8 0.4 %collective-permute-start.6 = (bf16[2,4,8192]{2,1,0:T(4,128)(2,1)S(1)}, bf16[2,4,8192]{2,1,0:T(4,128)(2,1)S(1)}, u32[]{:S(2)}, u32[]{:S(2)}) collective-permute-start(bf16[2,4,8192]{2,1,0:T(4,128)(2,1)S(1)} %collective-permute-done.2.refs_2_), channel_id=1, source_target_pairs={{0,1},{1,0},{2,3},{3,2},{4,5},{5,4},{6,7},{7,6},{8,9},{9,8},{10,11... | collective-permute-start | bytes 393224 | tf_op jit(solution)/shard_map/ppermute | solution.py:206
  22.2 3.8 %collective-permute-done.3.refs_3_ = bf16[2,4,8192]{2,1,0:T(4,128)(2,1)S(1)} collective-permute-done((bf16[2,4,8192]{2,1,0:T(4,128)(2,1)S(1)}, bf16[2,4,8192]{2,1,0:T(4,128)(2,1)S(1)}, u32[]{:S(2)}, u32[]{:S(2)}) %collective-permute-start.3) | collective-permute-done | bytes 131104 | tf_op jit(solution)/shard_map/ppermute | solution.py:206
  26.0 0.0 collective-permute-start.7
  26.0 0.0 collective-permute-done.14.refs_7_
  26.0 0.0 copy-done
  26.0 1.4 %map_rows.2.refs_13_ = f32[1,128]{1,0:T(1,128)S(1)} custom-call(bf16[2,4,8192]{2,1,0:T(4,128)(2,1)S(1)} %copy-done, bf16[2,4,8192]{2,1,0:T(4,128)(2,1)S(1)} %collective-permute-done.8.refs_1_, bf16[2,4,8192]{2,1,0:T(4,128)(2,1)S(1)} %collective-permute-done.9.refs_2_, bf16[2,4,8192]{2,1,0:T(4,128)(2,1)S(1)} %collective-permute-done.10.refs_3_, ...), custom_call_target="tpu_custom_call" | custom-call | flops 1073741824 | bytes 2097152 | tf_op jit(solution)/shard_map/map_rows/pallas_call | solution.py:147
  27.4 0.0 collective-permute-done.4.refs_4_
  27.4 0.0 collective-permute-done.5.refs_5_
  27.4 0.0 collective-permute-done.6.refs_6_
  27.4 0.0 collective-permute-done.7.refs_7_
  27.5 1.5 %map_rows.3 = (f32[1,128]{1,0:T(1,128)S(1)}, f32[1,128]{1,0:T(1,128)S(1)}) custom-call(bf16[2,4,8192]{2,1,0:T(4,128)(2,1)S(1)} %collective-permute-done.refs_0_, bf16[2,4,8192]{2,1,0:T(4,128)(2,1)S(1)} %collective-permute-done.1.refs_1_, bf16[2,4,8192]{2,1,0:T(4,128)(2,1)S(1)} %collective-permute-done.2.refs_2_, ...), custom_call_target="tpu_custom_call" | custom-call | flops 1073741824 | bytes 2097152 | tf_op jit(solution)/shard_map/map_rows/pallas_call | solution.py:147
  29.0 0.6 %collective-permute-start.15 = (f32[1,128]{1,0:T(1,128)S(1)}, f32[1,128]{1,0:T(1,128)S(1)}, u32[]{:S(2)}, u32[]{:S(2)}) collective-permute-start(f32[1,128]{1,0:T(1,128)S(1)} %get-tuple-element.22), channel_id=1, source_target_pairs={{0,1},{1,0},{2,3},{3,2},{4,5},{5,4},{6,7},{7,6},{8,9},{9,8},{10,11... | collective-permute-start | bytes 1544 | tf_op jit(solution)/shard_map/ppermute | solution.py:206
  29.5 0.8 %collective-permute-done.15.came = f32[1,128]{1,0:T(1,128)S(1)} collective-permute-done((f32[1,128]{1,0:T(1,128)S(1)}, f32[1,128]{1,0:T(1,128)S(1)}, u32[]{:S(2)}, u32[]{:S(2)}) %collective-permute-start.15) | collective-permute-done | bytes 544 | tf_op jit(solution)/shard_map/ppermute | solution.py:206
  30.3 0.1 fold.3
  30.4 0.5 %collective-permute-start.16 = (f32[1,64]{1,0:T(1,128)S(1)}, f32[1,64]{1,0:T(1,128)S(1)}, u32[]{:S(2)}, u32[]{:S(2)}) collective-permute-start(f32[1,64]{1,0:T(1,128)S(1)} %get-tuple-element.24), channel_id=1, source_target_pairs={{0,2},{1,3},{2,0},{3,1},{4,6},{5,7},{6,4},{7,5},{8,10},{9,11},{10,... | collective-permute-start | bytes 776 | tf_op jit(solution)/shard_map/ppermute | solution.py:206
  30.9 3.0 %collective-permute-done.16.came = f32[1,64]{1,0:T(1,128)S(1)} collective-permute-done((f32[1,64]{1,0:T(1,128)S(1)}, f32[1,64]{1,0:T(1,128)S(1)}, u32[]{:S(2)}, u32[]{:S(2)}) %collective-permute-start.16) | collective-permute-done | bytes 288 | tf_op jit(solution)/shard_map/ppermute | solution.py:206
  34.0 0.1 fold.4
  34.0 0.6 %collective-permute-start.17 = (f32[1,32]{1,0:T(1,128)S(1)}, f32[1,32]{1,0:T(1,128)S(1)}, u32[]{:S(2)}, u32[]{:S(2)}) collective-permute-start(f32[1,32]{1,0:T(1,128)S(1)} %get-tuple-element.26), channel_id=1, source_target_pairs={{0,4},{1,5},{2,6},{3,7},{4,0},{5,1},{6,2},{7,3},{8,12},{9,13},{10,... | collective-permute-start | bytes 392 | tf_op jit(solution)/shard_map/ppermute | solution.py:206
  34.6 3.0 %collective-permute-done.17.came = f32[1,32]{1,0:T(1,128)S(1)} collective-permute-done((f32[1,32]{1,0:T(1,128)S(1)}, f32[1,32]{1,0:T(1,128)S(1)}, u32[]{:S(2)}, u32[]{:S(2)}) %collective-permute-start.17) | collective-permute-done | bytes 160 | tf_op jit(solution)/shard_map/ppermute | solution.py:206
  37.6 0.1 fold.5
  37.6 1.6 %collective-permute-start.18 = (f32[1,16]{1,0:T(1,128)S(1)}, f32[1,16]{1,0:T(1,128)S(1)}, u32[]{:S(2)}, u32[]{:S(2)}) collective-permute-start(f32[1,16]{1,0:T(1,128)S(1)} %get-tuple-element.28), channel_id=1, source_target_pairs={{0,8},{1,9},{2,10},{3,11},{4,12},{5,13},{6,14},{7,15},{8,0},{9,1},... | collective-permute-start | bytes 200 | tf_op jit(solution)/shard_map/ppermute | solution.py:206
  39.2 2.9 %collective-permute-done.18.came = f32[1,16]{1,0:T(1,128)S(1)} collective-permute-done((f32[1,16]{1,0:T(1,128)S(1)}, f32[1,16]{1,0:T(1,128)S(1)}, u32[]{:S(2)}, u32[]{:S(2)}) %collective-permute-start.18) | collective-permute-done | bytes 96 | tf_op jit(solution)/shard_map/ppermute | solution.py:206
  42.1 0.6 %finish.1 = (f32[2,4]{1,0:T(2,128)}, f32[2,4]{1,0:T(2,128)}) custom-call(f32[1,16]{1,0:T(1,128)S(1)} %get-tuple-element.27.kept, f32[1,16]{1,0:T(1,128)S(1)} %collective-permute-done.18.came, f32[1,16]{1,0:T(1,128)S(1)} %get-tuple-element.29.own), custom_call_target="tpu_custom_call" | custom-call | tf_op jit(solution)/shard_map/finish/pallas_call | solution.py:190
  (3 shorter events, 0.0 us)
Async XLA Ops:
  0.6 25.3 %copy-start = (bf16[2,4,8192]{2,1,0:T(4,128)(2,1)S(1)}, bf16[2,4,8192]{2,1,0:T(4,128)(2,1)}, u32[]{:S(2)}) copy-start(bf16[2,4,8192]{2,1,0:T(4,128)(2,1)} %refs_0_.3) | copy-start | bytes 393220
  0.6 25.3 %copy-start.1 = (f32[2,512]{1,0:T(2,128)S(1)}, f32[2,512]{1,0:T(2,128)}, u32[]{:S(2)}) copy-start(f32[2,512]{1,0:T(2,128)} %refs_11_.3) | copy-start | bytes 12292
  0.7 25.3 %copy-start.2 = (f32[2,512]{1,0:T(2,128)S(1)}, f32[2,512]{1,0:T(2,128)}, u32[]{:S(2)}) copy-start(f32[2,512]{1,0:T(2,128)} %refs_12_.3) | copy-start | bytes 12292
  0.7 10.9 %collective-permute-start.8 = (bf16[2,4,8192]{2,1,0:T(4,128)(2,1)}, bf16[2,4,8192]{2,1,0:T(4,128)(2,1)S(1)}, u32[]{:S(2)}, u32[]{:S(2)}) collective-permute-start(bf16[2,4,8192]{2,1,0:T(4,128)(2,1)} %refs_0_.3), channel_id=1, source_target_pairs={{0,4},{1,5},{2,6},{3,7},{4,0},{5,1},{6,2},{7,3},{8,12},{9,13},{10,... | collective-permute-start | bytes 393224 | tf_op jit(solution)/shard_map/ppermute | solution.py:206
  3.8 8.4 %collective-permute-start.9 = (bf16[2,4,8192]{2,1,0:T(4,128)(2,1)}, bf16[2,4,8192]{2,1,0:T(4,128)(2,1)S(1)}, u32[]{:S(2)}, u32[]{:S(2)}) collective-permute-start(bf16[2,4,8192]{2,1,0:T(4,128)(2,1)} %refs_0_.3), channel_id=1, source_target_pairs={{0,2},{1,3},{2,0},{3,1},{4,6},{5,7},{6,4},{7,5},{8,10},{9,11},{10,... | collective-permute-start | bytes 393224 | tf_op jit(solution)/shard_map/ppermute | solution.py:206
  5.3 6.9 %collective-permute-start.11 = (bf16[2,4,8192]{2,1,0:T(4,128)(2,1)}, bf16[2,4,8192]{2,1,0:T(4,128)(2,1)S(1)}, u32[]{:S(2)}, u32[]{:S(2)}) collective-permute-start(bf16[2,4,8192]{2,1,0:T(4,128)(2,1)} %refs_0_.3), channel_id=1, source_target_pairs={{0,1},{1,0},{2,3},{3,2},{4,5},{5,4},{6,7},{7,6},{8,9},{9,8},{10,11... | collective-permute-start | bytes 393224 | tf_op jit(solution)/shard_map/ppermute | solution.py:206
  5.3 8.4 %collective-permute-start = (bf16[2,4,8192]{2,1,0:T(4,128)(2,1)}, bf16[2,4,8192]{2,1,0:T(4,128)(2,1)S(1)}, u32[]{:S(2)}, u32[]{:S(2)}) collective-permute-start(bf16[2,4,8192]{2,1,0:T(4,128)(2,1)} %refs_0_.3), channel_id=1, source_target_pairs={{0,12},{1,13},{2,14},{3,15},{4,8},{5,9},{6,10},{7,11},{8,4},{9,5},... | collective-permute-start | bytes 393224 | tf_op jit(solution)/shard_map/ppermute | solution.py:206
  7.8 12.9 %collective-permute-start.1 = (bf16[2,4,8192]{2,1,0:T(4,128)(2,1)}, bf16[2,4,8192]{2,1,0:T(4,128)(2,1)S(1)}, u32[]{:S(2)}, u32[]{:S(2)}) collective-permute-start(bf16[2,4,8192]{2,1,0:T(4,128)(2,1)} %refs_0_.3), channel_id=1, source_target_pairs={{0,8},{1,9},{2,10},{3,11},{4,12},{5,13},{6,14},{7,15},{8,0},{9,1},... | collective-permute-start | bytes 393224 | tf_op jit(solution)/shard_map/ppermute | solution.py:206
  11.6 9.6 %collective-permute-start.10 = (bf16[2,4,8192]{2,1,0:T(4,128)(2,1)S(1)}, bf16[2,4,8192]{2,1,0:T(4,128)(2,1)S(1)}, u32[]{:S(2)}, u32[]{:S(2)}) collective-permute-start(bf16[2,4,8192]{2,1,0:T(4,128)(2,1)S(1)} %collective-permute-done.8.refs_1_), channel_id=1, source_target_pairs={{0,2},{1,3},{2,0},{3,1},{4,6},{5,7},{6,4},{7,5},{8,10},{9,11},{10,... | collective-permute-start | bytes 393224 | tf_op jit(solution)/shard_map/ppermute | solution.py:206
  12.2 9.0 %collective-permute-start.12 = (bf16[2,4,8192]{2,1,0:T(4,128)(2,1)S(1)}, bf16[2,4,8192]{2,1,0:T(4,128)(2,1)S(1)}, u32[]{:S(2)}, u32[]{:S(2)}) collective-permute-start(bf16[2,4,8192]{2,1,0:T(4,128)(2,1)S(1)} %collective-permute-done.8.refs_1_), channel_id=1, source_target_pairs={{0,1},{1,0},{2,3},{3,2},{4,5},{5,4},{6,7},{7,6},{8,9},{9,8},{10,11... | collective-permute-start | bytes 393224 | tf_op jit(solution)/shard_map/ppermute | solution.py:206
  12.2 9.5 %collective-permute-start.13 = (bf16[2,4,8192]{2,1,0:T(4,128)(2,1)S(1)}, bf16[2,4,8192]{2,1,0:T(4,128)(2,1)S(1)}, u32[]{:S(2)}, u32[]{:S(2)}) collective-permute-start(bf16[2,4,8192]{2,1,0:T(4,128)(2,1)S(1)} %collective-permute-done.9.refs_2_), channel_id=1, source_target_pairs={{0,1},{1,0},{2,3},{3,2},{4,5},{5,4},{6,7},{7,6},{8,9},{9,8},{10,11... | collective-permute-start | bytes 393224 | tf_op jit(solution)/shard_map/ppermute | solution.py:206
  13.7 8.1 %collective-permute-start.2 = (bf16[2,4,8192]{2,1,0:T(4,128)(2,1)S(1)}, bf16[2,4,8192]{2,1,0:T(4,128)(2,1)S(1)}, u32[]{:S(2)}, u32[]{:S(2)}) collective-permute-start(bf16[2,4,8192]{2,1,0:T(4,128)(2,1)S(1)} %collective-permute-done.refs_0_), channel_id=1, source_target_pairs={{0,2},{1,3},{2,0},{3,1},{4,6},{5,7},{6,4},{7,5},{8,10},{9,11},{10,... | collective-permute-start | bytes 393224 | tf_op jit(solution)/shard_map/ppermute | solution.py:206
  20.7 5.3 %collective-permute-start.3 = (bf16[2,4,8192]{2,1,0:T(4,128)(2,1)S(1)}, bf16[2,4,8192]{2,1,0:T(4,128)(2,1)S(1)}, u32[]{:S(2)}, u32[]{:S(2)}) collective-permute-start(bf16[2,4,8192]{2,1,0:T(4,128)(2,1)S(1)} %collective-permute-done.1.refs_1_), channel_id=1, source_target_pairs={{0,2},{1,3},{2,0},{3,1},{4,6},{5,7},{6,4},{7,5},{8,10},{9,11},{10,... | collective-permute-start | bytes 393224 | tf_op jit(solution)/shard_map/ppermute | solution.py:206
  21.2 4.8 %collective-permute-start.14 = (bf16[2,4,8192]{2,1,0:T(4,128)(2,1)S(1)}, bf16[2,4,8192]{2,1,0:T(4,128)(2,1)S(1)}, u32[]{:S(2)}, u32[]{:S(2)}) collective-permute-start(bf16[2,4,8192]{2,1,0:T(4,128)(2,1)S(1)} %collective-permute-done.10.refs_3_), channel_id=1, source_target_pairs={{0,1},{1,0},{2,3},{3,2},{4,5},{5,4},{6,7},{7,6},{8,9},{9,8},{10,11... | collective-permute-start | bytes 393224 | tf_op jit(solution)/shard_map/ppermute | solution.py:206
  21.2 6.2 %collective-permute-start.4 = (bf16[2,4,8192]{2,1,0:T(4,128)(2,1)S(1)}, bf16[2,4,8192]{2,1,0:T(4,128)(2,1)S(1)}, u32[]{:S(2)}, u32[]{:S(2)}) collective-permute-start(bf16[2,4,8192]{2,1,0:T(4,128)(2,1)S(1)} %collective-permute-done.refs_0_), channel_id=1, source_target_pairs={{0,1},{1,0},{2,3},{3,2},{4,5},{5,4},{6,7},{7,6},{8,9},{9,8},{10,11... | collective-permute-start | bytes 393224 | tf_op jit(solution)/shard_map/ppermute | solution.py:206
  21.7 5.7 %collective-permute-start.5 = (bf16[2,4,8192]{2,1,0:T(4,128)(2,1)S(1)}, bf16[2,4,8192]{2,1,0:T(4,128)(2,1)S(1)}, u32[]{:S(2)}, u32[]{:S(2)}) collective-permute-start(bf16[2,4,8192]{2,1,0:T(4,128)(2,1)S(1)} %collective-permute-done.1.refs_1_), channel_id=1, source_target_pairs={{0,1},{1,0},{2,3},{3,2},{4,5},{5,4},{6,7},{7,6},{8,9},{9,8},{10,11... | collective-permute-start | bytes 393224 | tf_op jit(solution)/shard_map/ppermute | solution.py:206
  21.8 5.7 %collective-permute-start.6 = (bf16[2,4,8192]{2,1,0:T(4,128)(2,1)S(1)}, bf16[2,4,8192]{2,1,0:T(4,128)(2,1)S(1)}, u32[]{:S(2)}, u32[]{:S(2)}) collective-permute-start(bf16[2,4,8192]{2,1,0:T(4,128)(2,1)S(1)} %collective-permute-done.2.refs_2_), channel_id=1, source_target_pairs={{0,1},{1,0},{2,3},{3,2},{4,5},{5,4},{6,7},{7,6},{8,9},{9,8},{10,11... | collective-permute-start | bytes 393224 | tf_op jit(solution)/shard_map/ppermute | solution.py:206
  26.0 1.5 %collective-permute-start.7 = (bf16[2,4,8192]{2,1,0:T(4,128)(2,1)S(1)}, bf16[2,4,8192]{2,1,0:T(4,128)(2,1)S(1)}, u32[]{:S(2)}, u32[]{:S(2)}) collective-permute-start(bf16[2,4,8192]{2,1,0:T(4,128)(2,1)S(1)} %collective-permute-done.3.refs_3_), channel_id=1, source_target_pairs={{0,1},{1,0},{2,3},{3,2},{4,5},{5,4},{6,7},{7,6},{8,9},{9,8},{10,11... | collective-permute-start | bytes 393224 | tf_op jit(solution)/shard_map/ppermute | solution.py:206
  29.0 1.4 %collective-permute-start.15 = (f32[1,128]{1,0:T(1,128)S(1)}, f32[1,128]{1,0:T(1,128)S(1)}, u32[]{:S(2)}, u32[]{:S(2)}) collective-permute-start(f32[1,128]{1,0:T(1,128)S(1)} %get-tuple-element.22), channel_id=1, source_target_pairs={{0,1},{1,0},{2,3},{3,2},{4,5},{5,4},{6,7},{7,6},{8,9},{9,8},{10,11... | collective-permute-start | bytes 1544 | tf_op jit(solution)/shard_map/ppermute | solution.py:206
  30.4 3.5 %collective-permute-start.16 = (f32[1,64]{1,0:T(1,128)S(1)}, f32[1,64]{1,0:T(1,128)S(1)}, u32[]{:S(2)}, u32[]{:S(2)}) collective-permute-start(f32[1,64]{1,0:T(1,128)S(1)} %get-tuple-element.24), channel_id=1, source_target_pairs={{0,2},{1,3},{2,0},{3,1},{4,6},{5,7},{6,4},{7,5},{8,10},{9,11},{10,... | collective-permute-start | bytes 776 | tf_op jit(solution)/shard_map/ppermute | solution.py:206
  34.0 3.5 %collective-permute-start.17 = (f32[1,32]{1,0:T(1,128)S(1)}, f32[1,32]{1,0:T(1,128)S(1)}, u32[]{:S(2)}, u32[]{:S(2)}) collective-permute-start(f32[1,32]{1,0:T(1,128)S(1)} %get-tuple-element.26), channel_id=1, source_target_pairs={{0,4},{1,5},{2,6},{3,7},{4,0},{5,1},{6,2},{7,3},{8,12},{9,13},{10,... | collective-permute-start | bytes 392 | tf_op jit(solution)/shard_map/ppermute | solution.py:206
  37.6 4.4 %collective-permute-start.18 = (f32[1,16]{1,0:T(1,128)S(1)}, f32[1,16]{1,0:T(1,128)S(1)}, u32[]{:S(2)}, u32[]{:S(2)}) collective-permute-start(f32[1,16]{1,0:T(1,128)S(1)} %get-tuple-element.28), channel_id=1, source_target_pairs={{0,8},{1,9},{2,10},{3,11},{4,12},{5,13},{6,14},{7,15},{8,0},{9,1},... | collective-permute-start | bytes 200 | tf_op jit(solution)/shard_map/ppermute | solution.py:206

commit v4 on v3

--- a/solution.py
+++ b/solution.py
@@ -209,23 +209,31 @@
         bound_coeff, status, slope_bit, pre_lower, pre_upper, layer_bias.reshape(1, neurons), weight
     )
 
+    bits = num_devices.bit_length() - 1
+    far = sorted(range(4, num_devices, 4), key=lambda m: (m.bit_count(), -m))
+    direct = [m for m in far if m.bit_count() == 1]
+    relayed = [m for m in far if m not in direct]
     pieces = {0: bound_coeff}
-    for mask in range(4, num_devices, 4):
+    for mask in (*direct, 2):
         pieces[mask] = swap(bound_coeff, mask)
-    pieces[4], held = lax.optimization_barrier((pieces[4], held))
-    for mask in range(0, num_devices, 4):
+    args = (inner, outer, held, center_input, radius)
+    pieces[direct[0]], args = lax.optimization_barrier((pieces[direct[0]], args))
+    for mask in relayed:
+        low = mask & -mask
+        pieces[mask] = swap(pieces[mask ^ low], low)
+    for mask in direct[:-1]:
         pieces[mask + 2] = swap(pieces[mask], 2)
-    args = (inner, outer, held, center_input, radius)
-    early = [0, 4, 2, 6, 1, 5, 3, 7]
-    late = sorted(set(range(num_devices)) - set(early), key=lambda m: (m & 1, m & 2, -m))
-    for mask in (0, 4, 2, 6):
+    pieces[6] = swap(pieces[2], 4)
+    early = [0, *direct, 2]
+    first = map_rows([pieces[m] for m in early], args)
+    pieces[relayed[-1]], first = lax.optimization_barrier((pieces[relayed[-1]], first))
+    for mask in relayed:
+        pieces[mask + 2] = swap(pieces[mask], 2)
+    others = [*relayed, *[m + 2 for m in direct[:-1]], 6, *[m + 2 for m in relayed]]
+    for mask in (*early, *others):
         pieces[mask + 1] = swap(pieces[mask], 1)
-    first = map_rows([pieces[m] for m in early], args)
-    for mask in late:
-        if mask & 1 == 0:
-            pieces[mask + 1] = swap(pieces[mask], 1)
-
-    bits = num_devices.bit_length() - 1
+    late = [*others, *[m + 1 for m in early], *[m + 1 for m in others]]
+
     sent = [int(format(i, "b").zfill(bits)[::-1], 2) for i in range(num_devices)]
     order = [(0, early.index(m)) if m in early else (1, late.index(m)) for m in sent]
     keep, send = map_rows([pieces[m] for m in late], args, first, order)

time: 42.9 us -> 40 us (0.932)
  waiting for transfers between devices: 20.9 us -> 12.7 us
  starting transfers between devices: 13.6 us -> 18.1 us
  Pallas kernels: 7.45 us -> 8.28 us
    ppermute x19, waiting for transfers between devices: 20.9 us -> 12.7 us  [swap(): lax.ppermute(array, 'row', [(i, i ^ mask) for i in range(num_devices)])]
    ppermute x19, starting transfers between devices: 13.6 us -> 18.1 us  [swap(): lax.ppermute(array, 'row', [(i, i ^ mask) for i in range(num_devices)])]
    pallas_call x2, Pallas kernels: 2.9 us -> 3.73 us  [map_rows(): pl.pallas_call(kernel, in_specs=[VMEM] * (len(pieces) + len(args) + len(m...]
  transfers between devices with their start and end apart: 19 -> 19, of which waited for: 7 -> 7; matrix products, arithmetic and copies ran while one was open for 0% -> 0% of each run, Pallas kernels for 12% -> 14%
where the time goes in v4:
time: 40 us; the launch traced here: 39.8 us
  starting transfers between devices  18.1 us (45%)
  waiting for transfers between devices  12.7 us (32%)
  Pallas kernels  8.28 us (21%)
  between operations  0.74 us (2%)
    ppermute x19, starting transfers between devices, swap(): lax.ppermute(array, 'row', [(i, i ^ mask) for i in range(num_devices)])  18.1 us
    ppermute x19, waiting for transfers between devices, swap(): lax.ppermute(array, 'row', [(i, i ^ mask) for i in range(num_devices)])  12.7 us
    pallas_call x2, Pallas kernels, map_rows(): pl.pallas_call(kernel, in_specs=[VMEM] * (len(pieces) + len(args) + len(m...  3.73 us
    pallas_call x1, Pallas kernels, prep(): pl.pallas_call(prep_kernel, in_specs=[pl.BlockSpec(memory_space=pltpu.HBM...  3.7 us
  transfers between devices with their start and end apart: 19, of which 7 were waited for; matrix products, arithmetic and copies ran while one was open for 0% of the time, Pallas kernels for 14%

profile of v4, /device:TPU:0, one launch (start us, length us, event | category | flops | bytes accessed | tf_op | source)
XLA Modules:
  0.0 39.8 jit_solution(1279162812506438227)
XLA Ops:
  0.6 0.0 copy-start
  0.6 0.0 copy-start.2
  0.7 4.1 %collective-permute-start = (bf16[2,4,8192]{2,1,0:T(4,128)(2,1)}, bf16[2,4,8192]{2,1,0:T(4,128)(2,1)S(1)}, u32[]{:S(2)}, u32[]{:S(2)}) collective-permute-start(bf16[2,4,8192]{2,1,0:T(4,128)(2,1)} %refs_0_.3), channel_id=1, source_target_pairs={{0,8},{1,9},{2,10},{3,11},{4,12},{5,13},{6,14},{7,15},{8,0},{9,1},... | collective-permute-start | bytes 393224 | tf_op jit(solution)/shard_map/ppermute | solution.py:206
  4.8 1.5 %collective-permute-start.3 = (bf16[2,4,8192]{2,1,0:T(4,128)(2,1)}, bf16[2,4,8192]{2,1,0:T(4,128)(2,1)S(1)}, u32[]{:S(2)}, u32[]{:S(2)}) collective-permute-start(bf16[2,4,8192]{2,1,0:T(4,128)(2,1)} %refs_0_.3), channel_id=1, source_target_pairs={{0,2},{1,3},{2,0},{3,1},{4,6},{5,7},{6,4},{7,5},{8,10},{9,11},{10,... | collective-permute-start | bytes 393224 | tf_op jit(solution)/shard_map/ppermute | solution.py:206
  6.3 1.6 %collective-permute-start.2 = (bf16[2,4,8192]{2,1,0:T(4,128)(2,1)}, bf16[2,4,8192]{2,1,0:T(4,128)(2,1)S(1)}, u32[]{:S(2)}, u32[]{:S(2)}) collective-permute-start(bf16[2,4,8192]{2,1,0:T(4,128)(2,1)} %refs_0_.3), channel_id=1, source_target_pairs={{0,4},{1,5},{2,6},{3,7},{4,0},{5,1},{6,2},{7,3},{8,12},{9,13},{10,... | collective-permute-start | bytes 393224 | tf_op jit(solution)/shard_map/ppermute | solution.py:206
  7.9 3.7 %prep.1 = (f32[8,8192]{1,0:T(8,128)S(1)}, f32[8,8192]{1,0:T(8,128)S(1)}, f32[1,16]{1,0:T(1,128)S(1)}, bf16[8192,512]{1,0:T(8,128)(2,1)S(1)}) custom-call(bf16[2,4,8192]{2,1,0:T(4,128)(2,1)} %refs_0_.3, s32[2,8192]{1,0:T(2,128)} %refs_1_.1, s32[2,8192]{1,0:T(2,128)} %refs_2_.1, f32[2,8192]{1,0:T(2,128)} %refs_3_.1, f32[2,8192]{1,0:T(2,128)} %refs_4_.1, ...), custom_call_target="tpu_custom_call" | custom-call | flops 1310720 | bytes 9175040 | tf_op jit(solution)/shard_map/prep/pallas_call | solution.py:71
  11.6 0.0 collective-permute-done.refs_1_
  11.6 0.6 %collective-permute-start.1 = (bf16[2,4,8192]{2,1,0:T(4,128)(2,1)S(1)}, bf16[2,4,8192]{2,1,0:T(4,128)(2,1)S(1)}, u32[]{:S(2)}, u32[]{:S(2)}) collective-permute-start(bf16[2,4,8192]{2,1,0:T(4,128)(2,1)S(1)} %collective-permute-done.refs_1_), channel_id=1, source_target_pairs={{0,4},{1,5},{2,6},{3,7},{4,0},{5,1},{6,2},{7,3},{8,12},{9,13},{10,... | collective-permute-start | bytes 393224 | tf_op jit(solution)/shard_map/ppermute | solution.py:206
  12.2 0.0 collective-permute-start.7
  12.2 1.5 %collective-permute-start.4 = (bf16[2,4,8192]{2,1,0:T(4,128)(2,1)S(1)}, bf16[2,4,8192]{2,1,0:T(4,128)(2,1)S(1)}, u32[]{:S(2)}, u32[]{:S(2)}) collective-permute-start(bf16[2,4,8192]{2,1,0:T(4,128)(2,1)S(1)} %collective-permute-done.refs_1_), channel_id=1, source_target_pairs={{0,2},{1,3},{2,0},{3,1},{4,6},{5,7},{6,4},{7,5},{8,10},{9,11},{10,... | collective-permute-start | bytes 393224 | tf_op jit(solution)/shard_map/ppermute | solution.py:206
  13.6 0.0 collective-permute-done.3.refs_3_
  13.6 0.2 collective-permute-start.10
  13.9 0.0 collective-permute-done.2.refs_2_
  13.9 1.4 %collective-permute-start.5 = (bf16[2,4,8192]{2,1,0:T(4,128)(2,1)S(1)}, bf16[2,4,8192]{2,1,0:T(4,128)(2,1)S(1)}, u32[]{:S(2)}, u32[]{:S(2)}) collective-permute-start(bf16[2,4,8192]{2,1,0:T(4,128)(2,1)S(1)} %collective-permute-done.3.refs_3_), channel_id=1, source_target_pairs={{0,4},{1,5},{2,6},{3,7},{4,0},{5,1},{6,2},{7,3},{8,12},{9,13},{10,... | collective-permute-start | bytes 393224 | tf_op jit(solution)/shard_map/ppermute | solution.py:206
  15.2 0.0 copy-done.1
  15.2 1.7 %map_rows.2.refs_17_ = f32[1,64]{1,0:T(1,128)S(1)} custom-call(bf16[2,4,8192]{2,1,0:T(4,128)(2,1)S(1)} %copy-done, bf16[2,4,8192]{2,1,0:T(4,128)(2,1)S(1)} %collective-permute-done.refs_1_, bf16[2,4,8192]{2,1,0:T(4,128)(2,1)S(1)} %collective-permute-done.2.refs_2_, bf16[2,4,8192]{2,1,0:T(4,128)(2,1)S(1)} %collective-permute-done.3.refs_3_, ...), custom_call_target="tpu_custom_call" | custom-call | flops 536870912 | bytes 1048576 | tf_op jit(solution)/shard_map/map_rows/pallas_call | solution.py:147
  16.9 0.0 collective-permute-done.1.refs_0_
  17.0 0.1 collective-permute-start.9
  17.0 0.0 collective-permute-done.7.refs_4_
  17.0 1.5 %collective-permute-start.6 = (bf16[2,4,8192]{2,1,0:T(4,128)(2,1)S(1)}, bf16[2,4,8192]{2,1,0:T(4,128)(2,1)S(1)}, u32[]{:S(2)}, u32[]{:S(2)}) collective-permute-start(bf16[2,4,8192]{2,1,0:T(4,128)(2,1)S(1)} %collective-permute-done.1.refs_0_), channel_id=1, source_target_pairs={{0,2},{1,3},{2,0},{3,1},{4,6},{5,7},{6,4},{7,5},{8,10},{9,11},{10,... | collective-permute-start | bytes 393224 | tf_op jit(solution)/shard_map/ppermute | solution.py:206
  18.6 0.0 collective-permute-done.10.refs_7_
  18.6 0.2 collective-permute-start.8
  18.8 0.7 %collective-permute-done.5.refs_2_ = bf16[2,4,8192]{2,1,0:T(4,128)(2,1)S(1)} collective-permute-done((bf16[2,4,8192]{2,1,0:T(4,128)(2,1)S(1)}, bf16[2,4,8192]{2,1,0:T(4,128)(2,1)S(1)}, u32[]{:S(2)}, u32[]{:S(2)}) %collective-permute-start.5) | collective-permute-done | bytes 131104 | tf_op jit(solution)/shard_map/ppermute | solution.py:206
  19.6 0.0 collective-permute-start.11
  19.6 0.0 collective-permute-done.9.refs_6_
  19.6 0.5 %collective-permute-start.13 = (bf16[2,4,8192]{2,1,0:T(4,128)(2,1)S(1)}, bf16[2,4,8192]{2,1,0:T(4,128)(2,1)S(1)}, u32[]{:S(2)}, u32[]{:S(2)}) collective-permute-start(bf16[2,4,8192]{2,1,0:T(4,128)(2,1)S(1)} %collective-permute-done.5.refs_2_), channel_id=1, source_target_pairs={{0,1},{1,0},{2,3},{3,2},{4,5},{5,4},{6,7},{7,6},{8,9},{9,8},{10,11... | collective-permute-start | bytes 393224 | tf_op jit(solution)/shard_map/ppermute | solution.py:206
  20.1 0.0 collective-permute-done.4.refs_1_
  20.1 0.1 collective-permute-start.12
  20.1 2.8 %collective-permute-done.6.refs_3_ = bf16[2,4,8192]{2,1,0:T(4,128)(2,1)S(1)} collective-permute-done((bf16[2,4,8192]{2,1,0:T(4,128)(2,1)S(1)}, bf16[2,4,8192]{2,1,0:T(4,128)(2,1)S(1)}, u32[]{:S(2)}, u32[]{:S(2)}) %collective-permute-start.6) | collective-permute-done | bytes 131104 | tf_op jit(solution)/shard_map/ppermute | solution.py:206
  23.0 0.0 collective-permute-start.14
  23.0 0.0 collective-permute-done.8.refs_5_
  23.0 0.0 collective-permute-done.13.refs_10_
  23.0 0.0 collective-permute-done.12.refs_9_
  23.0 0.0 collective-permute-done.11.refs_8_
  23.0 1.3 %collective-permute-done.14.refs_11_ = bf16[2,4,8192]{2,1,0:T(4,128)(2,1)S(1)} collective-permute-done((bf16[2,4,8192]{2,1,0:T(4,128)(2,1)S(1)}, bf16[2,4,8192]{2,1,0:T(4,128)(2,1)S(1)}, u32[]{:S(2)}, u32[]{:S(2)}) %collective-permute-start.14) | collective-permute-done | bytes 131104 | tf_op jit(solution)/shard_map/ppermute | solution.py:206
  24.3 2.0 %map_rows.3 = (f32[1,128]{1,0:T(1,128)S(1)}, f32[1,128]{1,0:T(1,128)S(1)}) custom-call(bf16[2,4,8192]{2,1,0:T(4,128)(2,1)S(1)} %collective-permute-done.1.refs_0_, bf16[2,4,8192]{2,1,0:T(4,128)(2,1)S(1)} %collective-permute-done.4.refs_1_, bf16[2,4,8192]{2,1,0:T(4,128)(2,1)S(1)} %collective-permute-done.5.refs_2_, ...), custom_call_target="tpu_custom_call" | custom-call | flops 1610612736 | bytes 3145728 | tf_op jit(solution)/shard_map/map_rows/pallas_call | solution.py:147
  26.3 0.2 collective-permute-start.15
  26.5 1.0 %collective-permute-done.15.came = f32[1,128]{1,0:T(1,128)S(1)} collective-permute-done((f32[1,128]{1,0:T(1,128)S(1)}, f32[1,128]{1,0:T(1,128)S(1)}, u32[]{:S(2)}, u32[]{:S(2)}) %collective-permute-start.15) | collective-permute-done | bytes 544 | tf_op jit(solution)/shard_map/ppermute | solution.py:206
  27.4 0.1 fold.3
  27.5 1.5 %collective-permute-start.16 = (f32[1,64]{1,0:T(1,128)S(1)}, f32[1,64]{1,0:T(1,128)S(1)}, u32[]{:S(2)}, u32[]{:S(2)}) collective-permute-start(f32[1,64]{1,0:T(1,128)S(1)} %get-tuple-element.36), channel_id=1, source_target_pairs={{0,2},{1,3},{2,0},{3,1},{4,6},{5,7},{6,4},{7,5},{8,10},{9,11},{10,... | collective-permute-start | bytes 776 | tf_op jit(solution)/shard_map/ppermute | solution.py:206
  29.1 2.0 %collective-permute-done.16.came = f32[1,64]{1,0:T(1,128)S(1)} collective-permute-done((f32[1,64]{1,0:T(1,128)S(1)}, f32[1,64]{1,0:T(1,128)S(1)}, u32[]{:S(2)}, u32[]{:S(2)}) %collective-permute-start.16) | collective-permute-done | bytes 288 | tf_op jit(solution)/shard_map/ppermute | solution.py:206
  31.1 0.1 fold.4
  31.1 0.7 %collective-permute-start.17 = (f32[1,32]{1,0:T(1,128)S(1)}, f32[1,32]{1,0:T(1,128)S(1)}, u32[]{:S(2)}, u32[]{:S(2)}) collective-permute-start(f32[1,32]{1,0:T(1,128)S(1)} %get-tuple-element.38), channel_id=1, source_target_pairs={{0,4},{1,5},{2,6},{3,7},{4,0},{5,1},{6,2},{7,3},{8,12},{9,13},{10,... | collective-permute-start | bytes 392 | tf_op jit(solution)/shard_map/ppermute | solution.py:206
  31.8 2.9 %collective-permute-done.17.came = f32[1,32]{1,0:T(1,128)S(1)} collective-permute-done((f32[1,32]{1,0:T(1,128)S(1)}, f32[1,32]{1,0:T(1,128)S(1)}, u32[]{:S(2)}, u32[]{:S(2)}) %collective-permute-start.17) | collective-permute-done | bytes 160 | tf_op jit(solution)/shard_map/ppermute | solution.py:206
  34.7 0.1 fold.5
  34.7 2.5 %collective-permute-start.18 = (f32[1,16]{1,0:T(1,128)S(1)}, f32[1,16]{1,0:T(1,128)S(1)}, u32[]{:S(2)}, u32[]{:S(2)}) collective-permute-start(f32[1,16]{1,0:T(1,128)S(1)} %get-tuple-element.40), channel_id=1, source_target_pairs={{0,8},{1,9},{2,10},{3,11},{4,12},{5,13},{6,14},{7,15},{8,0},{9,1},... | collective-permute-start | bytes 200 | tf_op jit(solution)/shard_map/ppermute | solution.py:206
  37.2 2.0 %collective-permute-done.18.came = f32[1,16]{1,0:T(1,128)S(1)} collective-permute-done((f32[1,16]{1,0:T(1,128)S(1)}, f32[1,16]{1,0:T(1,128)S(1)}, u32[]{:S(2)}, u32[]{:S(2)}) %collective-permute-start.18) | collective-permute-done | bytes 96 | tf_op jit(solution)/shard_map/ppermute | solution.py:206
  39.2 0.6 %finish.1 = (f32[2,4]{1,0:T(2,128)}, f32[2,4]{1,0:T(2,128)}) custom-call(f32[1,16]{1,0:T(1,128)S(1)} %get-tuple-element.39.kept, f32[1,16]{1,0:T(1,128)S(1)} %collective-permute-done.18.came, f32[1,16]{1,0:T(1,128)S(1)} %get-tuple-element.41.own), custom_call_target="tpu_custom_call" | custom-call | tf_op jit(solution)/shard_map/finish/pallas_call | solution.py:190
  (3 shorter events, 0.0 us)
Async XLA Ops:
  0.6 11.5 %copy-start = (bf16[2,4,8192]{2,1,0:T(4,128)(2,1)S(1)}, bf16[2,4,8192]{2,1,0:T(4,128)(2,1)}, u32[]{:S(2)}) copy-start(bf16[2,4,8192]{2,1,0:T(4,128)(2,1)} %refs_0_.3) | copy-start | bytes 393220
  0.6 14.6 %copy-start.2 = (f32[2,512]{1,0:T(2,128)S(1)}, f32[2,512]{1,0:T(2,128)}, u32[]{:S(2)}) copy-start(f32[2,512]{1,0:T(2,128)} %refs_16_) | copy-start | bytes 12292
  0.7 14.6 %copy-start.1 = (f32[2,512]{1,0:T(2,128)S(1)}, f32[2,512]{1,0:T(2,128)}, u32[]{:S(2)}) copy-start(f32[2,512]{1,0:T(2,128)} %refs_15_) | copy-start | bytes 12292
  0.7 10.9 %collective-permute-start = (bf16[2,4,8192]{2,1,0:T(4,128)(2,1)}, bf16[2,4,8192]{2,1,0:T(4,128)(2,1)S(1)}, u32[]{:S(2)}, u32[]{:S(2)}) collective-permute-start(bf16[2,4,8192]{2,1,0:T(4,128)(2,1)} %refs_0_.3), channel_id=1, source_target_pairs={{0,8},{1,9},{2,10},{3,11},{4,12},{5,13},{6,14},{7,15},{8,0},{9,1},... | collective-permute-start | bytes 393224 | tf_op jit(solution)/shard_map/ppermute | solution.py:206
  4.8 8.9 %collective-permute-start.3 = (bf16[2,4,8192]{2,1,0:T(4,128)(2,1)}, bf16[2,4,8192]{2,1,0:T(4,128)(2,1)S(1)}, u32[]{:S(2)}, u32[]{:S(2)}) collective-permute-start(bf16[2,4,8192]{2,1,0:T(4,128)(2,1)} %refs_0_.3), channel_id=1, source_target_pairs={{0,2},{1,3},{2,0},{3,1},{4,6},{5,7},{6,4},{7,5},{8,10},{9,11},{10,... | collective-permute-start | bytes 393224 | tf_op jit(solution)/shard_map/ppermute | solution.py:206
  6.3 7.6 %collective-permute-start.2 = (bf16[2,4,8192]{2,1,0:T(4,128)(2,1)}, bf16[2,4,8192]{2,1,0:T(4,128)(2,1)S(1)}, u32[]{:S(2)}, u32[]{:S(2)}) collective-permute-start(bf16[2,4,8192]{2,1,0:T(4,128)(2,1)} %refs_0_.3), channel_id=1, source_target_pairs={{0,4},{1,5},{2,6},{3,7},{4,0},{5,1},{6,2},{7,3},{8,12},{9,13},{10,... | collective-permute-start | bytes 393224 | tf_op jit(solution)/shard_map/ppermute | solution.py:206
  11.6 5.4 %collective-permute-start.1 = (bf16[2,4,8192]{2,1,0:T(4,128)(2,1)S(1)}, bf16[2,4,8192]{2,1,0:T(4,128)(2,1)S(1)}, u32[]{:S(2)}, u32[]{:S(2)}) collective-permute-start(bf16[2,4,8192]{2,1,0:T(4,128)(2,1)S(1)} %collective-permute-done.refs_1_), channel_id=1, source_target_pairs={{0,4},{1,5},{2,6},{3,7},{4,0},{5,1},{6,2},{7,3},{8,12},{9,13},{10,... | collective-permute-start | bytes 393224 | tf_op jit(solution)/shard_map/ppermute | solution.py:206
  12.2 4.9 %collective-permute-start.7 = (bf16[2,4,8192]{2,1,0:T(4,128)(2,1)S(1)}, bf16[2,4,8192]{2,1,0:T(4,128)(2,1)S(1)}, u32[]{:S(2)}, u32[]{:S(2)}) collective-permute-start(bf16[2,4,8192]{2,1,0:T(4,128)(2,1)S(1)} %copy-done), channel_id=1, source_target_pairs={{0,1},{1,0},{2,3},{3,2},{4,5},{5,4},{6,7},{7,6},{8,9},{9,8},{10,11... | collective-permute-start | bytes 393224 | tf_op jit(solution)/shard_map/ppermute | solution.py:206
  12.2 7.9 %collective-permute-start.4 = (bf16[2,4,8192]{2,1,0:T(4,128)(2,1)S(1)}, bf16[2,4,8192]{2,1,0:T(4,128)(2,1)S(1)}, u32[]{:S(2)}, u32[]{:S(2)}) collective-permute-start(bf16[2,4,8192]{2,1,0:T(4,128)(2,1)S(1)} %collective-permute-done.refs_1_), channel_id=1, source_target_pairs={{0,2},{1,3},{2,0},{3,1},{4,6},{5,7},{6,4},{7,5},{8,10},{9,11},{10,... | collective-permute-start | bytes 393224 | tf_op jit(solution)/shard_map/ppermute | solution.py:206
  13.6 5.0 %collective-permute-start.10 = (bf16[2,4,8192]{2,1,0:T(4,128)(2,1)S(1)}, bf16[2,4,8192]{2,1,0:T(4,128)(2,1)S(1)}, u32[]{:S(2)}, u32[]{:S(2)}) collective-permute-start(bf16[2,4,8192]{2,1,0:T(4,128)(2,1)S(1)} %collective-permute-done.3.refs_3_), channel_id=1, source_target_pairs={{0,1},{1,0},{2,3},{3,2},{4,5},{5,4},{6,7},{7,6},{8,9},{9,8},{10,11... | collective-permute-start | bytes 393224 | tf_op jit(solution)/shard_map/ppermute | solution.py:206
  13.9 5.7 %collective-permute-start.5 = (bf16[2,4,8192]{2,1,0:T(4,128)(2,1)S(1)}, bf16[2,4,8192]{2,1,0:T(4,128)(2,1)S(1)}, u32[]{:S(2)}, u32[]{:S(2)}) collective-permute-start(bf16[2,4,8192]{2,1,0:T(4,128)(2,1)S(1)} %collective-permute-done.3.refs_3_), channel_id=1, source_target_pairs={{0,4},{1,5},{2,6},{3,7},{4,0},{5,1},{6,2},{7,3},{8,12},{9,13},{10,... | collective-permute-start | bytes 393224 | tf_op jit(solution)/shard_map/ppermute | solution.py:206
  17.0 2.6 %collective-permute-start.9 = (bf16[2,4,8192]{2,1,0:T(4,128)(2,1)S(1)}, bf16[2,4,8192]{2,1,0:T(4,128)(2,1)S(1)}, u32[]{:S(2)}, u32[]{:S(2)}) collective-permute-start(bf16[2,4,8192]{2,1,0:T(4,128)(2,1)S(1)} %collective-permute-done.2.refs_2_), channel_id=1, source_target_pairs={{0,1},{1,0},{2,3},{3,2},{4,5},{5,4},{6,7},{7,6},{8,9},{9,8},{10,11... | collective-permute-start | bytes 393224 | tf_op jit(solution)/shard_map/ppermute | solution.py:206
  17.0 5.9 %collective-permute-start.6 = (bf16[2,4,8192]{2,1,0:T(4,128)(2,1)S(1)}, bf16[2,4,8192]{2,1,0:T(4,128)(2,1)S(1)}, u32[]{:S(2)}, u32[]{:S(2)}) collective-permute-start(bf16[2,4,8192]{2,1,0:T(4,128)(2,1)S(1)} %collective-permute-done.1.refs_0_), channel_id=1, source_target_pairs={{0,2},{1,3},{2,0},{3,1},{4,6},{5,7},{6,4},{7,5},{8,10},{9,11},{10,... | collective-permute-start | bytes 393224 | tf_op jit(solution)/shard_map/ppermute | solution.py:206
  18.6 4.4 %collective-permute-start.8 = (bf16[2,4,8192]{2,1,0:T(4,128)(2,1)S(1)}, bf16[2,4,8192]{2,1,0:T(4,128)(2,1)S(1)}, u32[]{:S(2)}, u32[]{:S(2)}) collective-permute-start(bf16[2,4,8192]{2,1,0:T(4,128)(2,1)S(1)} %collective-permute-done.refs_1_), channel_id=1, source_target_pairs={{0,1},{1,0},{2,3},{3,2},{4,5},{5,4},{6,7},{7,6},{8,9},{9,8},{10,11... | collective-permute-start | bytes 393224 | tf_op jit(solution)/shard_map/ppermute | solution.py:206
  19.6 3.4 %collective-permute-start.11 = (bf16[2,4,8192]{2,1,0:T(4,128)(2,1)S(1)}, bf16[2,4,8192]{2,1,0:T(4,128)(2,1)S(1)}, u32[]{:S(2)}, u32[]{:S(2)}) collective-permute-start(bf16[2,4,8192]{2,1,0:T(4,128)(2,1)S(1)} %collective-permute-done.1.refs_0_), channel_id=1, source_target_pairs={{0,1},{1,0},{2,3},{3,2},{4,5},{5,4},{6,7},{7,6},{8,9},{9,8},{10,11... | collective-permute-start | bytes 393224 | tf_op jit(solution)/shard_map/ppermute | solution.py:206
  19.6 3.4 %collective-permute-start.13 = (bf16[2,4,8192]{2,1,0:T(4,128)(2,1)S(1)}, bf16[2,4,8192]{2,1,0:T(4,128)(2,1)S(1)}, u32[]{:S(2)}, u32[]{:S(2)}) collective-permute-start(bf16[2,4,8192]{2,1,0:T(4,128)(2,1)S(1)} %collective-permute-done.5.refs_2_), channel_id=1, source_target_pairs={{0,1},{1,0},{2,3},{3,2},{4,5},{5,4},{6,7},{7,6},{8,9},{9,8},{10,11... | collective-permute-start | bytes 393224 | tf_op jit(solution)/shard_map/ppermute | solution.py:206
  20.1 2.9 %collective-permute-start.12 = (bf16[2,4,8192]{2,1,0:T(4,128)(2,1)S(1)}, bf16[2,4,8192]{2,1,0:T(4,128)(2,1)S(1)}, u32[]{:S(2)}, u32[]{:S(2)}) collective-permute-start(bf16[2,4,8192]{2,1,0:T(4,128)(2,1)S(1)} %collective-permute-done.4.refs_1_), channel_id=1, source_target_pairs={{0,1},{1,0},{2,3},{3,2},{4,5},{5,4},{6,7},{7,6},{8,9},{9,8},{10,11... | collective-permute-start | bytes 393224 | tf_op jit(solution)/shard_map/ppermute | solution.py:206
  23.0 1.3 %collective-permute-start.14 = (bf16[2,4,8192]{2,1,0:T(4,128)(2,1)S(1)}, bf16[2,4,8192]{2,1,0:T(4,128)(2,1)S(1)}, u32[]{:S(2)}, u32[]{:S(2)}) collective-permute-start(bf16[2,4,8192]{2,1,0:T(4,128)(2,1)S(1)} %collective-permute-done.6.refs_3_), channel_id=1, source_target_pairs={{0,1},{1,0},{2,3},{3,2},{4,5},{5,4},{6,7},{7,6},{8,9},{9,8},{10,11... | collective-permute-start | bytes 393224 | tf_op jit(solution)/shard_map/ppermute | solution.py:206
  26.3 1.1 %collective-permute-start.15 = (f32[1,128]{1,0:T(1,128)S(1)}, f32[1,128]{1,0:T(1,128)S(1)}, u32[]{:S(2)}, u32[]{:S(2)}) collective-permute-start(f32[1,128]{1,0:T(1,128)S(1)} %get-tuple-element.34), channel_id=1, source_target_pairs={{0,1},{1,0},{2,3},{3,2},{4,5},{5,4},{6,7},{7,6},{8,9},{9,8},{10,11... | collective-permute-start | bytes 1544 | tf_op jit(solution)/shard_map/ppermute | solution.py:206
  27.5 3.5 %collective-permute-start.16 = (f32[1,64]{1,0:T(1,128)S(1)}, f32[1,64]{1,0:T(1,128)S(1)}, u32[]{:S(2)}, u32[]{:S(2)}) collective-permute-start(f32[1,64]{1,0:T(1,128)S(1)} %get-tuple-element.36), channel_id=1, source_target_pairs={{0,2},{1,3},{2,0},{3,1},{4,6},{5,7},{6,4},{7,5},{8,10},{9,11},{10,... | collective-permute-start | bytes 776 | tf_op jit(solution)/shard_map/ppermute | solution.py:206
  31.1 3.5 %collective-permute-start.17 = (f32[1,32]{1,0:T(1,128)S(1)}, f32[1,32]{1,0:T(1,128)S(1)}, u32[]{:S(2)}, u32[]{:S(2)}) collective-permute-start(f32[1,32]{1,0:T(1,128)S(1)} %get-tuple-element.38), channel_id=1, source_target_pairs={{0,4},{1,5},{2,6},{3,7},{4,0},{5,1},{6,2},{7,3},{8,12},{9,13},{10,... | collective-permute-start | bytes 392 | tf_op jit(solution)/shard_map/ppermute | solution.py:206
  34.7 4.4 %collective-permute-start.18 = (f32[1,16]{1,0:T(1,128)S(1)}, f32[1,16]{1,0:T(1,128)S(1)}, u32[]{:S(2)}, u32[]{:S(2)}) collective-permute-start(f32[1,16]{1,0:T(1,128)S(1)} %get-tuple-element.40), channel_id=1, source_target_pairs={{0,8},{1,9},{2,10},{3,11},{4,12},{5,13},{6,14},{7,15},{8,0},{9,1},... | collective-permute-start | bytes 200 | tf_op jit(solution)/shard_map/ppermute | solution.py:206

commit v5 on v3

--- a/solution.py
+++ b/solution.py
@@ -24,11 +24,15 @@
 
 def prep_kernel(*refs):
     sources, (inner_out, outer_out, own_out, weight_out), held, done = refs[:7], refs[7:11], refs[11:17], refs[17]
-    targets = (*held, weight_out)
-    copies = [pltpu.make_async_copy(s, t, done.at[i]) for i, (s, t) in enumerate(zip(sources, targets))]
+    weight = sources[-1]
+    chunks = done.shape[0] - len(held)
+    step = weight.shape[0] // chunks
+    spans = [pl.ds(i * step, step) for i in range(chunks)]
+    pairs = [*zip(sources, held), *[(weight.at[span], weight_out.at[span]) for span in spans]]
+    copies = [pltpu.make_async_copy(s, t, done.at[i]) for i, (s, t) in enumerate(pairs)]
     for copy in copies:
         copy.start()
-    for copy in copies[:-1]:
+    for copy in copies[: len(held)]:
         copy.wait()
     coeff, status, bit, lower, upper, bias = held
     examples, specs, neurons = coeff.shape
@@ -61,7 +65,8 @@
     if rows < LANES:
         folded = jnp.concatenate([folded, jnp.zeros((LANES - rows, LANES), F32)], axis=0)
     own_out[...] = jnp.sum(folded.T, axis=0, keepdims=True)[:, 0:rows]
-    copies[-1].wait()
+    for copy in copies[len(held) :]:
+        copy.wait()
 
 
 def prep(coeff, status, bit, lower, upper, bias, weight):
@@ -78,7 +83,7 @@
             jax.ShapeDtypeStruct((1, 2 * rows), F32),
             jax.ShapeDtypeStruct(weight.shape, weight.dtype),
         ),
-        scratch_shapes=[pltpu.VMEM(a.shape, a.dtype) for a in small] + [pltpu.SemaphoreType.DMA((7,))],
+        scratch_shapes=[pltpu.VMEM(a.shape, a.dtype) for a in small] + [pltpu.SemaphoreType.DMA((10,))],
         compiler_params=pltpu.CompilerParams(vmem_limit_bytes=8 << 20),
         cost_estimate=pl.CostEstimate(
             flops=20 * rows * neurons, bytes_accessed=2 * weight.size + 12 * rows * neurons, transcendentals=0
@@ -209,23 +214,30 @@
         bound_coeff, status, slope_bit, pre_lower, pre_upper, layer_bias.reshape(1, neurons), weight
     )
 
+    bits = num_devices.bit_length() - 1
+    highs = sorted(range(8, num_devices, 8), key=lambda m: (m.bit_count(), -m))
     pieces = {0: bound_coeff}
-    for mask in range(4, num_devices, 4):
+    for high in highs:
+        low = high & -high
+        pieces[high] = swap(pieces[high ^ low], low)
+    for mask in (4, 2, 6):
         pieces[mask] = swap(bound_coeff, mask)
-    pieces[4], held = lax.optimization_barrier((pieces[4], held))
-    for mask in range(0, num_devices, 4):
-        pieces[mask + 2] = swap(pieces[mask], 2)
     args = (inner, outer, held, center_input, radius)
-    early = [0, 4, 2, 6, 1, 5, 3, 7]
-    late = sorted(set(range(num_devices)) - set(early), key=lambda m: (m & 1, m & 2, -m))
-    for mask in (0, 4, 2, 6):
-        pieces[mask + 1] = swap(pieces[mask], 1)
+    pieces[8], args = lax.optimization_barrier((pieces[8], args))
+    for high in highs:
+        for mask in (6, 4, 2):
+            pieces[high + mask] = swap(pieces[high], mask)
+    early = [0, 8, 4, 2, 6]
+    for mask in early:
+        if mask & 1 and mask not in pieces:
+            pieces[mask] = swap(pieces[mask - 1], 1)
     first = map_rows([pieces[m] for m in early], args)
-    for mask in late:
-        if mask & 1 == 0:
+    pieces[highs[-1] + 6], first = lax.optimization_barrier((pieces[highs[-1] + 6], first))
+    for mask in range(0, num_devices, 2):
+        if mask + 1 not in pieces:
             pieces[mask + 1] = swap(pieces[mask], 1)
-
-    bits = num_devices.bit_length() - 1
+    late = sorted([m for m in range(num_devices) if m not in early], key=lambda m: (m & 1, -(m & 8), -(m & 6)))
+
     sent = [int(format(i, "b").zfill(bits)[::-1], 2) for i in range(num_devices)]
     order = [(0, early.index(m)) if m in early else (1, late.index(m)) for m in sent]
     keep, send = map_rows([pieces[m] for m in late], args, first, order)

time: 42.9 us -> 38.4 us (0.90)
  waiting for transfers between devices: 20.9 us -> 11.3 us
  starting transfers between devices: 13.6 us -> 18 us
  Pallas kernels: 7.45 us -> 8.24 us
    ppermute x19, waiting for transfers between devices: 20.9 us -> 11.3 us  [swap(): lax.ppermute(array, 'row', [(i, i ^ mask) for i in range(num_devices)])]
    ppermute x19, starting transfers between devices: 13.6 us -> 18 us  [swap(): lax.ppermute(array, 'row', [(i, i ^ mask) for i in range(num_devices)])]
    pallas_call x2, Pallas kernels: 2.9 us -> 3.6 us  [map_rows(): pl.pallas_call(kernel, in_specs=[VMEM] * (len(pieces) + len(args) + len(m...]
  transfers between devices with their start and end apart: 19 -> 19, of which waited for: 7 -> 12; matrix products, arithmetic and copies ran while one was open for 0% -> 0% of each run, Pallas kernels for 12% -> 14%
where the time goes in v5:
time: 38.4 us; the launch traced here: 38.3 us
  starting transfers between devices  18 us (47%)
  waiting for transfers between devices  11.3 us (29%)
  Pallas kernels  8.24 us (21%)
  between operations  0.72 us (2%)
    ppermute x19, starting transfers between devices, swap(): lax.ppermute(array, 'row', [(i, i ^ mask) for i in range(num_devices)])  18 us
    ppermute x19, waiting for transfers between devices, swap(): lax.ppermute(array, 'row', [(i, i ^ mask) for i in range(num_devices)])  11.3 us
    pallas_call x1, Pallas kernels, prep(): pl.pallas_call(prep_kernel, in_specs=[pl.BlockSpec(memory_space=pltpu.HBM...  3.79 us
    pallas_call x2, Pallas kernels, map_rows(): pl.pallas_call(kernel, in_specs=[VMEM] * (len(pieces) + len(args) + len(m...  3.6 us
  transfers between devices with their start and end apart: 19, of which 12 were waited for; matrix products, arithmetic and copies ran while one was open for 0% of the time, Pallas kernels for 14%

profile of v5, /device:TPU:0, one launch (start us, length us, event | category | flops | bytes accessed | tf_op | source)
XLA Modules:
  0.0 38.3 jit_solution(14449063726395817910)
XLA Ops:
  0.6 0.0 copy-start
  0.6 0.0 copy-start.2
  0.7 0.0 copy-start.1
  0.7 4.1 %collective-permute-start = (bf16[2,4,8192]{2,1,0:T(4,128)(2,1)}, bf16[2,4,8192]{2,1,0:T(4,128)(2,1)S(1)}, u32[]{:S(2)}, u32[]{:S(2)}) collective-permute-start(bf16[2,4,8192]{2,1,0:T(4,128)(2,1)} %refs_0_.3), channel_id=1, source_target_pairs={{0,8},{1,9},{2,10},{3,11},{4,12},{5,13},{6,14},{7,15},{8,0},{9,1},... | collective-permute-start | bytes 393224 | tf_op jit(solution)/shard_map/ppermute | solution.py:211
  4.8 2.5 %collective-permute-start.4 = (bf16[2,4,8192]{2,1,0:T(4,128)(2,1)}, bf16[2,4,8192]{2,1,0:T(4,128)(2,1)S(1)}, u32[]{:S(2)}, u32[]{:S(2)}) collective-permute-start(bf16[2,4,8192]{2,1,0:T(4,128)(2,1)} %refs_0_.3), channel_id=1, source_target_pairs={{0,6},{1,7},{2,4},{3,5},{4,2},{5,3},{6,0},{7,1},{8,14},{9,15},{10,... | collective-permute-start | bytes 393224 | tf_op jit(solution)/shard_map/ppermute | solution.py:211
  7.3 0.5 %collective-permute-start.3 = (bf16[2,4,8192]{2,1,0:T(4,128)(2,1)}, bf16[2,4,8192]{2,1,0:T(4,128)(2,1)S(1)}, u32[]{:S(2)}, u32[]{:S(2)}) collective-permute-start(bf16[2,4,8192]{2,1,0:T(4,128)(2,1)} %refs_0_.3), channel_id=1, source_target_pairs={{0,2},{1,3},{2,0},{3,1},{4,6},{5,7},{6,4},{7,5},{8,10},{9,11},{10,... | collective-permute-start | bytes 393224 | tf_op jit(solution)/shard_map/ppermute | solution.py:211
  7.8 0.4 %collective-permute-start.2 = (bf16[2,4,8192]{2,1,0:T(4,128)(2,1)}, bf16[2,4,8192]{2,1,0:T(4,128)(2,1)S(1)}, u32[]{:S(2)}, u32[]{:S(2)}) collective-permute-start(bf16[2,4,8192]{2,1,0:T(4,128)(2,1)} %refs_0_.3), channel_id=1, source_target_pairs={{0,4},{1,5},{2,6},{3,7},{4,0},{5,1},{6,2},{7,3},{8,12},{9,13},{10,... | collective-permute-start | bytes 393224 | tf_op jit(solution)/shard_map/ppermute | solution.py:211
  8.3 3.8 %prep.1 = (f32[8,8192]{1,0:T(8,128)S(1)}, f32[8,8192]{1,0:T(8,128)S(1)}, f32[1,16]{1,0:T(1,128)S(1)}, bf16[8192,512]{1,0:T(8,128)(2,1)S(1)}) custom-call(bf16[2,4,8192]{2,1,0:T(4,128)(2,1)} %refs_0_.3, s32[2,8192]{1,0:T(2,128)} %refs_1_.1, s32[2,8192]{1,0:T(2,128)} %refs_2_.1, f32[2,8192]{1,0:T(2,128)} %refs_3_.1, f32[2,8192]{1,0:T(2,128)} %refs_4_.1, ...), custom_call_target="tpu_custom_call" | custom-call | flops 1310720 | bytes 9175040 | tf_op jit(solution)/shard_map/prep/pallas_call | solution.py:76
  12.1 0.0 collective-permute-done.refs_1_
  12.1 2.6 %collective-permute-start.1 = (bf16[2,4,8192]{2,1,0:T(4,128)(2,1)S(1)}, bf16[2,4,8192]{2,1,0:T(4,128)(2,1)S(1)}, u32[]{:S(2)}, u32[]{:S(2)}) collective-permute-start(bf16[2,4,8192]{2,1,0:T(4,128)(2,1)S(1)} %collective-permute-done.refs_1_), channel_id=1, source_target_pairs={{0,6},{1,7},{2,4},{3,5},{4,2},{5,3},{6,0},{7,1},{8,14},{9,15},{10,... | collective-permute-start | bytes 393224 | tf_op jit(solution)/shard_map/ppermute | solution.py:211
  14.7 0.0 collective-permute-start.14
  14.7 0.0 collective-permute-done.4.refs_4_
  14.7 0.5 %collective-permute-start.11 = (bf16[2,4,8192]{2,1,0:T(4,128)(2,1)S(1)}, bf16[2,4,8192]{2,1,0:T(4,128)(2,1)S(1)}, u32[]{:S(2)}, u32[]{:S(2)}) collective-permute-start(bf16[2,4,8192]{2,1,0:T(4,128)(2,1)S(1)} %collective-permute-done.4.refs_4_), channel_id=1, source_target_pairs={{0,1},{1,0},{2,3},{3,2},{4,5},{5,4},{6,7},{7,6},{8,9},{9,8},{10,11... | collective-permute-start | bytes 393224 | tf_op jit(solution)/shard_map/ppermute | solution.py:211
  15.2 0.0 collective-permute-done.3.refs_3_
  15.2 0.5 %collective-permute-start.6 = (bf16[2,4,8192]{2,1,0:T(4,128)(2,1)S(1)}, bf16[2,4,8192]{2,1,0:T(4,128)(2,1)S(1)}, u32[]{:S(2)}, u32[]{:S(2)}) collective-permute-start(bf16[2,4,8192]{2,1,0:T(4,128)(2,1)S(1)} %collective-permute-done.refs_1_), channel_id=1, source_target_pairs={{0,2},{1,3},{2,0},{3,1},{4,6},{5,7},{6,4},{7,5},{8,10},{9,11},{10,... | collective-permute-start | bytes 393224 | tf_op jit(solution)/shard_map/ppermute | solution.py:211
  15.7 0.5 %collective-permute-done.2.refs_2_ = bf16[2,4,8192]{2,1,0:T(4,128)(2,1)S(1)} collective-permute-done((bf16[2,4,8192]{2,1,0:T(4,128)(2,1)}, bf16[2,4,8192]{2,1,0:T(4,128)(2,1)S(1)}, u32[]{:S(2)}, u32[]{:S(2)}) %collective-permute-start.2) | collective-permute-done | bytes 131104 | tf_op jit(solution)/shard_map/ppermute | solution.py:211
  16.2 0.0 collective-permute-start.5
  16.2 2.0 %collective-permute-done.1.refs_0_ = bf16[2,4,8192]{2,1,0:T(4,128)(2,1)S(1)} collective-permute-done((bf16[2,4,8192]{2,1,0:T(4,128)(2,1)S(1)}, bf16[2,4,8192]{2,1,0:T(4,128)(2,1)S(1)}, u32[]{:S(2)}, u32[]{:S(2)}) %collective-permute-start.1) | collective-permute-done | bytes 131104 | tf_op jit(solution)/shard_map/ppermute | solution.py:211
  18.2 0.0 collective-permute-start.13
  18.3 1.7 %map_rows.2.refs_16_ = f32[1,80]{1,0:T(1,128)S(1)} custom-call(bf16[2,4,8192]{2,1,0:T(4,128)(2,1)S(1)} %copy-done, bf16[2,4,8192]{2,1,0:T(4,128)(2,1)S(1)} %collective-permute-done.refs_1_, bf16[2,4,8192]{2,1,0:T(4,128)(2,1)S(1)} %collective-permute-done.2.refs_2_, bf16[2,4,8192]{2,1,0:T(4,128)(2,1)S(1)} %collective-permute-done.3.refs_3_, ...), custom_call_target="tpu_custom_call" | custom-call | flops 671088640 | bytes 1310720 | tf_op jit(solution)/shard_map/map_rows/pallas_call | solution.py:152
  20.0 0.0 collective-permute-done.14.refs_10_
  20.0 0.6 %collective-permute-start.10 = (bf16[2,4,8192]{2,1,0:T(4,128)(2,1)S(1)}, bf16[2,4,8192]{2,1,0:T(4,128)(2,1)S(1)}, u32[]{:S(2)}, u32[]{:S(2)}) collective-permute-start(bf16[2,4,8192]{2,1,0:T(4,128)(2,1)S(1)} %collective-permute-done.refs_1_), channel_id=1, source_target_pairs={{0,1},{1,0},{2,3},{3,2},{4,5},{5,4},{6,7},{7,6},{8,9},{9,8},{10,11... | collective-permute-start | bytes 393224 | tf_op jit(solution)/shard_map/ppermute | solution.py:211
  20.6 0.0 collective-permute-done.11.refs_7_
  20.6 0.1 collective-permute-start.12
  20.6 0.3 collective-permute-done.6.refs_2_
  21.0 0.1 collective-permute-start.9
  21.1 0.1 collective-permute-done.5.refs_1_
  21.2 0.3 collective-permute-start.8
  21.5 0.0 collective-permute-done.13.refs_9_
  21.5 0.2 collective-permute-start.7
  21.7 0.2 collective-permute-done.12.refs_8_
  21.9 0.0 collective-permute-done.10.refs_6_
  21.9 0.4 %collective-permute-done.9.refs_5_ = bf16[2,4,8192]{2,1,0:T(4,128)(2,1)S(1)} collective-permute-done((bf16[2,4,8192]{2,1,0:T(4,128)(2,1)S(1)}, bf16[2,4,8192]{2,1,0:T(4,128)(2,1)S(1)}, u32[]{:S(2)}, u32[]{:S(2)}) %collective-permute-start.9) | collective-permute-done | bytes 131104 | tf_op jit(solution)/shard_map/ppermute | solution.py:211
  22.3 0.2 collective-permute-done.8.refs_4_
  22.5 0.3 collective-permute-done.7.refs_3_
  22.8 1.9 %map_rows.3 = (f32[1,128]{1,0:T(1,128)S(1)}, f32[1,128]{1,0:T(1,128)S(1)}) custom-call(bf16[2,4,8192]{2,1,0:T(4,128)(2,1)S(1)} %collective-permute-done.1.refs_0_, bf16[2,4,8192]{2,1,0:T(4,128)(2,1)S(1)} %collective-permute-done.5.refs_1_, bf16[2,4,8192]{2,1,0:T(4,128)(2,1)S(1)} %collective-permute-done.6.refs_2_, ...), custom_call_target="tpu_custom_call" | custom-call | flops 1476395008 | bytes 2883584 | tf_op jit(solution)/shard_map/map_rows/pallas_call | solution.py:152
  24.7 0.3 collective-permute-start.15
  25.0 0.9 %collective-permute-done.15.came = f32[1,128]{1,0:T(1,128)S(1)} collective-permute-done((f32[1,128]{1,0:T(1,128)S(1)}, f32[1,128]{1,0:T(1,128)S(1)}, u32[]{:S(2)}, u32[]{:S(2)}) %collective-permute-start.15) | collective-permute-done | bytes 544 | tf_op jit(solution)/shard_map/ppermute | solution.py:211
  25.9 0.1 fold.3
  26.0 1.5 %collective-permute-start.16 = (f32[1,64]{1,0:T(1,128)S(1)}, f32[1,64]{1,0:T(1,128)S(1)}, u32[]{:S(2)}, u32[]{:S(2)}) collective-permute-start(f32[1,64]{1,0:T(1,128)S(1)} %get-tuple-element.36), channel_id=1, source_target_pairs={{0,2},{1,3},{2,0},{3,1},{4,6},{5,7},{6,4},{7,5},{8,10},{9,11},{10,... | collective-permute-start | bytes 776 | tf_op jit(solution)/shard_map/ppermute | solution.py:211
  27.4 2.1 %collective-permute-done.16.came = f32[1,64]{1,0:T(1,128)S(1)} collective-permute-done((f32[1,64]{1,0:T(1,128)S(1)}, f32[1,64]{1,0:T(1,128)S(1)}, u32[]{:S(2)}, u32[]{:S(2)}) %collective-permute-start.16) | collective-permute-done | bytes 288 | tf_op jit(solution)/shard_map/ppermute | solution.py:211
  29.5 0.1 fold.4
  29.6 1.8 %collective-permute-start.17 = (f32[1,32]{1,0:T(1,128)S(1)}, f32[1,32]{1,0:T(1,128)S(1)}, u32[]{:S(2)}, u32[]{:S(2)}) collective-permute-start(f32[1,32]{1,0:T(1,128)S(1)} %get-tuple-element.38), channel_id=1, source_target_pairs={{0,4},{1,5},{2,6},{3,7},{4,0},{5,1},{6,2},{7,3},{8,12},{9,13},{10,... | collective-permute-start | bytes 392 | tf_op jit(solution)/shard_map/ppermute | solution.py:211
  31.4 1.7 %collective-permute-done.17.came = f32[1,32]{1,0:T(1,128)S(1)} collective-permute-done((f32[1,32]{1,0:T(1,128)S(1)}, f32[1,32]{1,0:T(1,128)S(1)}, u32[]{:S(2)}, u32[]{:S(2)}) %collective-permute-start.17) | collective-permute-done | bytes 160 | tf_op jit(solution)/shard_map/ppermute | solution.py:211
  33.1 0.1 fold.5
  33.2 2.0 %collective-permute-start.18 = (f32[1,16]{1,0:T(1,128)S(1)}, f32[1,16]{1,0:T(1,128)S(1)}, u32[]{:S(2)}, u32[]{:S(2)}) collective-permute-start(f32[1,16]{1,0:T(1,128)S(1)} %get-tuple-element.40), channel_id=1, source_target_pairs={{0,8},{1,9},{2,10},{3,11},{4,12},{5,13},{6,14},{7,15},{8,0},{9,1},... | collective-permute-start | bytes 200 | tf_op jit(solution)/shard_map/ppermute | solution.py:211
  35.2 2.5 %collective-permute-done.18.came = f32[1,16]{1,0:T(1,128)S(1)} collective-permute-done((f32[1,16]{1,0:T(1,128)S(1)}, f32[1,16]{1,0:T(1,128)S(1)}, u32[]{:S(2)}, u32[]{:S(2)}) %collective-permute-start.18) | collective-permute-done | bytes 96 | tf_op jit(solution)/shard_map/ppermute | solution.py:211
  37.7 0.6 %finish.1 = (f32[2,4]{1,0:T(2,128)}, f32[2,4]{1,0:T(2,128)}) custom-call(f32[1,16]{1,0:T(1,128)S(1)} %get-tuple-element.39.kept, f32[1,16]{1,0:T(1,128)S(1)} %collective-permute-done.18.came, f32[1,16]{1,0:T(1,128)S(1)} %get-tuple-element.41.own), custom_call_target="tpu_custom_call" | custom-call | tf_op jit(solution)/shard_map/finish/pallas_call | solution.py:195
  (3 shorter events, 0.0 us)
Async XLA Ops:
  0.6 14.0 %copy-start = (bf16[2,4,8192]{2,1,0:T(4,128)(2,1)S(1)}, bf16[2,4,8192]{2,1,0:T(4,128)(2,1)}, u32[]{:S(2)}) copy-start(bf16[2,4,8192]{2,1,0:T(4,128)(2,1)} %refs_0_.3) | copy-start | bytes 393220
  0.6 17.6 %copy-start.2 = (f32[2,512]{1,0:T(2,128)S(1)}, f32[2,512]{1,0:T(2,128)}, u32[]{:S(2)}) copy-start(f32[2,512]{1,0:T(2,128)} %refs_15_) | copy-start | bytes 12292
  0.7 17.6 %copy-start.1 = (f32[2,512]{1,0:T(2,128)S(1)}, f32[2,512]{1,0:T(2,128)}, u32[]{:S(2)}) copy-start(f32[2,512]{1,0:T(2,128)} %refs_14_) | copy-start | bytes 12292
  0.7 11.4 %collective-permute-start = (bf16[2,4,8192]{2,1,0:T(4,128)(2,1)}, bf16[2,4,8192]{2,1,0:T(4,128)(2,1)S(1)}, u32[]{:S(2)}, u32[]{:S(2)}) collective-permute-start(bf16[2,4,8192]{2,1,0:T(4,128)(2,1)} %refs_0_.3), channel_id=1, source_target_pairs={{0,8},{1,9},{2,10},{3,11},{4,12},{5,13},{6,14},{7,15},{8,0},{9,1},... | collective-permute-start | bytes 393224 | tf_op jit(solution)/shard_map/ppermute | solution.py:211
  4.8 9.9 %collective-permute-start.4 = (bf16[2,4,8192]{2,1,0:T(4,128)(2,1)}, bf16[2,4,8192]{2,1,0:T(4,128)(2,1)S(1)}, u32[]{:S(2)}, u32[]{:S(2)}) collective-permute-start(bf16[2,4,8192]{2,1,0:T(4,128)(2,1)} %refs_0_.3), channel_id=1, source_target_pairs={{0,6},{1,7},{2,4},{3,5},{4,2},{5,3},{6,0},{7,1},{8,14},{9,15},{10,... | collective-permute-start | bytes 393224 | tf_op jit(solution)/shard_map/ppermute | solution.py:211
  7.3 7.9 %collective-permute-start.3 = (bf16[2,4,8192]{2,1,0:T(4,128)(2,1)}, bf16[2,4,8192]{2,1,0:T(4,128)(2,1)S(1)}, u32[]{:S(2)}, u32[]{:S(2)}) collective-permute-start(bf16[2,4,8192]{2,1,0:T(4,128)(2,1)} %refs_0_.3), channel_id=1, source_target_pairs={{0,2},{1,3},{2,0},{3,1},{4,6},{5,7},{6,4},{7,5},{8,10},{9,11},{10,... | collective-permute-start | bytes 393224 | tf_op jit(solution)/shard_map/ppermute | solution.py:211
  7.8 8.4 %collective-permute-start.2 = (bf16[2,4,8192]{2,1,0:T(4,128)(2,1)}, bf16[2,4,8192]{2,1,0:T(4,128)(2,1)S(1)}, u32[]{:S(2)}, u32[]{:S(2)}) collective-permute-start(bf16[2,4,8192]{2,1,0:T(4,128)(2,1)} %refs_0_.3), channel_id=1, source_target_pairs={{0,4},{1,5},{2,6},{3,7},{4,0},{5,1},{6,2},{7,3},{8,12},{9,13},{10,... | collective-permute-start | bytes 393224 | tf_op jit(solution)/shard_map/ppermute | solution.py:211
  12.1 6.2 %collective-permute-start.1 = (bf16[2,4,8192]{2,1,0:T(4,128)(2,1)S(1)}, bf16[2,4,8192]{2,1,0:T(4,128)(2,1)S(1)}, u32[]{:S(2)}, u32[]{:S(2)}) collective-permute-start(bf16[2,4,8192]{2,1,0:T(4,128)(2,1)S(1)} %collective-permute-done.refs_1_), channel_id=1, source_target_pairs={{0,6},{1,7},{2,4},{3,5},{4,2},{5,3},{6,0},{7,1},{8,14},{9,15},{10,... | collective-permute-start | bytes 393224 | tf_op jit(solution)/shard_map/ppermute | solution.py:211
  14.7 5.3 %collective-permute-start.14 = (bf16[2,4,8192]{2,1,0:T(4,128)(2,1)S(1)}, bf16[2,4,8192]{2,1,0:T(4,128)(2,1)S(1)}, u32[]{:S(2)}, u32[]{:S(2)}) collective-permute-start(bf16[2,4,8192]{2,1,0:T(4,128)(2,1)S(1)} %copy-done), channel_id=1, source_target_pairs={{0,1},{1,0},{2,3},{3,2},{4,5},{5,4},{6,7},{7,6},{8,9},{9,8},{10,11... | collective-permute-start | bytes 393224 | tf_op jit(solution)/shard_map/ppermute | solution.py:211
  14.7 5.9 %collective-permute-start.11 = (bf16[2,4,8192]{2,1,0:T(4,128)(2,1)S(1)}, bf16[2,4,8192]{2,1,0:T(4,128)(2,1)S(1)}, u32[]{:S(2)}, u32[]{:S(2)}) collective-permute-start(bf16[2,4,8192]{2,1,0:T(4,128)(2,1)S(1)} %collective-permute-done.4.refs_4_), channel_id=1, source_target_pairs={{0,1},{1,0},{2,3},{3,2},{4,5},{5,4},{6,7},{7,6},{8,9},{9,8},{10,11... | collective-permute-start | bytes 393224 | tf_op jit(solution)/shard_map/ppermute | solution.py:211
  15.2 5.8 %collective-permute-start.6 = (bf16[2,4,8192]{2,1,0:T(4,128)(2,1)S(1)}, bf16[2,4,8192]{2,1,0:T(4,128)(2,1)S(1)}, u32[]{:S(2)}, u32[]{:S(2)}) collective-permute-start(bf16[2,4,8192]{2,1,0:T(4,128)(2,1)S(1)} %collective-permute-done.refs_1_), channel_id=1, source_target_pairs={{0,2},{1,3},{2,0},{3,1},{4,6},{5,7},{6,4},{7,5},{8,10},{9,11},{10,... | collective-permute-start | bytes 393224 | tf_op jit(solution)/shard_map/ppermute | solution.py:211
  16.2 5.0 %collective-permute-start.5 = (bf16[2,4,8192]{2,1,0:T(4,128)(2,1)S(1)}, bf16[2,4,8192]{2,1,0:T(4,128)(2,1)S(1)}, u32[]{:S(2)}, u32[]{:S(2)}) collective-permute-start(bf16[2,4,8192]{2,1,0:T(4,128)(2,1)S(1)} %collective-permute-done.refs_1_), channel_id=1, source_target_pairs={{0,4},{1,5},{2,6},{3,7},{4,0},{5,1},{6,2},{7,3},{8,12},{9,13},{10,... | collective-permute-start | bytes 393224 | tf_op jit(solution)/shard_map/ppermute | solution.py:211
  18.2 3.2 %collective-permute-start.13 = (bf16[2,4,8192]{2,1,0:T(4,128)(2,1)S(1)}, bf16[2,4,8192]{2,1,0:T(4,128)(2,1)S(1)}, u32[]{:S(2)}, u32[]{:S(2)}) collective-permute-start(bf16[2,4,8192]{2,1,0:T(4,128)(2,1)S(1)} %collective-permute-done.3.refs_3_), channel_id=1, source_target_pairs={{0,1},{1,0},{2,3},{3,2},{4,5},{5,4},{6,7},{7,6},{8,9},{9,8},{10,11... | collective-permute-start | bytes 393224 | tf_op jit(solution)/shard_map/ppermute | solution.py:211
  20.0 1.9 %collective-permute-start.10 = (bf16[2,4,8192]{2,1,0:T(4,128)(2,1)S(1)}, bf16[2,4,8192]{2,1,0:T(4,128)(2,1)S(1)}, u32[]{:S(2)}, u32[]{:S(2)}) collective-permute-start(bf16[2,4,8192]{2,1,0:T(4,128)(2,1)S(1)} %collective-permute-done.refs_1_), channel_id=1, source_target_pairs={{0,1},{1,0},{2,3},{3,2},{4,5},{5,4},{6,7},{7,6},{8,9},{9,8},{10,11... | collective-permute-start | bytes 393224 | tf_op jit(solution)/shard_map/ppermute | solution.py:211
  20.6 1.3 %collective-permute-start.12 = (bf16[2,4,8192]{2,1,0:T(4,128)(2,1)S(1)}, bf16[2,4,8192]{2,1,0:T(4,128)(2,1)S(1)}, u32[]{:S(2)}, u32[]{:S(2)}) collective-permute-start(bf16[2,4,8192]{2,1,0:T(4,128)(2,1)S(1)} %collective-permute-done.2.refs_2_), channel_id=1, source_target_pairs={{0,1},{1,0},{2,3},{3,2},{4,5},{5,4},{6,7},{7,6},{8,9},{9,8},{10,11... | collective-permute-start | bytes 393224 | tf_op jit(solution)/shard_map/ppermute | solution.py:211
  21.0 1.3 %collective-permute-start.9 = (bf16[2,4,8192]{2,1,0:T(4,128)(2,1)S(1)}, bf16[2,4,8192]{2,1,0:T(4,128)(2,1)S(1)}, u32[]{:S(2)}, u32[]{:S(2)}) collective-permute-start(bf16[2,4,8192]{2,1,0:T(4,128)(2,1)S(1)} %collective-permute-done.6.refs_2_), channel_id=1, source_target_pairs={{0,1},{1,0},{2,3},{3,2},{4,5},{5,4},{6,7},{7,6},{8,9},{9,8},{10,11... | collective-permute-start | bytes 393224 | tf_op jit(solution)/shard_map/ppermute | solution.py:211
  21.2 1.3 %collective-permute-start.8 = (bf16[2,4,8192]{2,1,0:T(4,128)(2,1)S(1)}, bf16[2,4,8192]{2,1,0:T(4,128)(2,1)S(1)}, u32[]{:S(2)}, u32[]{:S(2)}) collective-permute-start(bf16[2,4,8192]{2,1,0:T(4,128)(2,1)S(1)} %collective-permute-done.5.refs_1_), channel_id=1, source_target_pairs={{0,1},{1,0},{2,3},{3,2},{4,5},{5,4},{6,7},{7,6},{8,9},{9,8},{10,11... | collective-permute-start | bytes 393224 | tf_op jit(solution)/shard_map/ppermute | solution.py:211
  21.5 1.3 %collective-permute-start.7 = (bf16[2,4,8192]{2,1,0:T(4,128)(2,1)S(1)}, bf16[2,4,8192]{2,1,0:T(4,128)(2,1)S(1)}, u32[]{:S(2)}, u32[]{:S(2)}) collective-permute-start(bf16[2,4,8192]{2,1,0:T(4,128)(2,1)S(1)} %collective-permute-done.1.refs_0_), channel_id=1, source_target_pairs={{0,1},{1,0},{2,3},{3,2},{4,5},{5,4},{6,7},{7,6},{8,9},{9,8},{10,11... | collective-permute-start | bytes 393224 | tf_op jit(solution)/shard_map/ppermute | solution.py:211
  24.7 1.2 %collective-permute-start.15 = (f32[1,128]{1,0:T(1,128)S(1)}, f32[1,128]{1,0:T(1,128)S(1)}, u32[]{:S(2)}, u32[]{:S(2)}) collective-permute-start(f32[1,128]{1,0:T(1,128)S(1)} %get-tuple-element.34), channel_id=1, source_target_pairs={{0,1},{1,0},{2,3},{3,2},{4,5},{5,4},{6,7},{7,6},{8,9},{9,8},{10,11... | collective-permute-start | bytes 1544 | tf_op jit(solution)/shard_map/ppermute | solution.py:211
  26.0 3.5 %collective-permute-start.16 = (f32[1,64]{1,0:T(1,128)S(1)}, f32[1,64]{1,0:T(1,128)S(1)}, u32[]{:S(2)}, u32[]{:S(2)}) collective-permute-start(f32[1,64]{1,0:T(1,128)S(1)} %get-tuple-element.36), channel_id=1, source_target_pairs={{0,2},{1,3},{2,0},{3,1},{4,6},{5,7},{6,4},{7,5},{8,10},{9,11},{10,... | collective-permute-start | bytes 776 | tf_op jit(solution)/shard_map/ppermute | solution.py:211
  29.6 3.5 %collective-permute-start.17 = (f32[1,32]{1,0:T(1,128)S(1)}, f32[1,32]{1,0:T(1,128)S(1)}, u32[]{:S(2)}, u32[]{:S(2)}) collective-permute-start(f32[1,32]{1,0:T(1,128)S(1)} %get-tuple-element.38), channel_id=1, source_target_pairs={{0,4},{1,5},{2,6},{3,7},{4,0},{5,1},{6,2},{7,3},{8,12},{9,13},{10,... | collective-permute-start | bytes 392 | tf_op jit(solution)/shard_map/ppermute | solution.py:211
  33.2 4.4 %collective-permute-start.18 = (f32[1,16]{1,0:T(1,128)S(1)}, f32[1,16]{1,0:T(1,128)S(1)}, u32[]{:S(2)}, u32[]{:S(2)}) collective-permute-start(f32[1,16]{1,0:T(1,128)S(1)} %get-tuple-element.40), channel_id=1, source_target_pairs={{0,8},{1,9},{2,10},{3,11},{4,12},{5,13},{6,14},{7,15},{8,0},{9,1},... | collective-permute-start | bytes 200 | tf_op jit(solution)/shard_map/ppermute | solution.py:211

commit v6 on v5

--- a/solution.py
+++ b/solution.py
@@ -98,7 +98,7 @@
     examples, specs, neurons = pieces[0].shape
     rows = examples * specs
     columns = weight.shape[1]
-    step = min(neurons, 2048)
+    step = min(neurons, 1024)
     for start in range(0, neurons, step):
         span = slice(start, start + step)
         inner_rows, outer_rows = inner[:, span], outer[:, span]
@@ -109,7 +109,8 @@
             up = (values * jnp.where(positive, outer_rows, inner_rows)).astype(BF16)
             at = index * 2 * rows
             relaxed[at : at + 2 * rows, span] = jnp.concatenate([low, up], axis=0)
-    mapped = jnp.dot(relaxed[...], weight[...], preferred_element_type=F32)
+        term = jnp.dot(relaxed[:, span], weight[span, :], preferred_element_type=F32)
+        mapped = term if start == 0 else mapped + term
     centers, radii = center[...], radius[...]
 
     def per_row(values_low, values_up):
@@ -224,6 +225,7 @@
         pieces[mask] = swap(bound_coeff, mask)
     args = (inner, outer, held, center_input, radius)
     pieces[8], args = lax.optimization_barrier((pieces[8], args))
+    pieces[6], args = lax.optimization_barrier((pieces[6], args))
     for high in highs:
         for mask in (6, 4, 2):
             pieces[high + mask] = swap(pieces[high], mask)

time: 38.4 us -> 38.4 us (level)
  no operation moved by 1% of the time
where the time goes in v6:
time: 38.4 us; the launch traced here: 38.3 us
  starting transfers between devices  17.8 us (46%)
  waiting for transfers between devices  11.5 us (30%)
  Pallas kernels  8.24 us (21%)
  between operations  0.72 us (2%)
    ppermute x19, starting transfers between devices, swap(): lax.ppermute(array, 'row', [(i, i ^ mask) for i in range(num_devices)])  17.8 us
    ppermute x19, waiting for transfers between devices, swap(): lax.ppermute(array, 'row', [(i, i ^ mask) for i in range(num_devices)])  11.5 us
    pallas_call x1, Pallas kernels, prep(): pl.pallas_call(prep_kernel, in_specs=[pl.BlockSpec(memory_space=pltpu.HBM...  3.79 us
    pallas_call x2, Pallas kernels, map_rows(): pl.pallas_call(kernel, in_specs=[VMEM] * (len(pieces) + len(args) + len(m...  3.6 us
  transfers between devices with their start and end apart: 19, of which 12 were waited for; matrix products, arithmetic and copies ran while one was open for 0% of the time, Pallas kernels for 14%

profile of v6, /device:TPU:0, one launch (start us, length us, event | category | flops | bytes accessed | tf_op | source)
XLA Modules:
  0.0 38.3 jit_solution(7336335907217223852)
XLA Ops:
  0.6 0.0 copy-start
  0.6 0.0 copy-start.2
  0.7 0.0 copy-start.1
  0.7 4.1 %collective-permute-start = (bf16[2,4,8192]{2,1,0:T(4,128)(2,1)}, bf16[2,4,8192]{2,1,0:T(4,128)(2,1)S(1)}, u32[]{:S(2)}, u32[]{:S(2)}) collective-permute-start(bf16[2,4,8192]{2,1,0:T(4,128)(2,1)} %refs_0_.3), channel_id=1, source_target_pairs={{0,8},{1,9},{2,10},{3,11},{4,12},{5,13},{6,14},{7,15},{8,0},{9,1},... | collective-permute-start | bytes 393224 | tf_op jit(solution)/shard_map/ppermute | solution.py:212
  4.8 2.5 %collective-permute-start.4 = (bf16[2,4,8192]{2,1,0:T(4,128)(2,1)}, bf16[2,4,8192]{2,1,0:T(4,128)(2,1)S(1)}, u32[]{:S(2)}, u32[]{:S(2)}) collective-permute-start(bf16[2,4,8192]{2,1,0:T(4,128)(2,1)} %refs_0_.3), channel_id=1, source_target_pairs={{0,6},{1,7},{2,4},{3,5},{4,2},{5,3},{6,0},{7,1},{8,14},{9,15},{10,... | collective-permute-start | bytes 393224 | tf_op jit(solution)/shard_map/ppermute | solution.py:212
  7.3 0.5 %collective-permute-start.3 = (bf16[2,4,8192]{2,1,0:T(4,128)(2,1)}, bf16[2,4,8192]{2,1,0:T(4,128)(2,1)S(1)}, u32[]{:S(2)}, u32[]{:S(2)}) collective-permute-start(bf16[2,4,8192]{2,1,0:T(4,128)(2,1)} %refs_0_.3), channel_id=1, source_target_pairs={{0,2},{1,3},{2,0},{3,1},{4,6},{5,7},{6,4},{7,5},{8,10},{9,11},{10,... | collective-permute-start | bytes 393224 | tf_op jit(solution)/shard_map/ppermute | solution.py:212
  7.8 0.4 %collective-permute-start.2 = (bf16[2,4,8192]{2,1,0:T(4,128)(2,1)}, bf16[2,4,8192]{2,1,0:T(4,128)(2,1)S(1)}, u32[]{:S(2)}, u32[]{:S(2)}) collective-permute-start(bf16[2,4,8192]{2,1,0:T(4,128)(2,1)} %refs_0_.3), channel_id=1, source_target_pairs={{0,4},{1,5},{2,6},{3,7},{4,0},{5,1},{6,2},{7,3},{8,12},{9,13},{10,... | collective-permute-start | bytes 393224 | tf_op jit(solution)/shard_map/ppermute | solution.py:212
  8.3 3.8 %prep.1 = (f32[8,8192]{1,0:T(8,128)S(1)}, f32[8,8192]{1,0:T(8,128)S(1)}, f32[1,16]{1,0:T(1,128)S(1)}, bf16[8192,512]{1,0:T(8,128)(2,1)S(1)}) custom-call(bf16[2,4,8192]{2,1,0:T(4,128)(2,1)} %refs_0_.3, s32[2,8192]{1,0:T(2,128)} %refs_1_.1, s32[2,8192]{1,0:T(2,128)} %refs_2_.1, f32[2,8192]{1,0:T(2,128)} %refs_3_.1, f32[2,8192]{1,0:T(2,128)} %refs_4_.1, ...), custom_call_target="tpu_custom_call" | custom-call | flops 1310720 | bytes 9175040 | tf_op jit(solution)/shard_map/prep/pallas_call | solution.py:76
  12.1 0.0 collective-permute-done.refs_1_
  12.1 2.6 %collective-permute-start.1 = (bf16[2,4,8192]{2,1,0:T(4,128)(2,1)S(1)}, bf16[2,4,8192]{2,1,0:T(4,128)(2,1)S(1)}, u32[]{:S(2)}, u32[]{:S(2)}) collective-permute-start(bf16[2,4,8192]{2,1,0:T(4,128)(2,1)S(1)} %collective-permute-done.refs_1_), channel_id=1, source_target_pairs={{0,6},{1,7},{2,4},{3,5},{4,2},{5,3},{6,0},{7,1},{8,14},{9,15},{10,... | collective-permute-start | bytes 393224 | tf_op jit(solution)/shard_map/ppermute | solution.py:212
  14.7 0.0 collective-permute-start.14
  14.7 0.0 collective-permute-done.3.refs_3_
  14.7 0.5 %collective-permute-start.13 = (bf16[2,4,8192]{2,1,0:T(4,128)(2,1)S(1)}, bf16[2,4,8192]{2,1,0:T(4,128)(2,1)S(1)}, u32[]{:S(2)}, u32[]{:S(2)}) collective-permute-start(bf16[2,4,8192]{2,1,0:T(4,128)(2,1)S(1)} %collective-permute-done.3.refs_3_), channel_id=1, source_target_pairs={{0,1},{1,0},{2,3},{3,2},{4,5},{5,4},{6,7},{7,6},{8,9},{9,8},{10,11... | collective-permute-start | bytes 393224 | tf_op jit(solution)/shard_map/ppermute | solution.py:212
  15.2 0.0 collective-permute-done.4.refs_4_
  15.2 0.5 %collective-permute-start.6 = (bf16[2,4,8192]{2,1,0:T(4,128)(2,1)S(1)}, bf16[2,4,8192]{2,1,0:T(4,128)(2,1)S(1)}, u32[]{:S(2)}, u32[]{:S(2)}) collective-permute-start(bf16[2,4,8192]{2,1,0:T(4,128)(2,1)S(1)} %collective-permute-done.refs_1_), channel_id=1, source_target_pairs={{0,2},{1,3},{2,0},{3,1},{4,6},{5,7},{6,4},{7,5},{8,10},{9,11},{10,... | collective-permute-start | bytes 393224 | tf_op jit(solution)/shard_map/ppermute | solution.py:212
  15.7 0.5 %collective-permute-done.2.refs_2_ = bf16[2,4,8192]{2,1,0:T(4,128)(2,1)S(1)} collective-permute-done((bf16[2,4,8192]{2,1,0:T(4,128)(2,1)}, bf16[2,4,8192]{2,1,0:T(4,128)(2,1)S(1)}, u32[]{:S(2)}, u32[]{:S(2)}) %collective-permute-start.2) | collective-permute-done | bytes 131104 | tf_op jit(solution)/shard_map/ppermute | solution.py:212
  16.2 0.0 collective-permute-start.5
  16.2 2.0 %collective-permute-done.1.refs_0_ = bf16[2,4,8192]{2,1,0:T(4,128)(2,1)S(1)} collective-permute-done((bf16[2,4,8192]{2,1,0:T(4,128)(2,1)S(1)}, bf16[2,4,8192]{2,1,0:T(4,128)(2,1)S(1)}, u32[]{:S(2)}, u32[]{:S(2)}) %collective-permute-start.1) | collective-permute-done | bytes 131104 | tf_op jit(solution)/shard_map/ppermute | solution.py:212
  18.2 0.0 collective-permute-start.12
  18.2 1.7 %map_rows.2.refs_16_ = f32[1,80]{1,0:T(1,128)S(1)} custom-call(bf16[2,4,8192]{2,1,0:T(4,128)(2,1)S(1)} %copy-done, bf16[2,4,8192]{2,1,0:T(4,128)(2,1)S(1)} %collective-permute-done.refs_1_, bf16[2,4,8192]{2,1,0:T(4,128)(2,1)S(1)} %collective-permute-done.2.refs_2_, bf16[2,4,8192]{2,1,0:T(4,128)(2,1)S(1)} %collective-permute-done.3.refs_3_, ...), custom_call_target="tpu_custom_call" | custom-call | flops 671088640 | bytes 1310720 | tf_op jit(solution)/shard_map/map_rows/pallas_call | solution.py:153
  19.9 0.0 collective-permute-done.14.refs_10_
  19.9 0.6 %collective-permute-start.11 = (bf16[2,4,8192]{2,1,0:T(4,128)(2,1)S(1)}, bf16[2,4,8192]{2,1,0:T(4,128)(2,1)S(1)}, u32[]{:S(2)}, u32[]{:S(2)}) collective-permute-start(bf16[2,4,8192]{2,1,0:T(4,128)(2,1)S(1)} %collective-permute-done.4.refs_4_), channel_id=1, source_target_pairs={{0,1},{1,0},{2,3},{3,2},{4,5},{5,4},{6,7},{7,6},{8,9},{9,8},{10,11... | collective-permute-start | bytes 393224 | tf_op jit(solution)/shard_map/ppermute | solution.py:212
  20.5 0.0 collective-permute-done.13.refs_9_
  20.5 0.1 collective-permute-start.10
  20.6 0.4 collective-permute-done.6.refs_2_
  21.0 0.0 collective-permute-start.9
  21.0 0.2 collective-permute-done.5.refs_1_
  21.2 0.3 collective-permute-start.8
  21.5 0.0 collective-permute-done.12.refs_8_
  21.5 0.2 collective-permute-start.7
  21.7 0.0 collective-permute-done.11.refs_7_
  21.7 0.1 collective-permute-done.10.refs_6_
  21.8 0.5 %collective-permute-done.9.refs_5_ = bf16[2,4,8192]{2,1,0:T(4,128)(2,1)S(1)} collective-permute-done((bf16[2,4,8192]{2,1,0:T(4,128)(2,1)S(1)}, bf16[2,4,8192]{2,1,0:T(4,128)(2,1)S(1)}, u32[]{:S(2)}, u32[]{:S(2)}) %collective-permute-start.9) | collective-permute-done | bytes 131104 | tf_op jit(solution)/shard_map/ppermute | solution.py:212
  22.3 0.2 collective-permute-done.8.refs_4_
  22.5 0.3 collective-permute-done.7.refs_3_
  22.8 1.9 %map_rows.3 = (f32[1,128]{1,0:T(1,128)S(1)}, f32[1,128]{1,0:T(1,128)S(1)}) custom-call(bf16[2,4,8192]{2,1,0:T(4,128)(2,1)S(1)} %collective-permute-done.1.refs_0_, bf16[2,4,8192]{2,1,0:T(4,128)(2,1)S(1)} %collective-permute-done.5.refs_1_, bf16[2,4,8192]{2,1,0:T(4,128)(2,1)S(1)} %collective-permute-done.6.refs_2_, ...), custom_call_target="tpu_custom_call" | custom-call | flops 1476395008 | bytes 2883584 | tf_op jit(solution)/shard_map/map_rows/pallas_call | solution.py:153
  24.7 0.3 collective-permute-start.15
  25.0 0.9 %collective-permute-done.15.came = f32[1,128]{1,0:T(1,128)S(1)} collective-permute-done((f32[1,128]{1,0:T(1,128)S(1)}, f32[1,128]{1,0:T(1,128)S(1)}, u32[]{:S(2)}, u32[]{:S(2)}) %collective-permute-start.15) | collective-permute-done | bytes 544 | tf_op jit(solution)/shard_map/ppermute | solution.py:212
  25.9 0.1 fold.3
  26.0 1.5 %collective-permute-start.16 = (f32[1,64]{1,0:T(1,128)S(1)}, f32[1,64]{1,0:T(1,128)S(1)}, u32[]{:S(2)}, u32[]{:S(2)}) collective-permute-start(f32[1,64]{1,0:T(1,128)S(1)} %get-tuple-element.48), channel_id=1, source_target_pairs={{0,2},{1,3},{2,0},{3,1},{4,6},{5,7},{6,4},{7,5},{8,10},{9,11},{10,... | collective-permute-start | bytes 776 | tf_op jit(solution)/shard_map/ppermute | solution.py:212
  27.5 2.1 %collective-permute-done.16.came = f32[1,64]{1,0:T(1,128)S(1)} collective-permute-done((f32[1,64]{1,0:T(1,128)S(1)}, f32[1,64]{1,0:T(1,128)S(1)}, u32[]{:S(2)}, u32[]{:S(2)}) %collective-permute-start.16) | collective-permute-done | bytes 288 | tf_op jit(solution)/shard_map/ppermute | solution.py:212
  29.5 0.1 fold.4
  29.6 1.6 %collective-permute-start.17 = (f32[1,32]{1,0:T(1,128)S(1)}, f32[1,32]{1,0:T(1,128)S(1)}, u32[]{:S(2)}, u32[]{:S(2)}) collective-permute-start(f32[1,32]{1,0:T(1,128)S(1)} %get-tuple-element.50), channel_id=1, source_target_pairs={{0,4},{1,5},{2,6},{3,7},{4,0},{5,1},{6,2},{7,3},{8,12},{9,13},{10,... | collective-permute-start | bytes 392 | tf_op jit(solution)/shard_map/ppermute | solution.py:212
  31.2 2.0 %collective-permute-done.17.came = f32[1,32]{1,0:T(1,128)S(1)} collective-permute-done((f32[1,32]{1,0:T(1,128)S(1)}, f32[1,32]{1,0:T(1,128)S(1)}, u32[]{:S(2)}, u32[]{:S(2)}) %collective-permute-start.17) | collective-permute-done | bytes 160 | tf_op jit(solution)/shard_map/ppermute | solution.py:212
  33.1 0.1 fold.5
  33.2 2.0 %collective-permute-start.18 = (f32[1,16]{1,0:T(1,128)S(1)}, f32[1,16]{1,0:T(1,128)S(1)}, u32[]{:S(2)}, u32[]{:S(2)}) collective-permute-start(f32[1,16]{1,0:T(1,128)S(1)} %get-tuple-element.52), channel_id=1, source_target_pairs={{0,8},{1,9},{2,10},{3,11},{4,12},{5,13},{6,14},{7,15},{8,0},{9,1},... | collective-permute-start | bytes 200 | tf_op jit(solution)/shard_map/ppermute | solution.py:212
  35.2 2.4 %collective-permute-done.18.came = f32[1,16]{1,0:T(1,128)S(1)} collective-permute-done((f32[1,16]{1,0:T(1,128)S(1)}, f32[1,16]{1,0:T(1,128)S(1)}, u32[]{:S(2)}, u32[]{:S(2)}) %collective-permute-start.18) | collective-permute-done | bytes 96 | tf_op jit(solution)/shard_map/ppermute | solution.py:212
  37.7 0.6 %finish.1 = (f32[2,4]{1,0:T(2,128)}, f32[2,4]{1,0:T(2,128)}) custom-call(f32[1,16]{1,0:T(1,128)S(1)} %get-tuple-element.51.kept, f32[1,16]{1,0:T(1,128)S(1)} %collective-permute-done.18.came, f32[1,16]{1,0:T(1,128)S(1)} %get-tuple-element.53.own), custom_call_target="tpu_custom_call" | custom-call | tf_op jit(solution)/shard_map/finish/pallas_call | solution.py:196
  (3 shorter events, 0.0 us)
Async XLA Ops:
  0.6 14.0 %copy-start = (bf16[2,4,8192]{2,1,0:T(4,128)(2,1)S(1)}, bf16[2,4,8192]{2,1,0:T(4,128)(2,1)}, u32[]{:S(2)}) copy-start(bf16[2,4,8192]{2,1,0:T(4,128)(2,1)} %refs_0_.3) | copy-start | bytes 393220
  0.6 17.6 %copy-start.2 = (f32[2,512]{1,0:T(2,128)S(1)}, f32[2,512]{1,0:T(2,128)}, u32[]{:S(2)}) copy-start(f32[2,512]{1,0:T(2,128)} %refs_15_) | copy-start | bytes 12292
  0.7 17.5 %copy-start.1 = (f32[2,512]{1,0:T(2,128)S(1)}, f32[2,512]{1,0:T(2,128)}, u32[]{:S(2)}) copy-start(f32[2,512]{1,0:T(2,128)} %refs_14_) | copy-start | bytes 12292
  0.7 11.4 %collective-permute-start = (bf16[2,4,8192]{2,1,0:T(4,128)(2,1)}, bf16[2,4,8192]{2,1,0:T(4,128)(2,1)S(1)}, u32[]{:S(2)}, u32[]{:S(2)}) collective-permute-start(bf16[2,4,8192]{2,1,0:T(4,128)(2,1)} %refs_0_.3), channel_id=1, source_target_pairs={{0,8},{1,9},{2,10},{3,11},{4,12},{5,13},{6,14},{7,15},{8,0},{9,1},... | collective-permute-start | bytes 393224 | tf_op jit(solution)/shard_map/ppermute | solution.py:212
  4.8 10.4 %collective-permute-start.4 = (bf16[2,4,8192]{2,1,0:T(4,128)(2,1)}, bf16[2,4,8192]{2,1,0:T(4,128)(2,1)S(1)}, u32[]{:S(2)}, u32[]{:S(2)}) collective-permute-start(bf16[2,4,8192]{2,1,0:T(4,128)(2,1)} %refs_0_.3), channel_id=1, source_target_pairs={{0,6},{1,7},{2,4},{3,5},{4,2},{5,3},{6,0},{7,1},{8,14},{9,15},{10,... | collective-permute-start | bytes 393224 | tf_op jit(solution)/shard_map/ppermute | solution.py:212
  7.3 7.4 %collective-permute-start.3 = (bf16[2,4,8192]{2,1,0:T(4,128)(2,1)}, bf16[2,4,8192]{2,1,0:T(4,128)(2,1)S(1)}, u32[]{:S(2)}, u32[]{:S(2)}) collective-permute-start(bf16[2,4,8192]{2,1,0:T(4,128)(2,1)} %refs_0_.3), channel_id=1, source_target_pairs={{0,2},{1,3},{2,0},{3,1},{4,6},{5,7},{6,4},{7,5},{8,10},{9,11},{10,... | collective-permute-start | bytes 393224 | tf_op jit(solution)/shard_map/ppermute | solution.py:212
  7.8 8.4 %collective-permute-start.2 = (bf16[2,4,8192]{2,1,0:T(4,128)(2,1)}, bf16[2,4,8192]{2,1,0:T(4,128)(2,1)S(1)}, u32[]{:S(2)}, u32[]{:S(2)}) collective-permute-start(bf16[2,4,8192]{2,1,0:T(4,128)(2,1)} %refs_0_.3), channel_id=1, source_target_pairs={{0,4},{1,5},{2,6},{3,7},{4,0},{5,1},{6,2},{7,3},{8,12},{9,13},{10,... | collective-permute-start | bytes 393224 | tf_op jit(solution)/shard_map/ppermute | solution.py:212
  12.1 6.1 %collective-permute-start.1 = (bf16[2,4,8192]{2,1,0:T(4,128)(2,1)S(1)}, bf16[2,4,8192]{2,1,0:T(4,128)(2,1)S(1)}, u32[]{:S(2)}, u32[]{:S(2)}) collective-permute-start(bf16[2,4,8192]{2,1,0:T(4,128)(2,1)S(1)} %collective-permute-done.refs_1_), channel_id=1, source_target_pairs={{0,6},{1,7},{2,4},{3,5},{4,2},{5,3},{6,0},{7,1},{8,14},{9,15},{10,... | collective-permute-start | bytes 393224 | tf_op jit(solution)/shard_map/ppermute | solution.py:212
  14.7 5.3 %collective-permute-start.14 = (bf16[2,4,8192]{2,1,0:T(4,128)(2,1)S(1)}, bf16[2,4,8192]{2,1,0:T(4,128)(2,1)S(1)}, u32[]{:S(2)}, u32[]{:S(2)}) collective-permute-start(bf16[2,4,8192]{2,1,0:T(4,128)(2,1)S(1)} %copy-done), channel_id=1, source_target_pairs={{0,1},{1,0},{2,3},{3,2},{4,5},{5,4},{6,7},{7,6},{8,9},{9,8},{10,11... | collective-permute-start | bytes 393224 | tf_op jit(solution)/shard_map/ppermute | solution.py:212
  14.7 5.8 %collective-permute-start.13 = (bf16[2,4,8192]{2,1,0:T(4,128)(2,1)S(1)}, bf16[2,4,8192]{2,1,0:T(4,128)(2,1)S(1)}, u32[]{:S(2)}, u32[]{:S(2)}) collective-permute-start(bf16[2,4,8192]{2,1,0:T(4,128)(2,1)S(1)} %collective-permute-done.3.refs_3_), channel_id=1, source_target_pairs={{0,1},{1,0},{2,3},{3,2},{4,5},{5,4},{6,7},{7,6},{8,9},{9,8},{10,11... | collective-permute-start | bytes 393224 | tf_op jit(solution)/shard_map/ppermute | solution.py:212
  15.2 5.8 %collective-permute-start.6 = (bf16[2,4,8192]{2,1,0:T(4,128)(2,1)S(1)}, bf16[2,4,8192]{2,1,0:T(4,128)(2,1)S(1)}, u32[]{:S(2)}, u32[]{:S(2)}) collective-permute-start(bf16[2,4,8192]{2,1,0:T(4,128)(2,1)S(1)} %collective-permute-done.refs_1_), channel_id=1, source_target_pairs={{0,2},{1,3},{2,0},{3,1},{4,6},{5,7},{6,4},{7,5},{8,10},{9,11},{10,... | collective-permute-start | bytes 393224 | tf_op jit(solution)/shard_map/ppermute | solution.py:212
  16.2 5.0 %collective-permute-start.5 = (bf16[2,4,8192]{2,1,0:T(4,128)(2,1)S(1)}, bf16[2,4,8192]{2,1,0:T(4,128)(2,1)S(1)}, u32[]{:S(2)}, u32[]{:S(2)}) collective-permute-start(bf16[2,4,8192]{2,1,0:T(4,128)(2,1)S(1)} %collective-permute-done.refs_1_), channel_id=1, source_target_pairs={{0,4},{1,5},{2,6},{3,7},{4,0},{5,1},{6,2},{7,3},{8,12},{9,13},{10,... | collective-permute-start | bytes 393224 | tf_op jit(solution)/shard_map/ppermute | solution.py:212
  18.2 3.3 %collective-permute-start.12 = (bf16[2,4,8192]{2,1,0:T(4,128)(2,1)S(1)}, bf16[2,4,8192]{2,1,0:T(4,128)(2,1)S(1)}, u32[]{:S(2)}, u32[]{:S(2)}) collective-permute-start(bf16[2,4,8192]{2,1,0:T(4,128)(2,1)S(1)} %collective-permute-done.2.refs_2_), channel_id=1, source_target_pairs={{0,1},{1,0},{2,3},{3,2},{4,5},{5,4},{6,7},{7,6},{8,9},{9,8},{10,11... | collective-permute-start | bytes 393224 | tf_op jit(solution)/shard_map/ppermute | solution.py:212
  19.9 1.8 %collective-permute-start.11 = (bf16[2,4,8192]{2,1,0:T(4,128)(2,1)S(1)}, bf16[2,4,8192]{2,1,0:T(4,128)(2,1)S(1)}, u32[]{:S(2)}, u32[]{:S(2)}) collective-permute-start(bf16[2,4,8192]{2,1,0:T(4,128)(2,1)S(1)} %collective-permute-done.4.refs_4_), channel_id=1, source_target_pairs={{0,1},{1,0},{2,3},{3,2},{4,5},{5,4},{6,7},{7,6},{8,9},{9,8},{10,11... | collective-permute-start | bytes 393224 | tf_op jit(solution)/shard_map/ppermute | solution.py:212
  20.5 1.3 %collective-permute-start.10 = (bf16[2,4,8192]{2,1,0:T(4,128)(2,1)S(1)}, bf16[2,4,8192]{2,1,0:T(4,128)(2,1)S(1)}, u32[]{:S(2)}, u32[]{:S(2)}) collective-permute-start(bf16[2,4,8192]{2,1,0:T(4,128)(2,1)S(1)} %collective-permute-done.refs_1_), channel_id=1, source_target_pairs={{0,1},{1,0},{2,3},{3,2},{4,5},{5,4},{6,7},{7,6},{8,9},{9,8},{10,11... | collective-permute-start | bytes 393224 | tf_op jit(solution)/shard_map/ppermute | solution.py:212
  21.0 1.3 %collective-permute-start.9 = (bf16[2,4,8192]{2,1,0:T(4,128)(2,1)S(1)}, bf16[2,4,8192]{2,1,0:T(4,128)(2,1)S(1)}, u32[]{:S(2)}, u32[]{:S(2)}) collective-permute-start(bf16[2,4,8192]{2,1,0:T(4,128)(2,1)S(1)} %collective-permute-done.6.refs_2_), channel_id=1, source_target_pairs={{0,1},{1,0},{2,3},{3,2},{4,5},{5,4},{6,7},{7,6},{8,9},{9,8},{10,11... | collective-permute-start | bytes 393224 | tf_op jit(solution)/shard_map/ppermute | solution.py:212
  21.2 1.3 %collective-permute-start.8 = (bf16[2,4,8192]{2,1,0:T(4,128)(2,1)S(1)}, bf16[2,4,8192]{2,1,0:T(4,128)(2,1)S(1)}, u32[]{:S(2)}, u32[]{:S(2)}) collective-permute-start(bf16[2,4,8192]{2,1,0:T(4,128)(2,1)S(1)} %collective-permute-done.5.refs_1_), channel_id=1, source_target_pairs={{0,1},{1,0},{2,3},{3,2},{4,5},{5,4},{6,7},{7,6},{8,9},{9,8},{10,11... | collective-permute-start | bytes 393224 | tf_op jit(solution)/shard_map/ppermute | solution.py:212
  21.5 1.3 %collective-permute-start.7 = (bf16[2,4,8192]{2,1,0:T(4,128)(2,1)S(1)}, bf16[2,4,8192]{2,1,0:T(4,128)(2,1)S(1)}, u32[]{:S(2)}, u32[]{:S(2)}) collective-permute-start(bf16[2,4,8192]{2,1,0:T(4,128)(2,1)S(1)} %collective-permute-done.1.refs_0_), channel_id=1, source_target_pairs={{0,1},{1,0},{2,3},{3,2},{4,5},{5,4},{6,7},{7,6},{8,9},{9,8},{10,11... | collective-permute-start | bytes 393224 | tf_op jit(solution)/shard_map/ppermute | solution.py:212
  24.7 1.2 %collective-permute-start.15 = (f32[1,128]{1,0:T(1,128)S(1)}, f32[1,128]{1,0:T(1,128)S(1)}, u32[]{:S(2)}, u32[]{:S(2)}) collective-permute-start(f32[1,128]{1,0:T(1,128)S(1)} %get-tuple-element.46), channel_id=1, source_target_pairs={{0,1},{1,0},{2,3},{3,2},{4,5},{5,4},{6,7},{7,6},{8,9},{9,8},{10,11... | collective-permute-start | bytes 1544 | tf_op jit(solution)/shard_map/ppermute | solution.py:212
  26.0 3.5 %collective-permute-start.16 = (f32[1,64]{1,0:T(1,128)S(1)}, f32[1,64]{1,0:T(1,128)S(1)}, u32[]{:S(2)}, u32[]{:S(2)}) collective-permute-start(f32[1,64]{1,0:T(1,128)S(1)} %get-tuple-element.48), channel_id=1, source_target_pairs={{0,2},{1,3},{2,0},{3,1},{4,6},{5,7},{6,4},{7,5},{8,10},{9,11},{10,... | collective-permute-start | bytes 776 | tf_op jit(solution)/shard_map/ppermute | solution.py:212
  29.6 3.5 %collective-permute-start.17 = (f32[1,32]{1,0:T(1,128)S(1)}, f32[1,32]{1,0:T(1,128)S(1)}, u32[]{:S(2)}, u32[]{:S(2)}) collective-permute-start(f32[1,32]{1,0:T(1,128)S(1)} %get-tuple-element.50), channel_id=1, source_target_pairs={{0,4},{1,5},{2,6},{3,7},{4,0},{5,1},{6,2},{7,3},{8,12},{9,13},{10,... | collective-permute-start | bytes 392 | tf_op jit(solution)/shard_map/ppermute | solution.py:212
  33.2 4.4 %collective-permute-start.18 = (f32[1,16]{1,0:T(1,128)S(1)}, f32[1,16]{1,0:T(1,128)S(1)}, u32[]{:S(2)}, u32[]{:S(2)}) collective-permute-start(f32[1,16]{1,0:T(1,128)S(1)} %get-tuple-element.52), channel_id=1, source_target_pairs={{0,8},{1,9},{2,10},{3,11},{4,12},{5,13},{6,14},{7,15},{8,0},{9,1},... | collective-permute-start | bytes 200 | tf_op jit(solution)/shard_map/ppermute | solution.py:212

commit v7 on v5

--- a/solution.py
+++ b/solution.py
@@ -233,6 +233,8 @@
             pieces[mask] = swap(pieces[mask - 1], 1)
     first = map_rows([pieces[m] for m in early], args)
     pieces[highs[-1] + 6], first = lax.optimization_barrier((pieces[highs[-1] + 6], first))
+    for mask in (8, 6):
+        pieces[mask], first = lax.optimization_barrier((pieces[mask], first))
     for mask in range(0, num_devices, 2):
         if mask + 1 not in pieces:
             pieces[mask + 1] = swap(pieces[mask], 1)

time: 38.4 us -> 38.4 us (level)
  transfers between devices with their start and end apart: 19 -> 19, of which waited for: 12 -> 11; matrix products, arithmetic and copies ran while one was open for 0% -> 0% of each run, Pallas kernels for 14% -> 14%
where the time goes in v7:
time: 38.4 us; the launch traced here: 38.3 us
  starting transfers between devices  17.8 us (46%)
  waiting for transfers between devices  11.5 us (30%)
  Pallas kernels  8.25 us (21%)
  between operations  0.72 us (2%)
    ppermute x19, starting transfers between devices, swap(): lax.ppermute(array, 'row', [(i, i ^ mask) for i in range(num_devices)])  17.8 us
    ppermute x19, waiting for transfers between devices, swap(): lax.ppermute(array, 'row', [(i, i ^ mask) for i in range(num_devices)])  11.5 us
    pallas_call x1, Pallas kernels, prep(): pl.pallas_call(prep_kernel, in_specs=[pl.BlockSpec(memory_space=pltpu.HBM...  3.79 us
    pallas_call x2, Pallas kernels, map_rows(): pl.pallas_call(kernel, in_specs=[VMEM] * (len(pieces) + len(args) + len(m...  3.61 us
  transfers between devices with their start and end apart: 19, of which 11 were waited for; matrix products, arithmetic and copies ran while one was open for 0% of the time, Pallas kernels for 14%

profile of v7, /device:TPU:0, one launch (start us, length us, event | category | flops | bytes accessed | tf_op | source)
XLA Modules:
  0.0 38.3 jit_solution(10345824964670577647)
XLA Ops:
  0.6 0.0 copy-start
  0.6 0.0 copy-start.2
  0.7 0.0 copy-start.1
  0.7 4.1 %collective-permute-start = (bf16[2,4,8192]{2,1,0:T(4,128)(2,1)}, bf16[2,4,8192]{2,1,0:T(4,128)(2,1)S(1)}, u32[]{:S(2)}, u32[]{:S(2)}) collective-permute-start(bf16[2,4,8192]{2,1,0:T(4,128)(2,1)} %refs_0_.3), channel_id=1, source_target_pairs={{0,8},{1,9},{2,10},{3,11},{4,12},{5,13},{6,14},{7,15},{8,0},{9,1},... | collective-permute-start | bytes 393224 | tf_op jit(solution)/shard_map/ppermute | solution.py:211
  4.8 2.5 %collective-permute-start.4 = (bf16[2,4,8192]{2,1,0:T(4,128)(2,1)}, bf16[2,4,8192]{2,1,0:T(4,128)(2,1)S(1)}, u32[]{:S(2)}, u32[]{:S(2)}) collective-permute-start(bf16[2,4,8192]{2,1,0:T(4,128)(2,1)} %refs_0_.3), channel_id=1, source_target_pairs={{0,6},{1,7},{2,4},{3,5},{4,2},{5,3},{6,0},{7,1},{8,14},{9,15},{10,... | collective-permute-start | bytes 393224 | tf_op jit(solution)/shard_map/ppermute | solution.py:211
  7.3 0.5 %collective-permute-start.3 = (bf16[2,4,8192]{2,1,0:T(4,128)(2,1)}, bf16[2,4,8192]{2,1,0:T(4,128)(2,1)S(1)}, u32[]{:S(2)}, u32[]{:S(2)}) collective-permute-start(bf16[2,4,8192]{2,1,0:T(4,128)(2,1)} %refs_0_.3), channel_id=1, source_target_pairs={{0,2},{1,3},{2,0},{3,1},{4,6},{5,7},{6,4},{7,5},{8,10},{9,11},{10,... | collective-permute-start | bytes 393224 | tf_op jit(solution)/shard_map/ppermute | solution.py:211
  7.8 0.4 %collective-permute-start.2 = (bf16[2,4,8192]{2,1,0:T(4,128)(2,1)}, bf16[2,4,8192]{2,1,0:T(4,128)(2,1)S(1)}, u32[]{:S(2)}, u32[]{:S(2)}) collective-permute-start(bf16[2,4,8192]{2,1,0:T(4,128)(2,1)} %refs_0_.3), channel_id=1, source_target_pairs={{0,4},{1,5},{2,6},{3,7},{4,0},{5,1},{6,2},{7,3},{8,12},{9,13},{10,... | collective-permute-start | bytes 393224 | tf_op jit(solution)/shard_map/ppermute | solution.py:211
  8.3 3.8 %prep.1 = (f32[8,8192]{1,0:T(8,128)S(1)}, f32[8,8192]{1,0:T(8,128)S(1)}, f32[1,16]{1,0:T(1,128)S(1)}, bf16[8192,512]{1,0:T(8,128)(2,1)S(1)}) custom-call(bf16[2,4,8192]{2,1,0:T(4,128)(2,1)} %refs_0_.3, s32[2,8192]{1,0:T(2,128)} %refs_1_.1, s32[2,8192]{1,0:T(2,128)} %refs_2_.1, f32[2,8192]{1,0:T(2,128)} %refs_3_.1, f32[2,8192]{1,0:T(2,128)} %refs_4_.1, ...), custom_call_target="tpu_custom_call" | custom-call | flops 1310720 | bytes 9175040 | tf_op jit(solution)/shard_map/prep/pallas_call | solution.py:76
  12.1 0.0 collective-permute-done.refs_1_
  12.1 2.6 %collective-permute-start.1 = (bf16[2,4,8192]{2,1,0:T(4,128)(2,1)S(1)}, bf16[2,4,8192]{2,1,0:T(4,128)(2,1)S(1)}, u32[]{:S(2)}, u32[]{:S(2)}) collective-permute-start(bf16[2,4,8192]{2,1,0:T(4,128)(2,1)S(1)} %collective-permute-done.refs_1_), channel_id=1, source_target_pairs={{0,6},{1,7},{2,4},{3,5},{4,2},{5,3},{6,0},{7,1},{8,14},{9,15},{10,... | collective-permute-start | bytes 393224 | tf_op jit(solution)/shard_map/ppermute | solution.py:211
  14.7 0.0 collective-permute-start.14
  14.7 0.0 collective-permute-done.3.refs_3_
  14.7 0.5 %collective-permute-start.13 = (bf16[2,4,8192]{2,1,0:T(4,128)(2,1)S(1)}, bf16[2,4,8192]{2,1,0:T(4,128)(2,1)S(1)}, u32[]{:S(2)}, u32[]{:S(2)}) collective-permute-start(bf16[2,4,8192]{2,1,0:T(4,128)(2,1)S(1)} %collective-permute-done.3.refs_3_), channel_id=1, source_target_pairs={{0,1},{1,0},{2,3},{3,2},{4,5},{5,4},{6,7},{7,6},{8,9},{9,8},{10,11... | collective-permute-start | bytes 393224 | tf_op jit(solution)/shard_map/ppermute | solution.py:211
  15.2 0.0 collective-permute-done.4.refs_4_
  15.2 0.5 %collective-permute-start.6 = (bf16[2,4,8192]{2,1,0:T(4,128)(2,1)S(1)}, bf16[2,4,8192]{2,1,0:T(4,128)(2,1)S(1)}, u32[]{:S(2)}, u32[]{:S(2)}) collective-permute-start(bf16[2,4,8192]{2,1,0:T(4,128)(2,1)S(1)} %collective-permute-done.refs_1_), channel_id=1, source_target_pairs={{0,2},{1,3},{2,0},{3,1},{4,6},{5,7},{6,4},{7,5},{8,10},{9,11},{10,... | collective-permute-start | bytes 393224 | tf_op jit(solution)/shard_map/ppermute | solution.py:211
  15.7 0.5 %collective-permute-done.2.refs_2_ = bf16[2,4,8192]{2,1,0:T(4,128)(2,1)S(1)} collective-permute-done((bf16[2,4,8192]{2,1,0:T(4,128)(2,1)}, bf16[2,4,8192]{2,1,0:T(4,128)(2,1)S(1)}, u32[]{:S(2)}, u32[]{:S(2)}) %collective-permute-start.2) | collective-permute-done | bytes 131104 | tf_op jit(solution)/shard_map/ppermute | solution.py:211
  16.2 0.0 collective-permute-start.5
  16.2 2.0 %collective-permute-done.1.refs_0_ = bf16[2,4,8192]{2,1,0:T(4,128)(2,1)S(1)} collective-permute-done((bf16[2,4,8192]{2,1,0:T(4,128)(2,1)S(1)}, bf16[2,4,8192]{2,1,0:T(4,128)(2,1)S(1)}, u32[]{:S(2)}, u32[]{:S(2)}) %collective-permute-start.1) | collective-permute-done | bytes 131104 | tf_op jit(solution)/shard_map/ppermute | solution.py:211
  18.2 0.0 collective-permute-start.12
  18.2 1.7 %map_rows.2.refs_16_ = f32[1,80]{1,0:T(1,128)S(1)} custom-call(bf16[2,4,8192]{2,1,0:T(4,128)(2,1)S(1)} %copy-done, bf16[2,4,8192]{2,1,0:T(4,128)(2,1)S(1)} %collective-permute-done.refs_1_, bf16[2,4,8192]{2,1,0:T(4,128)(2,1)S(1)} %collective-permute-done.2.refs_2_, bf16[2,4,8192]{2,1,0:T(4,128)(2,1)S(1)} %collective-permute-done.3.refs_3_, ...), custom_call_target="tpu_custom_call" | custom-call | flops 671088640 | bytes 1310720 | tf_op jit(solution)/shard_map/map_rows/pallas_call | solution.py:152
  19.9 0.0 collective-permute-done.14.refs_10_
  19.9 0.6 %collective-permute-start.11 = (bf16[2,4,8192]{2,1,0:T(4,128)(2,1)S(1)}, bf16[2,4,8192]{2,1,0:T(4,128)(2,1)S(1)}, u32[]{:S(2)}, u32[]{:S(2)}) collective-permute-start(bf16[2,4,8192]{2,1,0:T(4,128)(2,1)S(1)} %collective-permute-done.4.refs_4_), channel_id=1, source_target_pairs={{0,1},{1,0},{2,3},{3,2},{4,5},{5,4},{6,7},{7,6},{8,9},{9,8},{10,11... | collective-permute-start | bytes 393224 | tf_op jit(solution)/shard_map/ppermute | solution.py:211
  20.5 0.0 collective-permute-done.13.refs_9_
  20.5 0.1 collective-permute-start.10
  20.6 0.4 collective-permute-done.6.refs_2_
  21.0 0.1 collective-permute-start.9
  21.0 0.2 collective-permute-done.5.refs_1_
  21.2 0.3 collective-permute-start.8
  21.5 0.0 collective-permute-done.12.refs_8_
  21.5 0.2 collective-permute-start.7
  21.7 0.6 %collective-permute-done.9.refs_5_ = bf16[2,4,8192]{2,1,0:T(4,128)(2,1)S(1)} collective-permute-done((bf16[2,4,8192]{2,1,0:T(4,128)(2,1)S(1)}, bf16[2,4,8192]{2,1,0:T(4,128)(2,1)S(1)}, u32[]{:S(2)}, u32[]{:S(2)}) %collective-permute-start.9) | collective-permute-done | bytes 131104 | tf_op jit(solution)/shard_map/ppermute | solution.py:211
  22.3 0.2 collective-permute-done.8.refs_4_
  22.5 0.0 collective-permute-done.11.refs_7_
  22.5 0.0 collective-permute-done.10.refs_6_
  22.6 0.3 collective-permute-done.7.refs_3_
  22.8 1.9 %map_rows.3 = (f32[1,128]{1,0:T(1,128)S(1)}, f32[1,128]{1,0:T(1,128)S(1)}) custom-call(bf16[2,4,8192]{2,1,0:T(4,128)(2,1)S(1)} %collective-permute-done.1.refs_0_, bf16[2,4,8192]{2,1,0:T(4,128)(2,1)S(1)} %collective-permute-done.5.refs_1_, bf16[2,4,8192]{2,1,0:T(4,128)(2,1)S(1)} %collective-permute-done.6.refs_2_, ...), custom_call_target="tpu_custom_call" | custom-call | flops 1476395008 | bytes 2883584 | tf_op jit(solution)/shard_map/map_rows/pallas_call | solution.py:152
  24.7 0.3 collective-permute-start.15
  25.0 0.9 %collective-permute-done.15.came = f32[1,128]{1,0:T(1,128)S(1)} collective-permute-done((f32[1,128]{1,0:T(1,128)S(1)}, f32[1,128]{1,0:T(1,128)S(1)}, u32[]{:S(2)}, u32[]{:S(2)}) %collective-permute-start.15) | collective-permute-done | bytes 544 | tf_op jit(solution)/shard_map/ppermute | solution.py:211
  25.9 0.1 fold.3
  26.0 1.5 %collective-permute-start.16 = (f32[1,64]{1,0:T(1,128)S(1)}, f32[1,64]{1,0:T(1,128)S(1)}, u32[]{:S(2)}, u32[]{:S(2)}) collective-permute-start(f32[1,64]{1,0:T(1,128)S(1)} %get-tuple-element.44), channel_id=1, source_target_pairs={{0,2},{1,3},{2,0},{3,1},{4,6},{5,7},{6,4},{7,5},{8,10},{9,11},{10,... | collective-permute-start | bytes 776 | tf_op jit(solution)/shard_map/ppermute | solution.py:211
  27.4 2.1 %collective-permute-done.16.came = f32[1,64]{1,0:T(1,128)S(1)} collective-permute-done((f32[1,64]{1,0:T(1,128)S(1)}, f32[1,64]{1,0:T(1,128)S(1)}, u32[]{:S(2)}, u32[]{:S(2)}) %collective-permute-start.16) | collective-permute-done | bytes 288 | tf_op jit(solution)/shard_map/ppermute | solution.py:211
  29.5 0.1 fold.4
  29.6 1.6 %collective-permute-start.17 = (f32[1,32]{1,0:T(1,128)S(1)}, f32[1,32]{1,0:T(1,128)S(1)}, u32[]{:S(2)}, u32[]{:S(2)}) collective-permute-start(f32[1,32]{1,0:T(1,128)S(1)} %get-tuple-element.46), channel_id=1, source_target_pairs={{0,4},{1,5},{2,6},{3,7},{4,0},{5,1},{6,2},{7,3},{8,12},{9,13},{10,... | collective-permute-start | bytes 392 | tf_op jit(solution)/shard_map/ppermute | solution.py:211
  31.2 2.0 %collective-permute-done.17.came = f32[1,32]{1,0:T(1,128)S(1)} collective-permute-done((f32[1,32]{1,0:T(1,128)S(1)}, f32[1,32]{1,0:T(1,128)S(1)}, u32[]{:S(2)}, u32[]{:S(2)}) %collective-permute-start.17) | collective-permute-done | bytes 160 | tf_op jit(solution)/shard_map/ppermute | solution.py:211
  33.1 0.1 fold.5
  33.2 2.0 %collective-permute-start.18 = (f32[1,16]{1,0:T(1,128)S(1)}, f32[1,16]{1,0:T(1,128)S(1)}, u32[]{:S(2)}, u32[]{:S(2)}) collective-permute-start(f32[1,16]{1,0:T(1,128)S(1)} %get-tuple-element.48), channel_id=1, source_target_pairs={{0,8},{1,9},{2,10},{3,11},{4,12},{5,13},{6,14},{7,15},{8,0},{9,1},... | collective-permute-start | bytes 200 | tf_op jit(solution)/shard_map/ppermute | solution.py:211
  35.3 2.4 %collective-permute-done.18.came = f32[1,16]{1,0:T(1,128)S(1)} collective-permute-done((f32[1,16]{1,0:T(1,128)S(1)}, f32[1,16]{1,0:T(1,128)S(1)}, u32[]{:S(2)}, u32[]{:S(2)}) %collective-permute-start.18) | collective-permute-done | bytes 96 | tf_op jit(solution)/shard_map/ppermute | solution.py:211
  37.7 0.6 %finish.1 = (f32[2,4]{1,0:T(2,128)}, f32[2,4]{1,0:T(2,128)}) custom-call(f32[1,16]{1,0:T(1,128)S(1)} %get-tuple-element.47.kept, f32[1,16]{1,0:T(1,128)S(1)} %collective-permute-done.18.came, f32[1,16]{1,0:T(1,128)S(1)} %get-tuple-element.49.own), custom_call_target="tpu_custom_call" | custom-call | tf_op jit(solution)/shard_map/finish/pallas_call | solution.py:195
  (3 shorter events, 0.0 us)
Async XLA Ops:
  0.6 14.0 %copy-start = (bf16[2,4,8192]{2,1,0:T(4,128)(2,1)S(1)}, bf16[2,4,8192]{2,1,0:T(4,128)(2,1)}, u32[]{:S(2)}) copy-start(bf16[2,4,8192]{2,1,0:T(4,128)(2,1)} %refs_0_.3) | copy-start | bytes 393220
  0.6 17.6 %copy-start.2 = (f32[2,512]{1,0:T(2,128)S(1)}, f32[2,512]{1,0:T(2,128)}, u32[]{:S(2)}) copy-start(f32[2,512]{1,0:T(2,128)} %refs_15_) | copy-start | bytes 12292
  0.7 17.5 %copy-start.1 = (f32[2,512]{1,0:T(2,128)S(1)}, f32[2,512]{1,0:T(2,128)}, u32[]{:S(2)}) copy-start(f32[2,512]{1,0:T(2,128)} %refs_14_) | copy-start | bytes 12292
  0.7 11.4 %collective-permute-start = (bf16[2,4,8192]{2,1,0:T(4,128)(2,1)}, bf16[2,4,8192]{2,1,0:T(4,128)(2,1)S(1)}, u32[]{:S(2)}, u32[]{:S(2)}) collective-permute-start(bf16[2,4,8192]{2,1,0:T(4,128)(2,1)} %refs_0_.3), channel_id=1, source_target_pairs={{0,8},{1,9},{2,10},{3,11},{4,12},{5,13},{6,14},{7,15},{8,0},{9,1},... | collective-permute-start | bytes 393224 | tf_op jit(solution)/shard_map/ppermute | solution.py:211
  4.8 10.4 %collective-permute-start.4 = (bf16[2,4,8192]{2,1,0:T(4,128)(2,1)}, bf16[2,4,8192]{2,1,0:T(4,128)(2,1)S(1)}, u32[]{:S(2)}, u32[]{:S(2)}) collective-permute-start(bf16[2,4,8192]{2,1,0:T(4,128)(2,1)} %refs_0_.3), channel_id=1, source_target_pairs={{0,6},{1,7},{2,4},{3,5},{4,2},{5,3},{6,0},{7,1},{8,14},{9,15},{10,... | collective-permute-start | bytes 393224 | tf_op jit(solution)/shard_map/ppermute | solution.py:211
  7.3 7.4 %collective-permute-start.3 = (bf16[2,4,8192]{2,1,0:T(4,128)(2,1)}, bf16[2,4,8192]{2,1,0:T(4,128)(2,1)S(1)}, u32[]{:S(2)}, u32[]{:S(2)}) collective-permute-start(bf16[2,4,8192]{2,1,0:T(4,128)(2,1)} %refs_0_.3), channel_id=1, source_target_pairs={{0,2},{1,3},{2,0},{3,1},{4,6},{5,7},{6,4},{7,5},{8,10},{9,11},{10,... | collective-permute-start | bytes 393224 | tf_op jit(solution)/shard_map/ppermute | solution.py:211
  7.8 8.4 %collective-permute-start.2 = (bf16[2,4,8192]{2,1,0:T(4,128)(2,1)}, bf16[2,4,8192]{2,1,0:T(4,128)(2,1)S(1)}, u32[]{:S(2)}, u32[]{:S(2)}) collective-permute-start(bf16[2,4,8192]{2,1,0:T(4,128)(2,1)} %refs_0_.3), channel_id=1, source_target_pairs={{0,4},{1,5},{2,6},{3,7},{4,0},{5,1},{6,2},{7,3},{8,12},{9,13},{10,... | collective-permute-start | bytes 393224 | tf_op jit(solution)/shard_map/ppermute | solution.py:211
  12.1 6.1 %collective-permute-start.1 = (bf16[2,4,8192]{2,1,0:T(4,128)(2,1)S(1)}, bf16[2,4,8192]{2,1,0:T(4,128)(2,1)S(1)}, u32[]{:S(2)}, u32[]{:S(2)}) collective-permute-start(bf16[2,4,8192]{2,1,0:T(4,128)(2,1)S(1)} %collective-permute-done.refs_1_), channel_id=1, source_target_pairs={{0,6},{1,7},{2,4},{3,5},{4,2},{5,3},{6,0},{7,1},{8,14},{9,15},{10,... | collective-permute-start | bytes 393224 | tf_op jit(solution)/shard_map/ppermute | solution.py:211
  14.7 5.3 %collective-permute-start.14 = (bf16[2,4,8192]{2,1,0:T(4,128)(2,1)S(1)}, bf16[2,4,8192]{2,1,0:T(4,128)(2,1)S(1)}, u32[]{:S(2)}, u32[]{:S(2)}) collective-permute-start(bf16[2,4,8192]{2,1,0:T(4,128)(2,1)S(1)} %copy-done), channel_id=1, source_target_pairs={{0,1},{1,0},{2,3},{3,2},{4,5},{5,4},{6,7},{7,6},{8,9},{9,8},{10,11... | collective-permute-start | bytes 393224 | tf_op jit(solution)/shard_map/ppermute | solution.py:211
  14.7 5.8 %collective-permute-start.13 = (bf16[2,4,8192]{2,1,0:T(4,128)(2,1)S(1)}, bf16[2,4,8192]{2,1,0:T(4,128)(2,1)S(1)}, u32[]{:S(2)}, u32[]{:S(2)}) collective-permute-start(bf16[2,4,8192]{2,1,0:T(4,128)(2,1)S(1)} %collective-permute-done.3.refs_3_), channel_id=1, source_target_pairs={{0,1},{1,0},{2,3},{3,2},{4,5},{5,4},{6,7},{7,6},{8,9},{9,8},{10,11... | collective-permute-start | bytes 393224 | tf_op jit(solution)/shard_map/ppermute | solution.py:211
  15.2 5.8 %collective-permute-start.6 = (bf16[2,4,8192]{2,1,0:T(4,128)(2,1)S(1)}, bf16[2,4,8192]{2,1,0:T(4,128)(2,1)S(1)}, u32[]{:S(2)}, u32[]{:S(2)}) collective-permute-start(bf16[2,4,8192]{2,1,0:T(4,128)(2,1)S(1)} %collective-permute-done.refs_1_), channel_id=1, source_target_pairs={{0,2},{1,3},{2,0},{3,1},{4,6},{5,7},{6,4},{7,5},{8,10},{9,11},{10,... | collective-permute-start | bytes 393224 | tf_op jit(solution)/shard_map/ppermute | solution.py:211
  16.2 5.0 %collective-permute-start.5 = (bf16[2,4,8192]{2,1,0:T(4,128)(2,1)S(1)}, bf16[2,4,8192]{2,1,0:T(4,128)(2,1)S(1)}, u32[]{:S(2)}, u32[]{:S(2)}) collective-permute-start(bf16[2,4,8192]{2,1,0:T(4,128)(2,1)S(1)} %collective-permute-done.refs_1_), channel_id=1, source_target_pairs={{0,4},{1,5},{2,6},{3,7},{4,0},{5,1},{6,2},{7,3},{8,12},{9,13},{10,... | collective-permute-start | bytes 393224 | tf_op jit(solution)/shard_map/ppermute | solution.py:211
  18.2 3.3 %collective-permute-start.12 = (bf16[2,4,8192]{2,1,0:T(4,128)(2,1)S(1)}, bf16[2,4,8192]{2,1,0:T(4,128)(2,1)S(1)}, u32[]{:S(2)}, u32[]{:S(2)}) collective-permute-start(bf16[2,4,8192]{2,1,0:T(4,128)(2,1)S(1)} %collective-permute-done.2.refs_2_), channel_id=1, source_target_pairs={{0,1},{1,0},{2,3},{3,2},{4,5},{5,4},{6,7},{7,6},{8,9},{9,8},{10,11... | collective-permute-start | bytes 393224 | tf_op jit(solution)/shard_map/ppermute | solution.py:211
  19.9 2.6 %collective-permute-start.11 = (bf16[2,4,8192]{2,1,0:T(4,128)(2,1)S(1)}, bf16[2,4,8192]{2,1,0:T(4,128)(2,1)S(1)}, u32[]{:S(2)}, u32[]{:S(2)}) collective-permute-start(bf16[2,4,8192]{2,1,0:T(4,128)(2,1)S(1)} %collective-permute-done.4.refs_4_), channel_id=1, source_target_pairs={{0,1},{1,0},{2,3},{3,2},{4,5},{5,4},{6,7},{7,6},{8,9},{9,8},{10,11... | collective-permute-start | bytes 393224 | tf_op jit(solution)/shard_map/ppermute | solution.py:211
  20.5 2.0 %collective-permute-start.10 = (bf16[2,4,8192]{2,1,0:T(4,128)(2,1)S(1)}, bf16[2,4,8192]{2,1,0:T(4,128)(2,1)S(1)}, u32[]{:S(2)}, u32[]{:S(2)}) collective-permute-start(bf16[2,4,8192]{2,1,0:T(4,128)(2,1)S(1)} %collective-permute-done.refs_1_), channel_id=1, source_target_pairs={{0,1},{1,0},{2,3},{3,2},{4,5},{5,4},{6,7},{7,6},{8,9},{9,8},{10,11... | collective-permute-start | bytes 393224 | tf_op jit(solution)/shard_map/ppermute | solution.py:211
  21.0 1.3 %collective-permute-start.9 = (bf16[2,4,8192]{2,1,0:T(4,128)(2,1)S(1)}, bf16[2,4,8192]{2,1,0:T(4,128)(2,1)S(1)}, u32[]{:S(2)}, u32[]{:S(2)}) collective-permute-start(bf16[2,4,8192]{2,1,0:T(4,128)(2,1)S(1)} %collective-permute-done.6.refs_2_), channel_id=1, source_target_pairs={{0,1},{1,0},{2,3},{3,2},{4,5},{5,4},{6,7},{7,6},{8,9},{9,8},{10,11... | collective-permute-start | bytes 393224 | tf_op jit(solution)/shard_map/ppermute | solution.py:211
  21.2 1.3 %collective-permute-start.8 = (bf16[2,4,8192]{2,1,0:T(4,128)(2,1)S(1)}, bf16[2,4,8192]{2,1,0:T(4,128)(2,1)S(1)}, u32[]{:S(2)}, u32[]{:S(2)}) collective-permute-start(bf16[2,4,8192]{2,1,0:T(4,128)(2,1)S(1)} %collective-permute-done.5.refs_1_), channel_id=1, source_target_pairs={{0,1},{1,0},{2,3},{3,2},{4,5},{5,4},{6,7},{7,6},{8,9},{9,8},{10,11... | collective-permute-start | bytes 393224 | tf_op jit(solution)/shard_map/ppermute | solution.py:211
  21.5 1.3 %collective-permute-start.7 = (bf16[2,4,8192]{2,1,0:T(4,128)(2,1)S(1)}, bf16[2,4,8192]{2,1,0:T(4,128)(2,1)S(1)}, u32[]{:S(2)}, u32[]{:S(2)}) collective-permute-start(bf16[2,4,8192]{2,1,0:T(4,128)(2,1)S(1)} %collective-permute-done.1.refs_0_), channel_id=1, source_target_pairs={{0,1},{1,0},{2,3},{3,2},{4,5},{5,4},{6,7},{7,6},{8,9},{9,8},{10,11... | collective-permute-start | bytes 393224 | tf_op jit(solution)/shard_map/ppermute | solution.py:211
  24.7 1.2 %collective-permute-start.15 = (f32[1,128]{1,0:T(1,128)S(1)}, f32[1,128]{1,0:T(1,128)S(1)}, u32[]{:S(2)}, u32[]{:S(2)}) collective-permute-start(f32[1,128]{1,0:T(1,128)S(1)} %get-tuple-element.42), channel_id=1, source_target_pairs={{0,1},{1,0},{2,3},{3,2},{4,5},{5,4},{6,7},{7,6},{8,9},{9,8},{10,11... | collective-permute-start | bytes 1544 | tf_op jit(solution)/shard_map/ppermute | solution.py:211
  26.0 3.5 %collective-permute-start.16 = (f32[1,64]{1,0:T(1,128)S(1)}, f32[1,64]{1,0:T(1,128)S(1)}, u32[]{:S(2)}, u32[]{:S(2)}) collective-permute-start(f32[1,64]{1,0:T(1,128)S(1)} %get-tuple-element.44), channel_id=1, source_target_pairs={{0,2},{1,3},{2,0},{3,1},{4,6},{5,7},{6,4},{7,5},{8,10},{9,11},{10,... | collective-permute-start | bytes 776 | tf_op jit(solution)/shard_map/ppermute | solution.py:211
  29.6 3.5 %collective-permute-start.17 = (f32[1,32]{1,0:T(1,128)S(1)}, f32[1,32]{1,0:T(1,128)S(1)}, u32[]{:S(2)}, u32[]{:S(2)}) collective-permute-start(f32[1,32]{1,0:T(1,128)S(1)} %get-tuple-element.46), channel_id=1, source_target_pairs={{0,4},{1,5},{2,6},{3,7},{4,0},{5,1},{6,2},{7,3},{8,12},{9,13},{10,... | collective-permute-start | bytes 392 | tf_op jit(solution)/shard_map/ppermute | solution.py:211
  33.2 4.4 %collective-permute-start.18 = (f32[1,16]{1,0:T(1,128)S(1)}, f32[1,16]{1,0:T(1,128)S(1)}, u32[]{:S(2)}, u32[]{:S(2)}) collective-permute-start(f32[1,16]{1,0:T(1,128)S(1)} %get-tuple-element.48), channel_id=1, source_target_pairs={{0,8},{1,9},{2,10},{3,11},{4,12},{5,13},{6,14},{7,15},{8,0},{9,1},... | collective-permute-start | bytes 200 | tf_op jit(solution)/shard_map/ppermute | solution.py:211
